TPU v7x, 32 devices: a whole 2x2x4 slice. The times are simulated.
32 devices in a mesh: rep: 8 (over y, x, core), shard: 4 (over z).
Axes of the slice: x: 2, y: 2, z: 4, core: 2. Of those that a mesh axis runs over, the one named last changes fastest.
Arguments:
- tokens: bfloat16 [32, 512, 512], P(('rep', 'shard')), may hold values from -6 to 6
- segments: int32 [32, 512], P(('rep', 'shard')), may hold values from 0 to 7, never falling along the last dimension, each value on 1 to 256 neighbouring positions
- choices: int32 [32, 512, 2], P(('rep', 'shard')), may hold values from 0 to 7, all different within a row
- priority: int32 [32, 512], P(('rep', 'shard')), may hold values from 0 to 511, each once within a row
- cotangent: bfloat16 [32, 512, 512], P(('rep', 'shard')), may hold values from -6 to 6
- qkv_weights: bfloat16 [3, 512, 512], P(None, 'shard'), may hold values from -0.25 to 0.25
- out_weight: bfloat16 [512, 512], P('shard'), may hold values from -1.5 to 1.5
- router_weight: bfloat16 [512, 8], P('shard'), may hold values from -0.1875 to 0.1875
- gains: bfloat16 [2, 512], P(None, 'shard'), may hold values from 0.25 to 1.75
- w_in: bfloat16 [8, 512, 2048], P('shard'), may hold values from -0.25 to 0.25
- w_out: bfloat16 [8, 512, 2048], P('shard'), may hold values from -1 to 1
Outputs:
- result: bfloat16 [32, 512, 512], P(('rep', 'shard'))
- grad_tokens: bfloat16 [32, 512, 512], P(('rep', 'shard'))
- grad_qkv: float32 [3, 512, 512], P(None, 'shard')
- grad_out_weight: float32 [512, 512], P('shard')
- grad_router: float32 [512, 8], P('shard')
- grad_gains: float32 [2, 512], P(None, 'shard')
- grad_w_in: float32 [8, 512, 2048], P('shard')
- grad_w_out: float32 [8, 512, 2048], P('shard')
All inputs are finite; a program needn't handle non-finite values.
Results may differ from a plain program's by a relative error of at most 0.019.
Values may be sent and summed in bfloat16 or wider, within the bound.
No kernel may reach another device: no remote copies, remote signals or barrier semaphores. Data moves between devices by JAX's collectives and lax.ppermute only.
A program may use at most 256 MiB of HBM per device.

v0:
```python
import jax
import jax.numpy as jnp
from jax import lax
from jax.experimental import pallas as pl
from jax.experimental.pallas import tpu as pltpu
from jax.sharding import PartitionSpec as P

HEADS = 8
HEAD_DIM = 64
EXPERTS = 8
CAPACITY = 135
ROWS = 144
SLOTS = 136
EPS = 1e-06
F32 = jnp.float32
BF = jnp.bfloat16
AXES = ("rep", "shard")
FF_STEP = 512
KEPT = 7
SMALL = pl.CostEstimate(flops=1000, bytes_accessed=1000, transcendentals=0)
GELU_A = 0.7978845608028654
GELU_B = 0.044715


def dot_nn(a, b):
    return lax.dot_general(a, b, (((1,), (0,)), ((), ())), preferred_element_type=F32)


def dot_nt(a, b):
    return lax.dot_general(a, b, (((1,), (1,)), ((), ())), preferred_element_type=F32)


def dot_tn(a, b):
    return lax.dot_general(a, b, (((0,), (0,)), ((), ())), preferred_element_type=F32)


def after(value, *others):
    return lax.optimization_barrier((value, *others))[0]


def iota(shape, dim):
    return lax.broadcasted_iota(jnp.int32, shape, dim)


def unit_of(values):
    mean = jnp.mean(values, axis=-1, keepdims=True)
    centered = values - mean
    inv = lax.rsqrt(jnp.mean(centered * centered, axis=-1, keepdims=True) + EPS)
    return centered * inv, inv


def split3(values):
    high = values.astype(BF)
    rest = values - high.astype(F32)
    mid = rest.astype(BF)
    low = (rest - mid.astype(F32)).astype(BF)
    return high, mid, low


def piece_rows(values):
    high, mid, low = split3(values)
    shape = (8, values.shape[1])
    row = iota(shape, 0)
    parts = [jnp.broadcast_to(part.astype(F32), shape) for part in (high, mid, low)]
    return jnp.where(
        row == 0, parts[0], jnp.where(row == 1, parts[1], jnp.where(row == 2, parts[2], 0.0))
    )


def far(value):
    return pltpu.with_memory_space_constraint(value, pltpu.HBM)


def near(value):
    return pltpu.with_memory_space_constraint(value, pltpu.VMEM)


def vmem(n):
    return [pl.BlockSpec(memory_space=pltpu.VMEM)] * n


def params(mib):
    return pltpu.CompilerParams(vmem_limit_bytes=mib << 20)


def route_body(choice_ref, prio_ref, cot_ref, index_ref, sent_ref):
    count = cot_ref.shape[-2]
    choice = choice_ref[...]
    experts = iota((EXPERTS, count), 0)
    first = jnp.where(choice[0:1, :] == experts, 1.0, 0.0)
    second = jnp.where(choice[1:2, :] == experts, 1.0, 0.0)
    order = jnp.where(iota((count, count), 0) == prio_ref[...], 1.0, 0.0).astype(BF)
    earlier = jnp.where(iota((count, count), 0) < iota((count, count), 1), 1.0, 0.0).astype(BF)
    both = jnp.concatenate([first, second], axis=0).astype(BF)
    before = dot_nn(dot_nt(both, order).astype(BF), earlier)
    held = jnp.sum(first, axis=1, keepdims=True)
    before = jnp.concatenate([before[0:EXPERTS], before[EXPERTS:] + held], axis=0)
    before = dot_nn(jnp.minimum(before, 255.0).astype(BF), order)
    slot0 = jnp.sum(first * before[0:EXPERTS], axis=0, keepdims=True)
    slot1 = jnp.sum(second * before[EXPERTS:], axis=0, keepdims=True)
    slot = jnp.concatenate([slot0, slot1], axis=0).astype(jnp.int32)
    index = jnp.where(slot < CAPACITY, choice * ROWS + slot, -1)
    index_ref[...] = index
    cot = cot_ref[0]
    for e in range(EXPERTS):
        row = iota((ROWS, count), 0) + e * ROWS
        pick = (row == index[0:1, :]) | (row == index[1:2, :])
        sent_ref[e] = dot_nn(jnp.where(pick, 1.0, 0.0).astype(BF), cot).astype(BF)


def route(choice_t, prio, cot):
    _, count, width = cot.shape
    return pl.pallas_call(
        route_body,
        out_shape=(
            jax.ShapeDtypeStruct((2, count), jnp.int32),
            pltpu.HBM((EXPERTS, ROWS, width), BF),
        ),
        in_specs=vmem(3),
        out_specs=tuple(vmem(2)),
        compiler_params=params(12),
        cost_estimate=SMALL,
        name="route",
    )(far(choice_t), far(prio), far(cot))


def pack_body(where_ref, qkv_ref, out_ref, router_ref, gains_ref, pack_ref):
    rows = pack_ref.shape[1]
    start = pl.multiple_of(where_ref[0] * rows, rows)
    for s in range(3):
        pack_ref[s] = qkv_ref[s, pl.ds(start, rows), :]
    pack_ref[3] = out_ref[pl.ds(start, rows), :]
    depth = router_ref.shape[1]
    small = jnp.concatenate(
        [router_ref[...].astype(F32), gains_ref[...].astype(F32), jnp.zeros((6, depth), F32)],
        axis=0,
    )
    pack_ref[4, :, 0:depth] = small.astype(BF)
    pack_ref[4, :, depth:] = jnp.zeros((rows, pack_ref.shape[2] - depth), BF)


def pack_weights(rep, qkv, out, router, gains, rows):
    width = out.shape[1]
    return pl.pallas_call(
        pack_body,
        out_shape=jax.ShapeDtypeStruct((5, rows, width), BF),
        in_specs=[pl.BlockSpec(memory_space=pltpu.SMEM)] + vmem(4),
        out_specs=vmem(1)[0],
        compiler_params=params(4),
        name="pack_weights",
    )(rep.reshape(1), far(qkv), far(out), far(router), far(gains))


def gather_weights(rep, shard, reps, shards_n, qkv, out, router, gains):
    rows = qkv.shape[1] // reps
    pack = pack_weights(rep, qkv, out, router, gains, rows)
    lines = [
        lax.ppermute(pack, "shard", [(i, i ^ dz) for i in range(shards_n)])
        for dz in range(1, shards_n)
    ]
    block = jnp.stack([piece[0:4] for piece in lines])
    smalls = jnp.stack([piece[4] for piece in [pack] + lines])
    spread = [block] + [
        lax.ppermute(block, "rep", [(i, i ^ k) for i in range(reps)]) for k in range(2, reps, 2)
    ]
    twin = [lax.ppermute(piece, "rep", [(i, i ^ 1) for i in range(reps)]) for piece in spread]
    pieces = []
    for own, other in zip(spread, twin, strict=True):
        pieces += [own, other]
    return smalls, pieces, lines


def fill_weights(rep, shard, qkv_ref, out_ref, smalls_ref, piece_refs, full_ref, small_ref):
    depth = out_ref.shape[0]
    own = pl.multiple_of(shard * depth, depth)
    for s in range(3):
        full_ref[s, pl.ds(own, depth), :] = qkv_ref[s]
    full_ref[3, pl.ds(own, depth), :] = out_ref[...]
    small_ref[:, pl.ds(own, depth)] = smalls_ref[0, :, 0:depth]
    for far in range(1, smalls_ref.shape[0]):
        base = pl.multiple_of((shard ^ far) * depth, depth)
        small_ref[:, pl.ds(base, depth)] = smalls_ref[far, :, 0:depth]
        for k, piece in enumerate(piece_refs):
            rows = piece.shape[2]
            start = pl.multiple_of(base + (rep ^ k) * rows, rows)
            for s in range(4):
                full_ref[s, pl.ds(start, rows), :] = piece[far - 1, s]


def head_masks(count):
    lane = iota((count, 2 * HEAD_DIM), 1)
    return [lane < HEAD_DIM, lane >= HEAD_DIM]


def kept_shapes(count, width):
    return (
        ((4, width, width), BF),
        ((HEADS, count, count), BF),
        ((3, count, width), BF),
        ((count, width), BF),
        ((count, width), BF),
        ((count, width), F32),
        ((count, width), BF),
    )


def forward_body(fast, n_pieces, *refs):
    if fast:
        where_ref, x_ref, seg_ref, index_ref, qkv_ref, out_ref, smalls_ref = refs[:7]
        piece_refs = refs[7 : 7 + n_pieces]
        refs = refs[7 + n_pieces :]
    else:
        x_ref, seg_ref, index_ref, qkv_ref, out_ref, router_ref, gains_ref = refs[:7]
        refs = refs[7:]
    sent_ref, small_ref, gate_ref, *kept = refs[: 3 + KEPT]
    full_ref, weights_ref, proj_ref, n1_ref, mixed_ref, resid_ref, n2_ref = held = refs[3 + KEPT : -1]
    sem = refs[-1]

    def keep(*which):
        for i in which:
            pltpu.make_async_copy(held[i], kept[i], sem.at[i]).start()

    if fast:
        fill_weights(
            where_ref[0], where_ref[1], qkv_ref, out_ref, smalls_ref, piece_refs, full_ref, small_ref
        )
    else:
        full_ref[0:3] = qkv_ref[...]
        full_ref[3] = out_ref[...]
        small_ref[...] = jnp.concatenate(
            [
                router_ref[...].astype(F32),
                gains_ref[...].astype(F32),
                jnp.zeros((6, out_ref.shape[1]), F32),
            ],
            axis=0,
        ).astype(BF)
    keep(0)
    x = x_ref[0].astype(F32)
    count, width = x.shape
    small = small_ref[...].astype(F32)
    unit1, _ = unit_of(x)
    n1 = (unit1 * small[8:9, :]).astype(BF)
    n1_ref[...] = n1
    for s in range(3):
        proj_ref[s] = dot_nn(n1, full_ref[s]).astype(BF)
    keep(2, 3)
    document = jnp.where(iota((8, count), 0) == seg_ref[...], 1.0, 0.0).astype(BF)
    bias = jnp.where(dot_tn(document, document) > 0.5, 0.0, -1e30)
    masks = head_masks(count)
    for pair in range(HEADS // 2):
        lanes = slice(pair * 2 * HEAD_DIM, (pair + 1) * 2 * HEAD_DIM)
        q, k, v = proj_ref[0, :, lanes], proj_ref[1, :, lanes], proj_ref[2, :, lanes]
        q = q * BF(HEAD_DIM**-0.5)
        halves = []
        for half in range(2):
            scores = dot_nt(jnp.where(masks[half], q, BF(0)), k) + bias
            top = jnp.max(scores, axis=-1, keepdims=True)
            terms = jnp.exp(scores - top)
            total = jnp.sum(terms, axis=-1, keepdims=True)
            weights = (terms * (1.0 / total)).astype(BF)
            weights_ref[2 * pair + half] = weights
            halves.append(dot_nn(weights, v))
        mixed_ref[:, lanes] = jnp.where(masks[0], halves[0], halves[1]).astype(BF)
    keep(1, 4)
    resid = x + dot_nn(mixed_ref[...], full_ref[3])
    resid_ref[...] = resid
    keep(5)
    unit2, _ = unit_of(resid)
    n2 = (unit2 * small[9:10, :]).astype(BF)
    n2_ref[...] = n2
    keep(6)
    logits = dot_nt(small_ref[...], n2)[0:EXPERTS]
    terms = jnp.exp(logits - jnp.max(logits, axis=0, keepdims=True))
    gates = terms / jnp.sum(terms, axis=0, keepdims=True)
    gate_ref[...] = gates
    index = index_ref[...]
    for e in range(EXPERTS):
        row = iota((ROWS, count), 0) + e * ROWS
        pick = (row == index[0:1, :]) | (row == index[1:2, :])
        pick = jnp.where(pick, 1.0, 0.0).astype(BF)
        rows = dot_nn(pick, n2)
        side = dot_nt(piece_rows(gates[e : e + 1, :]).astype(BF), pick)
        side = jnp.concatenate([side, jnp.zeros((8, width - ROWS), F32)], axis=1)
        sent_ref[e] = jnp.concatenate([rows[0:SLOTS], side], axis=0).astype(BF)
    for i in range(KEPT):
        pltpu.make_async_copy(held[i], kept[i], sem.at[i]).wait()


def forward(fast, where, x, seg, index, weights_in, pieces):
    _, count, width = x.shape
    body = lambda *refs: forward_body(fast, len(pieces), *refs)
    operands = [far(x), far(seg), index, *(far(w) for w in weights_in[:2]), *weights_in[2:], *pieces]
    specs = vmem(len(operands))
    if fast:
        operands = [where] + operands
        specs = [pl.BlockSpec(memory_space=pltpu.SMEM)] + specs
    shown = (
        pltpu.HBM((EXPERTS, ROWS, width), BF),
        jax.ShapeDtypeStruct((16, width), BF),
        jax.ShapeDtypeStruct((EXPERTS, count), F32),
    )
    kept = kept_shapes(count, width)
    return pl.pallas_call(
        body,
        out_shape=(*shown, *(pltpu.HBM(*k) for k in kept)),
        in_specs=specs,
        out_specs=(*vmem(3), *([pl.BlockSpec(memory_space=pltpu.HBM)] * KEPT)),
        scratch_shapes=[*(pltpu.VMEM(*k) for k in kept), pltpu.SemaphoreType.DMA((KEPT,))],
        compiler_params=params(40),
        cost_estimate=SMALL,
        name="forward",
    )(*operands)


def expert_rows(n2_ref, cot_ref, w_in_ref, w_out_ref, back_ref, out_ref, span, scratch):
    hidden_ref, pre_ref, rows_ref, gso_ref = scratch
    row = iota((ROWS, 1), 0)
    eye = jnp.where(iota((ROWS, ROWS), 0) == iota((ROWS, ROWS), 1), 1.0, 0.0).astype(BF)
    gates, rows_all, gso_all = [], [], []
    for g in range(2):
        rows = n2_ref[g]
        side = rows.astype(F32)[SLOTS:, 0:ROWS].astype(BF)
        gate = jnp.sum(dot_nt(eye, side), axis=1, keepdims=True)
        gates.append(gate)
        rows_all.append(jnp.where(row < SLOTS, rows, BF(0)))
        gso_all.append((gate * cot_ref[g].astype(F32)).astype(BF))
    rows, gso = jnp.concatenate(rows_all, axis=0), jnp.concatenate(gso_all, axis=0)
    rows_ref[span], gso_ref[span] = rows, gso
    for start in range(0, w_in_ref.shape[2], FF_STEP):
        cols = slice(start, start + FF_STEP)
        u = dot_nn(rows, w_in_ref[0, :, cols])
        square = u * u
        t = jnp.tanh(GELU_A * (u + GELU_B * (u * square)))
        half = 0.5 * (1.0 + t)
        hidden = u * half
        slope = half + hidden * (1.0 - t) * (GELU_A * (1.0 + 3.0 * GELU_B * square))
        hidden_ref[span, cols] = hidden.astype(BF)
        pre_ref[span, cols] = (dot_nn(gso, w_out_ref[0, :, cols]) * slope).astype(BF)
    grad_in = dot_nt(pre_ref[span], w_in_ref[0])
    result = dot_nt(hidden_ref[span], w_out_ref[0])
    ones = jnp.ones((8, rows.shape[1]), BF)
    for g in range(2):
        part = slice(g * ROWS, (g + 1) * ROWS)
        out = (gates[g] * result[part]).astype(BF)
        out_ref[g] = out
        product = out.astype(F32) * cot_ref[g].astype(F32)
        high = product.astype(BF)
        low = (product - high.astype(F32)).astype(BF)
        inner = dot_nt(ones, high) + dot_nt(ones, low)
        side = piece_rows(inner[0:1, :])
        side = jnp.concatenate([side, jnp.zeros((8, out.shape[1] - ROWS), F32)], axis=1)
        back_ref[g] = jnp.concatenate([grad_in[part][0:SLOTS], side], axis=0).astype(BF)


def experts_body(where_ref, *refs):
    expert_rows(*refs[:6], slice(None), refs[6:])


def experts(where, n2, cot, w_in, w_out):
    groups, _, width = n2.shape
    hidden_n = w_in.shape[2]
    total = groups * ROWS
    weight = pl.BlockSpec((1, width, hidden_n), lambda i, w: (w[0], 0, 0))
    payload = pl.BlockSpec((2, ROWS, width), lambda i, w: (i, 0, 0))
    narrow = pl.BlockSpec((2 * ROWS, width), lambda i, w: (i, 0))
    wide = pl.BlockSpec((2 * ROWS, hidden_n), lambda i, w: (i, 0))
    return pl.pallas_call(
        experts_body,
        out_shape=(
            [pltpu.HBM((groups, ROWS, width), BF)] * 2
            + [pltpu.HBM((total, hidden_n), BF)] * 2
            + [pltpu.HBM((total, width), BF)] * 2
        ),
        grid_spec=pltpu.PrefetchScalarGridSpec(
            num_scalar_prefetch=1,
            grid=(groups // 2,),
            in_specs=[payload, payload, weight, weight],
            out_specs=[payload, payload, wide, wide, narrow, narrow],
        ),
        compiler_params=params(40),
        cost_estimate=SMALL,
        name="experts",
    )(where, n2, cot, far(w_in), far(w_out))


def expert_grads_body(split, where_ref, hidden_ref, pre_ref, rows_ref, gso_ref, *refs):
    grad_refs, sum_ref = refs[:-1], refs[-1]
    step, steps = pl.program_id(0), pl.num_programs(0)
    for half, (left, right) in enumerate(((rows_ref, pre_ref), (gso_ref, hidden_ref))):
        grad = dot_tn(left[...], right[...]).astype(BF)
        if not split:
            grad_refs[0][half] = grad
            continue
        sum_ref[half] = grad
    if not split:
        return
    depth = sum_ref.shape[1] // 4
    for late in range(2):

        @pl.when((step < steps // 2) if late == 0 else (step >= steps // 2))
        def _(late=late):
            for half in range(2):
                for k in range(4):
                    start = pl.multiple_of((where_ref[1] ^ k) * depth, depth)
                    goes = k == 3 or k == 1 + late
                    ref = grad_refs[2 * late + (0 if goes else 1)]
                    ref[int(k == 3 or k == 2 - late), half] = sum_ref[half, pl.ds(start, depth), :]


def expert_grads(where, split, hidden, pre, rows, gso):
    total, width = rows.shape
    hidden_n = hidden.shape[1]
    steps = hidden_n // FF_STEP
    narrow = pl.BlockSpec((total, width), lambda i, w: (0, 0))
    wide = pl.BlockSpec((total, FF_STEP), lambda i, w: (0, i))
    if split:
        part = (2, 2, width // 4, FF_STEP)
        first = pl.BlockSpec(part, lambda i, w: (0, 0, 0, jnp.minimum(i, steps // 2 - 1)))
        second = pl.BlockSpec(part, lambda i, w: (0, 0, 0, jnp.maximum(i - steps // 2, 0)))
        grad_specs = [first, first, second, second]
        grad_shapes = [jax.ShapeDtypeStruct((2, 2, width // 4, hidden_n // 2), BF)] * 4
    else:
        grad_specs = [pl.BlockSpec((2, width, FF_STEP), lambda i, w: (0, 0, i))]
        grad_shapes = [pltpu.HBM((2, width, hidden_n), BF)]
    return pl.pallas_call(
        lambda *refs: expert_grads_body(split, *refs),
        out_shape=grad_shapes,
        grid_spec=pltpu.PrefetchScalarGridSpec(
            num_scalar_prefetch=1,
            grid=(steps,),
            in_specs=[wide, wide, narrow, narrow],
            out_specs=grad_specs,
            scratch_shapes=[pltpu.VMEM((2, width, FF_STEP), BF)],
        ),
        compiler_params=params(30),
        cost_estimate=SMALL,
        name="expert_grads",
    )(where, far(hidden), far(pre), far(rows), far(gso))


def place_grads(fast, reps, shards_n, pack_ref, which, grad):
    if not fast:
        pack_ref[which] = grad.astype(BF)
        return
    width = grad.shape[0]
    depth = width // shards_n
    rows = depth // reps
    grad = grad.astype(BF)
    for z in range(shards_n):
        for r in range(reps):
            start = z * depth + r * rows
            span = slice(which * rows, (which + 1) * rows)
            pack_ref[r % 2, z, r // 2, span, :] = grad[start : start + rows]


def backward_body(fast, reps, shards_n, where_ref, *refs):
    core = where_ref[0]
    back_ref, x_ref, cot_ref, index_ref, small_ref, gate_ref, *kept = refs[: 6 + KEPT]
    if fast:
        grad_x_ref, mine_ref, twin_ref, pack_ref, gp_ref = refs[6 + KEPT : 11 + KEPT]
        refs = refs[11 + KEPT :]
    else:
        grad_x_ref, pack_ref, sums_ref, gp_ref = refs[6 + KEPT : 10 + KEPT]
        refs = refs[10 + KEPT :]
    full_ref, weights_ref, proj_ref, n1_ref, mixed_ref, resid_ref, n2_ref = held = refs[:-1]
    sem = refs[-1]
    for i in (5, 6, 4, 0, 2, 1, 3):
        pltpu.make_async_copy(kept[i], held[i], sem.at[i]).start()

    def need(*which):
        for i in which:
            pltpu.make_async_copy(kept[i], held[i], sem.at[i]).wait()

    count, width = resid_ref.shape
    small = small_ref[...].astype(F32)
    index = index_ref[...]
    gates = gate_ref[...]
    grad_n2 = jnp.zeros((count, width), F32)
    rows_h = []
    for e in range(EXPERTS):
        row = iota((ROWS, count), 0) + e * ROWS
        pick = (row == index[0:1, :]) | (row == index[1:2, :])
        pick = jnp.where(pick, 1.0, 0.0).astype(BF)
        back = back_ref[e]
        side = back.astype(F32)[SLOTS:, 0:ROWS].astype(BF)
        rows_h.append(jnp.sum(dot_nn(side, pick), axis=0, keepdims=True))
        grad_n2 = grad_n2 + dot_tn(pick, back)
    inner = jnp.concatenate(rows_h, axis=0)
    grad_logits = (inner - gates * jnp.sum(inner, axis=0, keepdims=True)).astype(BF)
    wide_logits = jnp.concatenate(
        [grad_logits.astype(F32), jnp.zeros((8, count), F32)], axis=0
    ).astype(BF)
    grad_n2 = grad_n2 + dot_tn(wide_logits, small_ref[...])
    need(5, 6)
    grad_router = dot_nn(wide_logits, n2_ref[...])[0:EXPERTS]
    unit2, inv2 = unit_of(resid_ref[...])
    grad_gain2 = jnp.sum(grad_n2 * unit2, axis=0, keepdims=True)
    a = grad_n2 * small[9:10, :]
    grad_resid = cot_ref[0].astype(F32) + inv2 * (
        a
        - jnp.mean(a, axis=-1, keepdims=True)
        - unit2 * jnp.mean(a * unit2, axis=-1, keepdims=True)
    )
    branch = grad_resid.astype(BF)
    need(4, 0)
    place_grads(fast, reps, shards_n, pack_ref, 3, dot_tn(mixed_ref[...], branch))
    grad_mixed = dot_nt(branch, full_ref[3]).astype(BF)
    need(2, 1)
    masks = head_masks(count)
    factor = HEAD_DIM**-0.5
    for pair in range(HEADS // 2):
        lanes = slice(pair * 2 * HEAD_DIM, (pair + 1) * 2 * HEAD_DIM)
        q, k, v = proj_ref[0, :, lanes], proj_ref[1, :, lanes], proj_ref[2, :, lanes]
        gm = grad_mixed[:, lanes]
        parts = []
        for half in range(2):
            weights = weights_ref[2 * pair + half]
            probs = weights.astype(F32)
            grad_probs = dot_nt(jnp.where(masks[half], gm, BF(0)), v)
            total = jnp.sum(probs * grad_probs, axis=-1, keepdims=True)
            grad_scores = (probs * (grad_probs - total)).astype(BF)
            parts.append(
                (dot_nn(grad_scores, k), dot_tn(grad_scores, q), dot_tn(weights, gm))
            )
        for s in range(3):
            both = jnp.where(masks[0], parts[0][s], parts[1][s])
            gp_ref[s, :, lanes] = (both * factor if s < 2 else both).astype(BF)
    need(3)
    n1 = n1_ref[...]
    grad_n1 = jnp.zeros((count, width), F32)
    for s in range(3):
        grads = gp_ref[s]
        place_grads(fast, reps, shards_n, pack_ref, s, dot_tn(n1, grads))
        grad_n1 = grad_n1 + dot_nt(grads, full_ref[s])
    unit1, inv1 = unit_of(x_ref[0].astype(F32))
    grad_gain1 = jnp.sum(grad_n1 * unit1, axis=0, keepdims=True)
    b = grad_n1 * small[8:9, :]
    grad_x = grad_resid + inv1 * (
        b
        - jnp.mean(b, axis=-1, keepdims=True)
        - unit1 * jnp.mean(b * unit1, axis=-1, keepdims=True)
    )
    grad_x_ref[0] = grad_x.astype(BF)
    sums = jnp.concatenate(
        [grad_router, grad_gain1, grad_gain2, jnp.zeros((6, width), F32)], axis=0
    )
    if not fast:
        sums_ref[...] = sums
        return
    depth = width // shards_n
    rows = depth // reps
    for z in range(shards_n):
        for r in range(reps):
            two = sums[2 * r : 2 * r + 2, z * depth : (z + 1) * depth]
            two = jnp.concatenate([two, jnp.zeros((6, depth), F32)], axis=0)
            two = jnp.concatenate([two, jnp.zeros((8, width - depth), F32)], axis=1)
            pack_ref[r % 2, z, r // 2, 4 * rows :, :] = two.astype(BF)
    copies = [
        pltpu.make_async_copy(pack_ref.at[core ^ i], (mine_ref, twin_ref)[i], sem.at[i])
        for i in range(2)
    ]
    for copy in copies:
        copy.start()
    for copy in copies:
        copy.wait()


def backward(fast, reps, shards_n, where, operands):
    x = operands[1]
    _, count, width = x.shape
    outs = [jax.ShapeDtypeStruct(x.shape, BF)]
    scratch = [pltpu.VMEM((3, count, width), BF)]
    if fast:
        part = (shards_n, reps // 2, 4 * (width // shards_n // reps) + 8, width)
        outs += [pltpu.HBM(part, BF)] * 2
        out_specs = vmem(1) + [pl.BlockSpec(memory_space=pltpu.HBM)] * 2
        scratch = [pltpu.VMEM((2, *part), BF)] + scratch
    else:
        outs += [
            jax.ShapeDtypeStruct((4, width, width), BF),
            jax.ShapeDtypeStruct((16, width), F32),
        ]
        out_specs = vmem(3)
    return pl.pallas_call(
        lambda *refs: backward_body(fast, reps, shards_n, *refs),
        out_shape=tuple(outs),
        in_specs=[pl.BlockSpec(memory_space=pltpu.SMEM)]
        + vmem(len(operands) - KEPT)
        + [pl.BlockSpec(memory_space=pltpu.HBM)] * KEPT,
        out_specs=tuple(out_specs),
        scratch_shapes=[
            *scratch,
            *(pltpu.VMEM(*k) for k in kept_shapes(count, width)),
            pltpu.SemaphoreType.DMA((KEPT,)),
        ],
        compiler_params=params(40),
        cost_estimate=SMALL,
        name="backward",
    )(where, operands[0], *(far(v) for v in operands[1:3]), *operands[3:6], *(far(v) for v in operands[6:]))


def result_body(out_ref, index_ref, resid_ref, result_ref):
    total = resid_ref[...]
    count = total.shape[0]
    index = index_ref[...]
    for e in range(EXPERTS):
        row = iota((ROWS, count), 0) + e * ROWS
        pick = (row == index[0:1, :]) | (row == index[1:2, :])
        total = total + dot_tn(jnp.where(pick, 1.0, 0.0).astype(BF), out_ref[e])
    result_ref[0] = total.astype(BF)


def combine(out, index, resid):
    count, width = resid.shape
    return pl.pallas_call(
        result_body,
        out_shape=jax.ShapeDtypeStruct((1, count, width), BF),
        in_specs=vmem(3),
        out_specs=vmem(1)[0],
        compiler_params=params(8),
        cost_estimate=SMALL,
        name="combine",
    )(far(out), index, far(resid))


def plain(body, outs, *operands):
    return pl.pallas_call(
        body,
        out_shape=tuple(outs) if len(outs) > 1 else outs[0],
        in_specs=vmem(len(operands)),
        out_specs=tuple(vmem(len(outs))) if len(outs) > 1 else vmem(1)[0],
        compiler_params=params(16),
        cost_estimate=SMALL,
        name=body.__name__,
    )(*operands)


def first_sums(stay0_ref, come0_ref, stay1_ref, come1_ref, keep_ref, go0_ref, go1_ref):
    for half, (stay, come, go) in enumerate(
        ((stay0_ref, come0_ref, go0_ref), (stay1_ref, come1_ref, go1_ref))
    ):
        keep_ref[half] = (stay[0].astype(F32) + come[0].astype(F32)).astype(BF)
        go[...] = (stay[1].astype(F32) + come[1].astype(F32)).astype(BF)


def second_sums(keep_ref, come0_ref, come1_ref, sum_ref):
    for half, come in enumerate((come0_ref, come1_ref)):
        sum_ref[half] = (keep_ref[half].astype(F32) + come[...].astype(F32)).astype(BF)


def pair_sum(a_ref, b_ref, sum_ref):
    sum_ref[...] = (a_ref[...].astype(F32) + b_ref[...].astype(F32)).astype(BF)


def lead_sum(parts_ref, sum_ref):
    total = parts_ref[0].astype(F32)
    for i in range(1, parts_ref.shape[0]):
        total = total + parts_ref[i].astype(F32)
    sum_ref[...] = total.astype(BF)


def widen_body(every_ref, w_in_ref, w_out_ref):
    cols = every_ref.shape[-1]
    for half in range(2):
        span = slice(half * cols, (half + 1) * cols)
        w_in_ref[0, :, span] = every_ref[0, half, 0].astype(F32)
        w_out_ref[0, :, span] = every_ref[0, half, 1].astype(F32)


def widen(every, owned):
    reps, _, _, depth, cols = every.shape
    out = pltpu.HBM((owned, depth * (reps // owned), 2 * cols), F32)
    spot = pl.BlockSpec((1, depth, 2 * cols), lambda i: (i % owned, i // owned, 0))
    return pl.pallas_call(
        widen_body,
        out_shape=(out, out),
        grid=(reps,),
        in_specs=[pl.BlockSpec((1, *every.shape[1:]), lambda i: (i, 0, 0, 0, 0))],
        out_specs=(spot, spot),
        compiler_params=params(12),
        cost_estimate=SMALL,
        name="widen",
    )(far(every))


def finish_body(rows, parts_ref, qkv_ref, out_ref, router_ref, gains_ref):
    reps = parts_ref.shape[0]
    depth = out_ref.shape[0]
    smalls = []
    for r in range(reps):
        for s in range(3):
            qkv_ref[s, r * rows : (r + 1) * rows, :] = parts_ref[
                r, s * rows : (s + 1) * rows, :
            ].astype(F32)
        out_ref[r * rows : (r + 1) * rows, :] = parts_ref[r, 3 * rows : 4 * rows, :].astype(F32)
        smalls.append(parts_ref[r].astype(F32)[4 * rows : 4 * rows + 2, 0:depth])
    small = jnp.concatenate(smalls, axis=0)
    router_ref[...] = small[0:EXPERTS]
    gains_ref[...] = small[EXPERTS : EXPERTS + 2]


def finish(parts, rows):
    reps, _, width = parts.shape
    depth = rows * reps
    return pl.pallas_call(
        lambda *refs: finish_body(rows, *refs),
        out_shape=(
            jax.ShapeDtypeStruct((3, depth, width), F32),
            jax.ShapeDtypeStruct((depth, width), F32),
            jax.ShapeDtypeStruct((EXPERTS, depth), F32),
            jax.ShapeDtypeStruct((2, depth), F32),
        ),
        in_specs=vmem(1),
        out_specs=tuple(vmem(4)),
        compiler_params=params(4),
        name="finish",
    )(parts)


def shards(reps, shards_n, *args):
    tokens, segments, choices, priority, cotangent = args[:5]
    qkv_weights, out_weight, router_weight, gains, w_in, w_out = args[5:]
    rep, shard = lax.axis_index("rep"), lax.axis_index("shard")
    width, hidden = w_in.shape[1:]
    owned = w_in.shape[0]
    peers = reps // owned
    depth = width // shards_n
    fast = depth % (16 * reps) == 0 and depth == 128 and owned == 2 and peers == 4
    if not fast and owned != 1:
        raise NotImplementedError("mesh")
    column = [
        [(c * owned + e % owned) * shards_n + e // owned for e in range(EXPERTS)]
        for c in range(peers)
    ]

    def to_experts(rows):
        return lax.all_to_all(rows, AXES, 0, 0, axis_index_groups=column, tiled=True)

    where = jnp.stack([rep % owned, rep // owned]).astype(jnp.int32)
    index, cot_sent = route(choices[0].T, priority, cotangent)
    if fast:
        smalls, pieces, lines = gather_weights(
            rep, shard, reps, shards_n, qkv_weights, out_weight, router_weight.T, gains
        )
        place = jnp.stack([rep, shard]).astype(jnp.int32)
        weights_in = (qkv_weights, out_weight, smalls)
    else:
        place, pieces, lines = None, [], []
        weights_in = (
            lax.all_gather(qkv_weights, "shard", axis=1, tiled=True),
            lax.all_gather(out_weight, "shard", axis=0, tiled=True),
            lax.all_gather(router_weight, "shard", axis=0, tiled=True).T,
            lax.all_gather(gains, "shard", axis=1, tiled=True),
        )
    cot_in = to_experts(after(cot_sent, *lines))
    sent, small, gates, *kept = forward(
        fast, place, tokens, segments, index, weights_in, pieces
    )
    n2_in = to_experts(sent)

    def peer(value, k):
        return lax.ppermute(value, "rep", [(i, i ^ k) for i in range(reps)])

    back, out, *parts_in = experts(where, n2_in, cot_in, w_in, w_out)
    grads = expert_grads(where, fast, *parts_in)
    back_in = to_experts(back)
    if fast:
        axes = ((owned, 2 * owned), (2 * owned, owned))
        halves = [peer(grads[2 * half], axes[half][0]) for half in range(2)]
        back_in, *halves = lax.optimization_barrier((back_in, *halves))
        part = halves[0].shape[1:]
        small_part = jax.ShapeDtypeStruct(part, BF)
        keep, *leaves = plain(
            first_sums,
            [jax.ShapeDtypeStruct((2, *part), BF), small_part, small_part],
            grads[1],
            halves[0],
            grads[3],
            halves[1],
        )
        arrived = [peer(leaves[half], axes[half][1]) for half in range(2)]
    out_in = to_experts(after(out, back_in))
    grad_tokens, *packs = backward(
        fast,
        reps,
        shards_n,
        where,
        [back_in, tokens, cotangent, index, small, gates, *kept],
    )
    result = combine(out_in, index, kept[5])
    if fast:
        arrived = lax.optimization_barrier((packs[0], out_in, *arrived))[2:]
        total = plain(second_sums, [jax.ShapeDtypeStruct(keep.shape, BF)], keep, *arrived)
        every = lax.all_gather(total, "rep", axis=0, tiled=False)
        mine, twin = packs
        chip = plain(pair_sum, [jax.ShapeDtypeStruct(mine.shape, BF)], mine, peer(twin, 1))
        line = lax.all_to_all(chip, "shard", 0, 0, tiled=True)
        line = after(line, result)
        line = plain(lead_sum, [jax.ShapeDtypeStruct(line.shape[1:], BF)], line)
        plane_groups = [[p * owned + c for p in range(peers)] for c in range(owned)]
        plane = lax.all_to_all(line, "rep", 0, 0, axis_index_groups=plane_groups, tiled=True)
        share = plain(lead_sum, [jax.ShapeDtypeStruct(plane.shape[1:], BF)], plane)
        parts = lax.all_gather(share, "rep", axis=0, tiled=False)
        grad_qkv, grad_out, grad_router, grad_gains = finish(parts, depth // reps)
        grad_router = grad_router.T
        grad_w_in, grad_w_out = widen(every, owned)
    else:
        share = lax.psum_scatter(grads[0], "rep", scatter_dimension=1, tiled=True)
        every = lax.all_gather(share, "rep", axis=1, tiled=True).astype(F32)
        grad_w_in, grad_w_out = every[0:1], every[1:2]
        pack, sums = packs
        owned_rows = lax.psum_scatter(pack, "shard", scatter_dimension=1, tiled=True)
        owned_rows = lax.psum(owned_rows, "rep").astype(F32)
        grad_qkv, grad_out = owned_rows[0:3], owned_rows[3]
        sums = lax.psum(sums, AXES)
        mine = lax.dynamic_slice_in_dim(sums, shard * depth, depth, axis=1)
        grad_router, grad_gains = mine[0:EXPERTS].T, mine[EXPERTS : EXPERTS + 2]
    return (
        result,
        grad_tokens,
        grad_qkv,
        grad_out,
        grad_router,
        grad_gains,
        grad_w_in,
        grad_w_out,
    )


def solution(mesh):
    reps, shards_n = mesh.shape["rep"], mesh.shape["shard"]
    rows = P(("rep", "shard"), None, None)
    flat = P(("rep", "shard"), None)
    first = P("shard", None)
    stack = P("shard", None, None)
    second = P(None, "shard", None)
    return jax.shard_map(
        lambda *args: shards(reps, shards_n, *args),
        mesh=mesh,
        in_specs=(
            rows, flat, rows, flat, rows, second, first, first, P(None, "shard"), stack, stack,
        ),
        out_specs=(rows, rows, second, first, first, P(None, "shard"), stack, stack),
        check_vma=False,
    )
```

profile of v0, /device:TPU:0, one launch (start us, length us, event | category | flops | bytes accessed | tf_op | source)
XLA Modules:
  0.0 261.2 jit_solution(2849519040973747516)
XLA Ops:
  7.2 1.1 pack_weights.1
  8.3 5.1 %collective-permute-start.2 = (bf16[5,16,512]{2,1,0:T(8,128)(2,1)S(1)}, bf16[5,16,512]{2,1,0:T(8,128)(2,1)S(1)}, u32[]{:S(2)}, u32[]{:S(2)}) collective-permute-start(bf16[5,16,512]{2,1,0:T(8,128)(2,1)S(1)} %pack_weights.1), channel_id=1, source_target_pairs={{0,3},{1,2},{2,1},{3,0},{4,7},{5,6},{6,5},{7,4},{8,11},{9,10},{10,... | collective-permute-start | bytes 245768 | tf_op jit(solution)/shard_map/ppermute | solution.py:158
  13.4 0.6 collective-permute-start
  14.0 3.5 %route.1 = (s32[2,512]{1,0:T(2,128)S(1)}, bf16[8,144,512]{2,1,0:T(8,128)(2,1)}) custom-call(s32[2,512]{1,0:T(2,128)} %bitcast.19, s32[1,512]{1,0:T(1,128)} %prio_ref.1, bf16[1,512,512]{2,1,0:T(8,128)(2,1)} %refs_3_.3), custom_call_target="tpu_custom_call" | custom-call | flops 1000 | bytes 1000 | tf_op jit(solution)/shard_map/route/pallas_call | solution.py:113
  17.5 2.7 %collective-permute-done.1 = bf16[5,16,512]{2,1,0:T(8,128)(2,1)S(1)} collective-permute-done((bf16[5,16,512]{2,1,0:T(8,128)(2,1)S(1)}, bf16[5,16,512]{2,1,0:T(8,128)(2,1)S(1)}, u32[]{:S(2)}, u32[]{:S(2)}) %collective-permute-start.1) | collective-permute-done | bytes 81952 | tf_op jit(solution)/shard_map/ppermute | solution.py:158
  20.2 4.0 %all-to-all-start.1 = ((bf16[8,144,512]{2,1,0:T(8,128)(2,1)}), bf16[8,144,512]{2,1,0:T(8,128)(2,1)S(1)}, u32[]{:S(2)}, u32[]{:S(2)}) async-start(bf16[8,144,512]{2,1,0:T(8,128)(2,1)} %get-tuple-element.53), calls=%async_computation.1 | async-start | bytes 2359296 | tf_op jit(solution)/shard_map/all_to_all | solution.py:738
  24.3 2.5 collective-permute-start.8
  26.8 0.5 collective-permute-start.6
  27.3 0.5 collective-permute-start.4
  27.8 5.1 %collective-permute-done.8.refs_13_ = bf16[3,4,16,512]{3,2,1,0:T(8,128)(2,1)S(1)} collective-permute-done((bf16[3,4,16,512]{3,2,1,0:T(8,128)(2,1)S(1)}, bf16[3,4,16,512]{3,2,1,0:T(8,128)(2,1)S(1)}, u32[]{:S(2)}, u32[]{:S(2)}) %collective-permute-start.8) | collective-permute-done | bytes 196640 | tf_op jit(solution)/shard_map/ppermute | solution.py:164
  33.0 3.8 %collective-permute-done.6.refs_11_ = bf16[3,4,16,512]{3,2,1,0:T(8,128)(2,1)S(1)} collective-permute-done((bf16[3,4,16,512]{3,2,1,0:T(8,128)(2,1)S(1)}, bf16[3,4,16,512]{3,2,1,0:T(8,128)(2,1)S(1)}, u32[]{:S(2)}, u32[]{:S(2)}) %collective-permute-start.6) | collective-permute-done | bytes 196640 | tf_op jit(solution)/shard_map/ppermute | solution.py:164
  36.9 0.4 collective-permute-start.5
  37.4 0.8 collective-permute-done.7.refs_12_
  38.2 0.3 collective-permute-done.5.refs_10_
  38.5 13.0 %forward.1 = (bf16[8,144,512]{2,1,0:T(8,128)(2,1)}, bf16[16,512]{1,0:T(8,128)(2,1)S(1)}, f32[8,512]{1,0:T(8,128)S(1)}, bf16[4,512,512]{2,1,0:T(8,128)(2,1)}, bf1...) custom-call(s32[2]{0:T(128)S(1)} %pad_add_fusion.1.refs_0_, ...), custom_call_target="tpu_custom_call" | custom-call | flops 1000 | bytes 1000 | tf_op jit(solution)/shard_map/forward/pallas_call | solution.py:304
  51.5 2.1 all-to-all-done.1.refs_1_
  53.6 3.7 %all-to-all-start = ((bf16[8,144,512]{2,1,0:T(8,128)(2,1)}), bf16[8,144,512]{2,1,0:T(8,128)(2,1)S(1)}, u32[]{:S(2)}, u32[]{:S(2)}) async-start(bf16[8,144,512]{2,1,0:T(8,128)(2,1)} %get-tuple-element.51), calls=%async_computation | async-start | bytes 2359296 | tf_op jit(solution)/shard_map/all_to_all | solution.py:738
  57.4 0.1 pad_add_fusion.where_ref.refs_0_
  57.5 29.0 %all-to-all-done.refs_0_ = bf16[8,144,512]{2,1,0:T(8,128)(2,1)S(1)} async-done(((bf16[8,144,512]{2,1,0:T(8,128)(2,1)}), bf16[8,144,512]{2,1,0:T(8,128)(2,1)S(1)}, u32[]{:S(2)}, u32[]{:S(2)}) %all-to-all-start) | async-done | bytes 1179680 | tf_op jit(solution)/shard_map/all_to_all | solution.py:738
  86.5 19.7 %experts.1 = (bf16[8,144,512]{2,1,0:T(8,128)(2,1)}, bf16[8,144,512]{2,1,0:T(8,128)(2,1)}, bf16[1152,2048]{1,0:T(8,128)(2,1)}, bf16[1152,2048]{1,0:T(8,128)(2,1)}...) custom-call(s32[2]{0:T(128)S(1)} %pad_add_fusion.where_ref.refs_0_, ...), custom_call_target="tpu_custom_call" | custom-call | flops 1000 | bytes 1000 | tf_op jit(solution)/shard_map/experts/pallas_call | solution.py:368
  106.3 3.6 %all-to-all-start.2 = ((bf16[8,144,512]{2,1,0:T(8,128)(2,1)}), bf16[8,144,512]{2,1,0:T(8,128)(2,1)S(1)}, u32[]{:S(2)}, u32[]{:S(2)}) async-start(bf16[8,144,512]{2,1,0:T(8,128)(2,1)} %get-tuple-element.55), calls=%async_computation.2 | async-start | bytes 2359296 | tf_op jit(solution)/shard_map/all_to_all | solution.py:738
  109.8 9.9 %expert_grads.1 = (bf16[2,2,128,1024]{3,2,1,0:T(8,128)(2,1)S(1)}, bf16[2,2,128,1024]{3,2,1,0:T(8,128)(2,1)S(1)}, bf16[2,2,128,1024]{3,2,1,0:T(8,128)(2,1)S(1)}, bf16[2,2,128,1024]{3,2,1,0:T(8,128)(2,1)S(1)}) custom-call(s32[2]{0:T(128)S(1)} %pad_add_fusion.where_ref.refs_0_, bf16[1152,2048]{1,0:T(8,128)(2,1)} %get-tuple-element.56.refs_1_, ...), custom_call_target="tpu_custom_call" | custom-call | flops 1000 | bytes 1000 | tf_op jit(solution)/shard_map/expert_grads/pallas_call | solution.py:426
  119.8 1.0 copy-done.1
  120.7 1.5 collective-permute-start.10
  122.2 1.5 collective-permute-start.11
  123.8 22.4 %collective-permute-done.10.come0_ref = bf16[2,2,128,1024]{3,2,1,0:T(8,128)(2,1)S(1)} collective-permute-done((bf16[2,2,128,1024]{3,2,1,0:T(8,128)(2,1)S(1)}, bf16[2,2,128,1024]{3,2,1,0:T(8,128)(2,1)S(1)}, u32[]{:S(2)}, u32[]{:S(2)}) %collective-permute-start.10) | collective-permute-done | bytes 1048608 | tf_op jit(solution)/shard_map/ppermute | solution.py:763
  146.2 1.2 collective-permute-done.11.come1_ref
  147.4 1.0 copy-done.5
  148.4 4.8 %all-to-all-start.3 = ((bf16[8,144,512]{2,1,0:T(8,128)(2,1)}), bf16[8,144,512]{2,1,0:T(8,128)(2,1)}, u32[]{:S(2)}, u32[]{:S(2)}) async-start(bf16[8,144,512]{2,1,0:T(8,128)(2,1)} %get-tuple-element.63), calls=%async_computation.3 | async-start | bytes 2359296 | tf_op jit(solution)/shard_map/all_to_all | solution.py:738
  153.2 1.2 copy-done.2
  154.4 1.2 copy-done.4
  155.6 1.2 copy-done.6
  156.9 0.5 first_sums.1
  157.3 1.6 collective-permute-start.13
  158.9 0.6 collective-permute-start.14
  159.6 16.2 %backward.1 = (bf16[1,512,512]{2,1,0:T(8,128)(2,1)}, bf16[4,4,72,512]{3,2,1,0:T(8,128)(2,1)}, bf16[4,4,72,512]{3,2,1,0:T(8,128)(2,1)}) custom-call(s32[2]{0:T(128)S(1)} %pad_add_fusion.where_ref.refs_0_, bf16[8,144,512]{2,1,0:T(8,128)(2,1)S(1)} %all-to-all-done.2.refs_1_, bf16[1,512,512]{2,1,0:T(8,128)(2,1)} %refs_2_.5, bf16[1,512,512]{2,1,0:T(8,128)(2,1)} %refs_3_.3, ...), custom_call_target="tpu_custom_call" | custom-call | flops 1000 | bytes 1000 | tf_op jit(solution)/shard_map/backward/pallas_call | solution.py:585
  175.8 6.9 %all-to-all-done.3.out_ref = bf16[8,144,512]{2,1,0:T(8,128)(2,1)} async-done(((bf16[8,144,512]{2,1,0:T(8,128)(2,1)}), bf16[8,144,512]{2,1,0:T(8,128)(2,1)}, u32[]{:S(2)}, u32[]{:S(2)}) %all-to-all-start.3) | async-done | bytes 1179680 | tf_op jit(solution)/shard_map/all_to_all | solution.py:738
  182.7 1.2 second_sums.1
  184.0 3.0 %collective-permute-done.12.b_ref = bf16[4,4,72,512]{3,2,1,0:T(8,128)(2,1)S(1)} collective-permute-done((bf16[4,4,72,512]{3,2,1,0:T(8,128)(2,1)}, bf16[4,4,72,512]{3,2,1,0:T(8,128)(2,1)S(1)}, u32[]{:S(2)}, u32[]{:S(2)}) %collective-permute-start.12) | collective-permute-done | bytes 1179680 | tf_op jit(solution)/shard_map/ppermute | solution.py:763
  187.0 1.3 pair_sum.1
  188.3 3.8 %all-to-all-start.4 = ((bf16[4,4,72,512]{3,2,1,0:T(8,128)(2,1)}), bf16[4,4,72,512]{3,2,1,0:T(8,128)(2,1)S(1)}, u32[]{:S(2)}, u32[]{:S(2)}) async-start(bf16[4,4,72,512]{3,2,1,0:T(8,128)(2,1)} %pair_sum.1), calls=%async_computation.4 | async-start | bytes 2359296 | tf_op jit(solution)/shard_map/all_to_all | solution.py:798
  192.1 3.7 %combine.1 = bf16[1,512,512]{2,1,0:T(8,128)(2,1)} custom-call(bf16[8,144,512]{2,1,0:T(8,128)(2,1)} %all-to-all-done.3.out_ref, s32[2,512]{1,0:T(2,128)S(1)} %get-tuple-element.50.refs_3_.index_ref.refs_4_, f32[512,512]{1,0:T(8,128)} %get-tuple-element.64.resid_ref.refs_12_), custom_call_target="tpu_custom_call" | custom-call | flops 1000 | bytes 1000 | tf_op jit(solution)/shard_map/combine/pallas_call | solution.py:616
  195.8 25.2 %all-to-all-done.4.parts_ref = bf16[4,4,72,512]{3,2,1,0:T(8,128)(2,1)S(1)} async-done(((bf16[4,4,72,512]{3,2,1,0:T(8,128)(2,1)}), bf16[4,4,72,512]{3,2,1,0:T(8,128)(2,1)S(1)}, u32[]{:S(2)}, u32[]{:S(2)}) %all-to-all-start.4) | async-done | bytes 1179680 | tf_op jit(solution)/shard_map/all_to_all | solution.py:798
  221.0 0.1 lead_sum.2
  221.1 12.7 %all_to_all.30.parts_ref = bf16[4,72,512]{2,1,0:T(8,128)(2,1)S(1)} all-to-all(bf16[4,72,512]{2,1,0:T(8,128)(2,1)S(1)} %lead_sum.2), channel_id=1, replica_groups={{0,8,16,24},{4,12,20,28},{1,9,17,25},{5,13,21,29},{2,10,18,26},{6,14,22..., dimensions={0} | all-to-all | bytes 589824 | tf_op jit(solution)/shard_map/all_to_all | solution.py:802
  233.9 9.3 %all-gather = bf16[576,512]{1,0:T(8,128)(2,1)S(1)} all-gather(bf16[72,512]{1,0:T(8,128)(2,1)S(1)} %lead_sum.3), channel_id=2, replica_groups=mesh['rep'=8,'shard'=4] {'rep'}, dimensions={0}, use_global_device_ids=true | all-gather | bytes 663552 | tf_op jit(solution)/shard_map/all_gather | solution.py:804
  243.2 1.0 finish.1
  244.2 10.2 %widen.1 = (f32[2,512,2048]{2,1,0:T(8,128)}, f32[2,512,2048]{2,1,0:T(8,128)}) custom-call(bf16[8,2,2,128,1024]{4,3,2,1,0:T(8,128)(2,1)} %bitcast.18), custom_call_target="tpu_custom_call" | custom-call | flops 1000 | bytes 1000 | tf_op jit(solution)/shard_map/widen/pallas_call | solution.py:675
  (36 shorter events, 0.5 us)
Async XLA Ops:
  8.3 9.2 %collective-permute-start.2 = (bf16[5,16,512]{2,1,0:T(8,128)(2,1)S(1)}, bf16[5,16,512]{2,1,0:T(8,128)(2,1)S(1)}, u32[]{:S(2)}, u32[]{:S(2)}) collective-permute-start(bf16[5,16,512]{2,1,0:T(8,128)(2,1)S(1)} %pack_weights.1), channel_id=1, source_target_pairs={{0,3},{1,2},{2,1},{3,0},{4,7},{5,6},{6,5},{7,4},{8,11},{9,10},{10,... | collective-permute-start | bytes 245768 | tf_op jit(solution)/shard_map/ppermute | solution.py:158
  13.4 6.9 %collective-permute-start.1 = (bf16[5,16,512]{2,1,0:T(8,128)(2,1)S(1)}, bf16[5,16,512]{2,1,0:T(8,128)(2,1)S(1)}, u32[]{:S(2)}, u32[]{:S(2)}) collective-permute-start(bf16[5,16,512]{2,1,0:T(8,128)(2,1)S(1)} %pack_weights.1), channel_id=1, source_target_pairs={{0,2},{1,3},{2,0},{3,1},{4,6},{5,7},{6,4},{7,5},{8,10},{9,11},{10,... | collective-permute-start | bytes 245768 | tf_op jit(solution)/shard_map/ppermute | solution.py:158
  13.4 6.9 %collective-permute-start = (bf16[5,16,512]{2,1,0:T(8,128)(2,1)S(1)}, bf16[5,16,512]{2,1,0:T(8,128)(2,1)S(1)}, u32[]{:S(2)}, u32[]{:S(2)}) collective-permute-start(bf16[5,16,512]{2,1,0:T(8,128)(2,1)S(1)} %pack_weights.1), channel_id=1, source_target_pairs={{0,1},{1,0},{2,3},{3,2},{4,5},{5,4},{6,7},{7,6},{8,9},{9,8},{10,11... | collective-permute-start | bytes 245768 | tf_op jit(solution)/shard_map/ppermute | solution.py:158
  20.2 33.4 %all-to-all-start.1 = ((bf16[8,144,512]{2,1,0:T(8,128)(2,1)}), bf16[8,144,512]{2,1,0:T(8,128)(2,1)S(1)}, u32[]{:S(2)}, u32[]{:S(2)}) async-start(bf16[8,144,512]{2,1,0:T(8,128)(2,1)} %get-tuple-element.53), calls=%async_computation.1 | async-start | bytes 2359296 | tf_op jit(solution)/shard_map/all_to_all | solution.py:738
  24.3 8.7 %collective-permute-start.8 = (bf16[3,4,16,512]{3,2,1,0:T(8,128)(2,1)S(1)}, bf16[3,4,16,512]{3,2,1,0:T(8,128)(2,1)S(1)}, u32[]{:S(2)}, u32[]{:S(2)}) collective-permute-start(bf16[3,4,16,512]{3,2,1,0:T(8,128)(2,1)S(1)} %pad_maximum_fusion.refs_7_), channel_id=1, source_target_pairs={{0,24},{4,28},{8,16},{12,20},{16,8},{20,12},{24,0},{28,4},{1,25},{... | collective-permute-start | bytes 589832 | tf_op jit(solution)/shard_map/ppermute | solution.py:164
  26.8 10.0 %collective-permute-start.6 = (bf16[3,4,16,512]{3,2,1,0:T(8,128)(2,1)S(1)}, bf16[3,4,16,512]{3,2,1,0:T(8,128)(2,1)S(1)}, u32[]{:S(2)}, u32[]{:S(2)}) collective-permute-start(bf16[3,4,16,512]{3,2,1,0:T(8,128)(2,1)S(1)} %pad_maximum_fusion.refs_7_), channel_id=1, source_target_pairs={{0,16},{4,20},{8,24},{12,28},{16,0},{20,4},{24,8},{28,12},{1,17},{... | collective-permute-start | bytes 589832 | tf_op jit(solution)/shard_map/ppermute | solution.py:164
  27.3 9.6 %collective-permute-start.4 = (bf16[3,4,16,512]{3,2,1,0:T(8,128)(2,1)S(1)}, bf16[3,4,16,512]{3,2,1,0:T(8,128)(2,1)S(1)}, u32[]{:S(2)}, u32[]{:S(2)}) collective-permute-start(bf16[3,4,16,512]{3,2,1,0:T(8,128)(2,1)S(1)} %pad_maximum_fusion.refs_7_), channel_id=1, source_target_pairs={{0,8},{4,12},{8,0},{12,4},{16,24},{20,28},{24,16},{28,20},{1,9},{5... | collective-permute-start | bytes 589832 | tf_op jit(solution)/shard_map/ppermute | solution.py:164
  27.8 9.5 %collective-permute-start.3 = (bf16[3,4,16,512]{3,2,1,0:T(8,128)(2,1)S(1)}, bf16[3,4,16,512]{3,2,1,0:T(8,128)(2,1)S(1)}, u32[]{:S(2)}, u32[]{:S(2)}) collective-permute-start(bf16[3,4,16,512]{3,2,1,0:T(8,128)(2,1)S(1)} %pad_maximum_fusion.refs_7_), channel_id=1, source_target_pairs={{0,4},{4,0},{8,12},{12,8},{16,20},{20,16},{24,28},{28,24},{1,5},{5... | collective-permute-start | bytes 589832 | tf_op jit(solution)/shard_map/ppermute | solution.py:166
  33.0 4.4 %collective-permute-start.9 = (bf16[3,4,16,512]{3,2,1,0:T(8,128)(2,1)S(1)}, bf16[3,4,16,512]{3,2,1,0:T(8,128)(2,1)S(1)}, u32[]{:S(2)}, u32[]{:S(2)}) collective-permute-start(bf16[3,4,16,512]{3,2,1,0:T(8,128)(2,1)S(1)} %collective-permute-done.8.refs_13_), channel_id=1, source_target_pairs={{0,4},{4,0},{8,12},{12,8},{16,20},{20,16},{24,28},{28,24},{1,5},{5... | collective-permute-start | bytes 589832 | tf_op jit(solution)/shard_map/ppermute | solution.py:166
  36.8 1.4 collective-permute-start.7
  36.9 1.6 collective-permute-start.5
  53.6 32.9 %all-to-all-start = ((bf16[8,144,512]{2,1,0:T(8,128)(2,1)}), bf16[8,144,512]{2,1,0:T(8,128)(2,1)S(1)}, u32[]{:S(2)}, u32[]{:S(2)}) async-start(bf16[8,144,512]{2,1,0:T(8,128)(2,1)} %get-tuple-element.51), calls=%async_computation | async-start | bytes 2359296 | tf_op jit(solution)/shard_map/all_to_all | solution.py:738
  106.3 42.1 %all-to-all-start.2 = ((bf16[8,144,512]{2,1,0:T(8,128)(2,1)}), bf16[8,144,512]{2,1,0:T(8,128)(2,1)S(1)}, u32[]{:S(2)}, u32[]{:S(2)}) async-start(bf16[8,144,512]{2,1,0:T(8,128)(2,1)} %get-tuple-element.55), calls=%async_computation.2 | async-start | bytes 2359296 | tf_op jit(solution)/shard_map/all_to_all | solution.py:738
  119.7 1.0 copy-start.1
  120.7 25.5 %collective-permute-start.10 = (bf16[2,2,128,1024]{3,2,1,0:T(8,128)(2,1)S(1)}, bf16[2,2,128,1024]{3,2,1,0:T(8,128)(2,1)S(1)}, u32[]{:S(2)}, u32[]{:S(2)}) collective-permute-start(bf16[2,2,128,1024]{3,2,1,0:T(8,128)(2,1)S(1)} %get-tuple-element.60), channel_id=1, source_target_pairs={{0,8},{4,12},{8,0},{12,4},{16,24},{20,28},{24,16},{28,20},{1,9},{5... | collective-permute-start | bytes 3145736 | tf_op jit(solution)/shard_map/ppermute | solution.py:763
  122.2 25.1 %collective-permute-start.11 = (bf16[2,2,128,1024]{3,2,1,0:T(8,128)(2,1)S(1)}, bf16[2,2,128,1024]{3,2,1,0:T(8,128)(2,1)S(1)}, u32[]{:S(2)}, u32[]{:S(2)}) collective-permute-start(bf16[2,2,128,1024]{3,2,1,0:T(8,128)(2,1)S(1)} %get-tuple-element.61), channel_id=1, source_target_pairs={{0,16},{4,20},{8,24},{12,28},{16,0},{20,4},{24,8},{28,12},{1,17},{... | collective-permute-start | bytes 3145736 | tf_op jit(solution)/shard_map/ppermute | solution.py:763
  146.2 2.2 copy-start.3
  147.4 1.0 copy-start.5
  148.4 34.3 %all-to-all-start.3 = ((bf16[8,144,512]{2,1,0:T(8,128)(2,1)}), bf16[8,144,512]{2,1,0:T(8,128)(2,1)}, u32[]{:S(2)}, u32[]{:S(2)}) async-start(bf16[8,144,512]{2,1,0:T(8,128)(2,1)} %get-tuple-element.63), calls=%async_computation.3 | async-start | bytes 2359296 | tf_op jit(solution)/shard_map/all_to_all | solution.py:738
  153.1 91.0 %all-gather.4.cloned.1.call-start = ((), (), s32[]{:S(2)}) async-start(), calls=%async_computation.6 | async-start | bytes 9437184 | tf_op jit(solution)/shard_map/all_gather | solution.py:795
  153.2 1.2 copy-start.2
  154.4 1.2 copy-start.4
  155.6 1.2 copy-start.6
  157.3 18.4 %collective-permute-start.13 = (bf16[2,128,1024]{2,1,0:T(8,128)(2,1)S(1)}, bf16[2,128,1024]{2,1,0:T(8,128)(2,1)S(1)}, u32[]{:S(2)}, u32[]{:S(2)}) collective-permute-start(bf16[2,128,1024]{2,1,0:T(8,128)(2,1)S(1)} %get-tuple-element.86), channel_id=1, source_target_pairs={{0,16},{4,20},{8,24},{12,28},{16,0},{20,4},{24,8},{28,12},{1,17},{... | collective-permute-start | bytes 1572872 | tf_op jit(solution)/shard_map/ppermute | solution.py:763
  158.9 16.9 %collective-permute-start.14 = (bf16[2,128,1024]{2,1,0:T(8,128)(2,1)S(1)}, bf16[2,128,1024]{2,1,0:T(8,128)(2,1)S(1)}, u32[]{:S(2)}, u32[]{:S(2)}) collective-permute-start(bf16[2,128,1024]{2,1,0:T(8,128)(2,1)S(1)} %get-tuple-element.87), channel_id=1, source_target_pairs={{0,8},{4,12},{8,0},{12,4},{16,24},{20,28},{24,16},{28,20},{1,9},{5... | collective-permute-start | bytes 1572872 | tf_op jit(solution)/shard_map/ppermute | solution.py:763
  182.7 4.4 %copy-start = (bf16[4,4,72,512]{3,2,1,0:T(8,128)(2,1)S(1)}, bf16[4,4,72,512]{3,2,1,0:T(8,128)(2,1)}, u32[]{:S(2)}) copy-start(bf16[4,4,72,512]{3,2,1,0:T(8,128)(2,1)} %get-tuple-element.74.a_ref) | copy-start | bytes 3538948
  183.9 3.1 %collective-permute-start.12 = (bf16[4,4,72,512]{3,2,1,0:T(8,128)(2,1)}, bf16[4,4,72,512]{3,2,1,0:T(8,128)(2,1)S(1)}, u32[]{:S(2)}, u32[]{:S(2)}) collective-permute-start(bf16[4,4,72,512]{3,2,1,0:T(8,128)(2,1)} %get-tuple-element.75), channel_id=1, source_target_pairs={{0,4},{4,0},{8,12},{12,8},{16,20},{20,16},{24,28},{28,24},{1,5},{5... | collective-permute-start | bytes 3538952 | tf_op jit(solution)/shard_map/ppermute | solution.py:763
  188.3 32.6 %all-to-all-start.4 = ((bf16[4,4,72,512]{3,2,1,0:T(8,128)(2,1)}), bf16[4,4,72,512]{3,2,1,0:T(8,128)(2,1)S(1)}, u32[]{:S(2)}, u32[]{:S(2)}) async-start(bf16[4,4,72,512]{3,2,1,0:T(8,128)(2,1)} %pair_sum.1), calls=%async_computation.4 | async-start | bytes 2359296 | tf_op jit(solution)/shard_map/all_to_all | solution.py:798
Sparse Core Ops, SparseCore 0:
  184.0 55.8 all-gather.3
where the time goes:
time: 262 us; the launch traced here: 261 us
  waiting for transfers between devices  103 us (39%)
  Pallas kernels  81.5 us (31%)
  starting transfers between devices  34.9 us (13%)
  blocking collectives  22 us (8%)
  between operations  14.2 us (5%)
  local copies, waits for them, and re-layouts  5.65 us (2%)
    all_to_all x4, waiting for transfers between devices, to_experts(): lax.all_to_all(rows, AXES, 0, 0, axis_index_groups=column, tiled=True)  38 us
    ppermute x5, waiting for transfers between devices, peer(): return lax.ppermute(value, 'rep', [(i, i ^ k) for i in range(reps)])  26.7 us
    all_to_all x1, waiting for transfers between devices, shards(): line = lax.all_to_all(chip, 'shard', 0, 0, tiled=True)  25.2 us
    pallas_call x1, Pallas kernels, experts(): pl.pallas_call(experts_body, out_shape=[pltpu.HBM((groups, ROWS, width),...  19.7 us
    pallas_call x1, Pallas kernels, backward(): pl.pallas_call(lambda *refs: backward_body(fast, reps, shards_n, *refs),...  16.2 us
    all_to_all x4, starting transfers between devices, to_experts(): lax.all_to_all(rows, AXES, 0, 0, axis_index_groups=column, tiled=True)  16.1 us
    pallas_call x1, Pallas kernels, forward(): pl.pallas_call(body, out_shape=(*shown, *(pltpu.HBM(*k) for k in kept)),...  13 us
    all_to_all x1, blocking collectives, shards(): lax.all_to_all(line, 'rep', 0, 0, axis_index_groups=plane_groups, tiled=T...  12.7 us
  transfers between devices with their start and end apart: 21, of which 13 were waited for; matrix products, arithmetic and copies ran while one was open for 0% of the time, Pallas kernels for 19%

commit v1 on v0

--- a/solution.py
+++ b/solution.py
@@ -313,7 +313,35 @@
     )(*operands)
 
 
-def expert_rows(n2_ref, cot_ref, w_in_ref, w_out_ref, back_ref, out_ref, span, scratch):
+def cot_hidden_body(where_ref, cot_ref, w_out_ref, through_ref):
+    rows = jnp.concatenate([cot_ref[0], cot_ref[1]], axis=0)
+    for start in range(0, w_out_ref.shape[2], FF_STEP):
+        cols = slice(start, start + FF_STEP)
+        through_ref[:, cols] = dot_nn(rows, w_out_ref[0, :, cols])
+
+
+def cot_hidden(where, cot, w_out):
+    groups, _, width = cot.shape
+    hidden_n = w_out.shape[2]
+    return pl.pallas_call(
+        cot_hidden_body,
+        out_shape=pltpu.HBM((groups * ROWS, hidden_n), F32),
+        grid_spec=pltpu.PrefetchScalarGridSpec(
+            num_scalar_prefetch=1,
+            grid=(groups // 2,),
+            in_specs=[
+                pl.BlockSpec((2, ROWS, width), lambda i, w: (i, 0, 0)),
+                pl.BlockSpec((1, width, hidden_n), lambda i, w: (w[0], 0, 0)),
+            ],
+            out_specs=pl.BlockSpec((2 * ROWS, hidden_n), lambda i, w: (i, 0)),
+        ),
+        compiler_params=params(24),
+        cost_estimate=SMALL,
+        name="cot_hidden",
+    )(where, cot, far(w_out))
+
+
+def expert_rows(n2_ref, cot_ref, through_ref, w_in_ref, w_out_ref, back_ref, out_ref, span, scratch):
     hidden_ref, pre_ref, rows_ref, gso_ref = scratch
     row = iota((ROWS, 1), 0)
     eye = jnp.where(iota((ROWS, ROWS), 0) == iota((ROWS, ROWS), 1), 1.0, 0.0).astype(BF)
@@ -325,8 +353,8 @@
         gates.append(gate)
         rows_all.append(jnp.where(row < SLOTS, rows, BF(0)))
         gso_all.append((gate * cot_ref[g].astype(F32)).astype(BF))
-    rows, gso = jnp.concatenate(rows_all, axis=0), jnp.concatenate(gso_all, axis=0)
-    rows_ref[span], gso_ref[span] = rows, gso
+    rows, gate_col = jnp.concatenate(rows_all, axis=0), jnp.concatenate(gates, axis=0)
+    rows_ref[span], gso_ref[span] = rows, jnp.concatenate(gso_all, axis=0)
     for start in range(0, w_in_ref.shape[2], FF_STEP):
         cols = slice(start, start + FF_STEP)
         u = dot_nn(rows, w_in_ref[0, :, cols])
@@ -336,7 +364,7 @@
         hidden = u * half
         slope = half + hidden * (1.0 - t) * (GELU_A * (1.0 + 3.0 * GELU_B * square))
         hidden_ref[span, cols] = hidden.astype(BF)
-        pre_ref[span, cols] = (dot_nn(gso, w_out_ref[0, :, cols]) * slope).astype(BF)
+        pre_ref[span, cols] = (through_ref[:, cols] * (gate_col * slope)).astype(BF)
     grad_in = dot_nt(pre_ref[span], w_in_ref[0])
     result = dot_nt(hidden_ref[span], w_out_ref[0])
     ones = jnp.ones((8, rows.shape[1]), BF)
@@ -354,10 +382,10 @@
 
 
 def experts_body(where_ref, *refs):
-    expert_rows(*refs[:6], slice(None), refs[6:])
-
-
-def experts(where, n2, cot, w_in, w_out):
+    expert_rows(*refs[:7], slice(None), refs[7:])
+
+
+def experts(where, n2, cot, through, w_in, w_out):
     groups, _, width = n2.shape
     hidden_n = w_in.shape[2]
     total = groups * ROWS
@@ -375,13 +403,13 @@
         grid_spec=pltpu.PrefetchScalarGridSpec(
             num_scalar_prefetch=1,
             grid=(groups // 2,),
-            in_specs=[payload, payload, weight, weight],
+            in_specs=[payload, payload, wide, weight, weight],
             out_specs=[payload, payload, wide, wide, narrow, narrow],
         ),
-        compiler_params=params(40),
+        compiler_params=params(44),
         cost_estimate=SMALL,
         name="experts",
-    )(where, n2, cot, far(w_in), far(w_out))
+    )(where, n2, cot, through, far(w_in), far(w_out))
 
 
 def expert_grads_body(split, where_ref, hidden_ref, pre_ref, rows_ref, gso_ref, *refs):
@@ -660,28 +688,54 @@
     sum_ref[...] = total.astype(BF)
 
 
-def widen_body(every_ref, w_in_ref, w_out_ref):
-    cols = every_ref.shape[-1]
-    for half in range(2):
-        span = slice(half * cols, (half + 1) * cols)
-        w_in_ref[0, :, span] = every_ref[0, half, 0].astype(F32)
-        w_out_ref[0, :, span] = every_ref[0, half, 1].astype(F32)
-
-
-def widen(every, owned):
-    reps, _, _, depth, cols = every.shape
-    out = pltpu.HBM((owned, depth * (reps // owned), 2 * cols), F32)
-    spot = pl.BlockSpec((1, depth, 2 * cols), lambda i: (i % owned, i // owned, 0))
-    return pl.pallas_call(
-        widen_body,
-        out_shape=(out, out),
-        grid=(reps,),
-        in_specs=[pl.BlockSpec((1, *every.shape[1:]), lambda i: (i, 0, 0, 0, 0))],
-        out_specs=(spot, spot),
-        compiler_params=params(12),
+def widen_body(places, aliased, where_ref, *refs):
+    n = len(places)
+    taken, wide, sem_in, sem_out = refs[-4:]
+    outs = refs[-6:-4]
+    srcs = refs[: len(refs) - 6 - 2 * aliased]
+    _, depth, cols = srcs[0].shape[-3:]
+    pieces = [ref.at[half] for ref in srcs for half in range(2)] if len(srcs) < n else srcs
+    fetch = [pltpu.make_async_copy(pieces[i], taken.at[i], sem_in.at[i]) for i in range(n)]
+    for copy in fetch:
+        copy.start()
+    sent = []
+    for i, (other, k, half) in enumerate(places):
+        fetch[i].wait()
+        row = pl.multiple_of((where_ref[1] ^ k) * depth, depth)
+        for which in range(2):
+            wide[i, which] = taken[i, which].astype(F32)
+            spot = outs[which].at[
+                where_ref[0] ^ other, pl.ds(row, depth), half * cols : (half + 1) * cols
+            ]
+            copy = pltpu.make_async_copy(wide.at[i, which], spot, sem_out.at[i, which])
+            copy.start()
+            sent.append(copy)
+    for copy in sent:
+        copy.wait()
+
+
+def widen(where, places, sources, shape, so_far=None):
+    n = len(places)
+    part = sources[0].shape[-3:]
+    aliased = so_far is not None
+    held = pl.BlockSpec(memory_space=pltpu.HBM)
+    operands = [far(source) for source in sources] + (list(so_far) if aliased else [])
+    return pl.pallas_call(
+        lambda *refs: widen_body(places, aliased, *refs),
+        out_shape=(pltpu.HBM(shape, F32), pltpu.HBM(shape, F32)),
+        in_specs=[pl.BlockSpec(memory_space=pltpu.SMEM)] + [held] * len(operands),
+        out_specs=(held, held),
+        scratch_shapes=[
+            pltpu.VMEM((n, *part), BF),
+            pltpu.VMEM((n, *part), F32),
+            pltpu.SemaphoreType.DMA((n,)),
+            pltpu.SemaphoreType.DMA((n, 2)),
+        ],
+        input_output_aliases={len(sources) + 1: 0, len(sources) + 2: 1} if aliased else {},
+        compiler_params=params(24),
         cost_estimate=SMALL,
         name="widen",
-    )(far(every))
+    )(where, *operands)
 
 
 def finish_body(rows, parts_ref, qkv_ref, out_ref, router_ref, gains_ref):
@@ -762,13 +816,14 @@
     def peer(value, k):
         return lax.ppermute(value, "rep", [(i, i ^ k) for i in range(reps)])
 
-    back, out, *parts_in = experts(where, n2_in, cot_in, w_in, w_out)
+    through = cot_hidden(where, cot_in, w_out)
+    back, out, *parts_in = experts(where, n2_in, cot_in, through, w_in, w_out)
     grads = expert_grads(where, fast, *parts_in)
     back_in = to_experts(back)
+    out_in = to_experts(after(out, back_in))
     if fast:
         axes = ((owned, 2 * owned), (2 * owned, owned))
         halves = [peer(grads[2 * half], axes[half][0]) for half in range(2)]
-        back_in, *halves = lax.optimization_barrier((back_in, *halves))
         part = halves[0].shape[1:]
         small_part = jax.ShapeDtypeStruct(part, BF)
         keep, *leaves = plain(
@@ -780,7 +835,7 @@
             halves[1],
         )
         arrived = [peer(leaves[half], axes[half][1]) for half in range(2)]
-    out_in = to_experts(after(out, back_in))
+        back_in = after(back_in, keep)
     grad_tokens, *packs = backward(
         fast,
         reps,
@@ -790,21 +845,32 @@
     )
     result = combine(out_in, index, kept[5])
     if fast:
-        arrived = lax.optimization_barrier((packs[0], out_in, *arrived))[2:]
+        mine, twin, *arrived = lax.optimization_barrier((*packs, *arrived))
         total = plain(second_sums, [jax.ShapeDtypeStruct(keep.shape, BF)], keep, *arrived)
-        every = lax.all_gather(total, "rep", axis=0, tiled=False)
-        mine, twin = packs
+        twin = after(twin, total)
         chip = plain(pair_sum, [jax.ShapeDtypeStruct(mine.shape, BF)], mine, peer(twin, 1))
         line = lax.all_to_all(chip, "shard", 0, 0, tiled=True)
         line = after(line, result)
         line = plain(lead_sum, [jax.ShapeDtypeStruct(line.shape[1:], BF)], line)
+        early = [total] + [peer(total, k * owned) for k in (1, 2)]
+        late = [
+            peer(early[axes[half][0] // owned][half], 3 * owned - axes[half][0]) for half in range(2)
+        ]
+        early += [peer(value, 1) for value in early]
+        shape = (owned, width, hidden)
+        places = [(other, k, half) for other in range(2) for k in range(3) for half in range(2)]
+        so_far = widen(where, places, early, shape)
         plane_groups = [[p * owned + c for p in range(peers)] for c in range(owned)]
         plane = lax.all_to_all(line, "rep", 0, 0, axis_index_groups=plane_groups, tiled=True)
+        plane, *so_far = lax.optimization_barrier((plane, *so_far))
         share = plain(lead_sum, [jax.ShapeDtypeStruct(plane.shape[1:], BF)], plane)
+        share, *late = lax.optimization_barrier((share, *late))
+        late += [peer(value, 1) for value in late]
         parts = lax.all_gather(share, "rep", axis=0, tiled=False)
         grad_qkv, grad_out, grad_router, grad_gains = finish(parts, depth // reps)
         grad_router = grad_router.T
-        grad_w_in, grad_w_out = widen(every, owned)
+        places = [(other, 3, half) for other in range(2) for half in range(2)]
+        grad_w_in, grad_w_out = widen(where, places, late, shape, so_far)
     else:
         share = lax.psum_scatter(grads[0], "rep", scatter_dimension=1, tiled=True)
         every = lax.all_gather(share, "rep", axis=1, tiled=True).astype(F32)

time: 262 us -> 230 us (0.88)
  waiting for transfers between devices: 103 us -> 78.7 us
  between operations: 14.2 us -> 1.1 us
  blocking collectives: 22 us -> 10.4 us
  Pallas kernels: 81.5 us -> 90.8 us
  starting transfers between devices: 34.9 us -> 42.2 us
    all_to_all x1, waiting for transfers between devices: 25.2 us -> 3.21 us  [shards(): line = lax.all_to_all(chip, 'shard', 0, 0, tiled=True)]
    all_to_all x1 -> x0, blocking collectives: 12.7 us -> none  [shards(): lax.all_to_all(line, 'rep', 0, 0, axis_index_groups=plane_groups, tiled=T...]
    pallas_call x1 -> x3, Pallas kernels: 10.2 us -> 18 us  [the longest x2 10.5 us: widen(): pl.pallas_call(lambda *refs: widen_body(places, aliased, *refs), out_shap...]
    ppermute x5 -> x14, waiting for transfers between devices: 26.7 us -> 23.1 us  [peer(): return lax.ppermute(value, 'rep', [(i, i ^ k) for i in range(reps)])]
    ppermute x5 -> x14, starting transfers between devices: 5.31 us -> 8.9 us  [peer(): return lax.ppermute(value, 'rep', [(i, i ^ k) for i in range(reps)])]
    all_to_all x0 -> x1, starting transfers between devices: none -> 3.45 us  [shards(): lax.all_to_all(line, 'rep', 0, 0, axis_index_groups=plane_groups, tiled=T...]
    unnamed x14 -> x12, local copies, waits for them, and re-layouts: 5.63 us -> 2.63 us
    squeeze x0 -> x2, local copies, waits for them, and re-layouts: none -> 2.71 us  [shards(): early[axes[half][0] // owned][half]]
  transfers between devices with their start and end apart: 21 -> 30, of which waited for: 13 -> 14; matrix products, arithmetic and copies ran while one was open for 0% -> 1% of each run, Pallas kernels for 19% -> 29%
where the time goes in v1:
time: 230 us; the launch traced here: 229 us
  Pallas kernels  90.8 us (39%)
  waiting for transfers between devices  78.7 us (34%)
  starting transfers between devices  42.2 us (18%)
  blocking collectives  10.4 us (5%)
  local copies, waits for them, and re-layouts  5.36 us (2%)
    all_to_all x4, waiting for transfers between devices, to_experts(): lax.all_to_all(rows, AXES, 0, 0, axis_index_groups=column, tiled=True)  39 us
    ppermute x14, waiting for transfers between devices, peer(): return lax.ppermute(value, 'rep', [(i, i ^ k) for i in range(reps)])  23.1 us
    pallas_call x1, Pallas kernels, experts(): pl.pallas_call(experts_body, out_shape=[pltpu.HBM((groups, ROWS, width),...  19 us
    pallas_call x1, Pallas kernels, backward(): pl.pallas_call(lambda *refs: backward_body(fast, reps, shards_n, *refs),...  16.2 us
    all_to_all x4, starting transfers between devices, to_experts(): lax.all_to_all(rows, AXES, 0, 0, axis_index_groups=column, tiled=True)  15.3 us
    pallas_call x1, Pallas kernels, forward(): pl.pallas_call(body, out_shape=(*shown, *(pltpu.HBM(*k) for k in kept)),...  13 us
    pallas_call x1, Pallas kernels, expert_grads(): pl.pallas_call(lambda *refs: expert_grads_body(split, *refs), out_shape=g...  10.8 us
    pallas_call x2, Pallas kernels, widen(): pl.pallas_call(lambda *refs: widen_body(places, aliased, *refs), out_shap...  10.5 us
  transfers between devices with their start and end apart: 30, of which 14 were waited for; matrix products, arithmetic and copies ran while one was open for 1% of the time, Pallas kernels for 29%

profile of v1, /device:TPU:0, one launch (start us, length us, event | category | flops | bytes accessed | tf_op | source)
XLA Modules:
  0.0 228.8 jit_solution(14483758899968881971)
XLA Ops:
  0.6 1.1 pack_weights.1
  1.7 3.1 %collective-permute-start = (bf16[5,16,512]{2,1,0:T(8,128)(2,1)S(1)}, bf16[5,16,512]{2,1,0:T(8,128)(2,1)S(1)}, u32[]{:S(2)}, u32[]{:S(2)}) collective-permute-start(bf16[5,16,512]{2,1,0:T(8,128)(2,1)S(1)} %pack_weights.1), channel_id=1, source_target_pairs={{0,1},{1,0},{2,3},{3,2},{4,5},{5,4},{6,7},{7,6},{8,9},{9,8},{10,11... | collective-permute-start | bytes 245768 | tf_op jit(solution)/shard_map/ppermute | solution.py:158
  4.8 2.6 %collective-permute-start.1 = (bf16[5,16,512]{2,1,0:T(8,128)(2,1)S(1)}, bf16[5,16,512]{2,1,0:T(8,128)(2,1)S(1)}, u32[]{:S(2)}, u32[]{:S(2)}) collective-permute-start(bf16[5,16,512]{2,1,0:T(8,128)(2,1)S(1)} %pack_weights.1), channel_id=1, source_target_pairs={{0,2},{1,3},{2,0},{3,1},{4,6},{5,7},{6,4},{7,5},{8,10},{9,11},{10,... | collective-permute-start | bytes 245768 | tf_op jit(solution)/shard_map/ppermute | solution.py:158
  7.4 3.5 %route.1 = (s32[2,512]{1,0:T(2,128)S(1)}, bf16[8,144,512]{2,1,0:T(8,128)(2,1)}) custom-call(s32[2,512]{1,0:T(2,128)} %bitcast.21, s32[1,512]{1,0:T(1,128)} %prio_ref.1, bf16[1,512,512]{2,1,0:T(8,128)(2,1)} %refs_3_.3), custom_call_target="tpu_custom_call" | custom-call | flops 1000 | bytes 1000 | tf_op jit(solution)/shard_map/route/pallas_call | solution.py:113
  10.9 3.1 %collective-permute-done.1 = bf16[5,16,512]{2,1,0:T(8,128)(2,1)S(1)} collective-permute-done((bf16[5,16,512]{2,1,0:T(8,128)(2,1)S(1)}, bf16[5,16,512]{2,1,0:T(8,128)(2,1)S(1)}, u32[]{:S(2)}, u32[]{:S(2)}) %collective-permute-start.1) | collective-permute-done | bytes 81952 | tf_op jit(solution)/shard_map/ppermute | solution.py:158
  14.0 3.8 %all-to-all-start.1 = ((bf16[8,144,512]{2,1,0:T(8,128)(2,1)}), bf16[8,144,512]{2,1,0:T(8,128)(2,1)S(1)}, u32[]{:S(2)}, u32[]{:S(2)}) async-start(bf16[8,144,512]{2,1,0:T(8,128)(2,1)} %get-tuple-element.62), calls=%async_computation.1 | async-start | bytes 2359296 | tf_op jit(solution)/shard_map/all_to_all | solution.py:792
  17.8 1.6 collective-permute-start.4
  19.4 1.5 collective-permute-start.6
  21.4 4.2 %collective-permute-done.4.refs_9_ = bf16[3,4,16,512]{3,2,1,0:T(8,128)(2,1)S(1)} collective-permute-done((bf16[3,4,16,512]{3,2,1,0:T(8,128)(2,1)S(1)}, bf16[3,4,16,512]{3,2,1,0:T(8,128)(2,1)S(1)}, u32[]{:S(2)}, u32[]{:S(2)}) %collective-permute-start.4) | collective-permute-done | bytes 196640 | tf_op jit(solution)/shard_map/ppermute | solution.py:164
  25.6 5.0 %collective-permute-done.6.refs_11_ = bf16[3,4,16,512]{3,2,1,0:T(8,128)(2,1)S(1)} collective-permute-done((bf16[3,4,16,512]{3,2,1,0:T(8,128)(2,1)S(1)}, bf16[3,4,16,512]{3,2,1,0:T(8,128)(2,1)S(1)}, u32[]{:S(2)}, u32[]{:S(2)}) %collective-permute-start.6) | collective-permute-done | bytes 196640 | tf_op jit(solution)/shard_map/ppermute | solution.py:164
  31.3 0.8 collective-permute-done.7.refs_12_
  32.4 13.0 %forward.1 = (bf16[8,144,512]{2,1,0:T(8,128)(2,1)}, bf16[16,512]{1,0:T(8,128)(2,1)S(1)}, f32[8,512]{1,0:T(8,128)S(1)}, bf16[4,512,512]{2,1,0:T(8,128)(2,1)}, bf1...) custom-call(s32[2]{0:T(128)S(1)} %pad_add_fusion.1.refs_0_, ...), custom_call_target="tpu_custom_call" | custom-call | flops 1000 | bytes 1000 | tf_op jit(solution)/shard_map/forward/pallas_call | solution.py:304
  45.3 1.8 all-to-all-done.1.cot_ref.refs_1_
  47.2 3.7 %all-to-all-start = ((bf16[8,144,512]{2,1,0:T(8,128)(2,1)}), bf16[8,144,512]{2,1,0:T(8,128)(2,1)S(1)}, u32[]{:S(2)}, u32[]{:S(2)}) async-start(bf16[8,144,512]{2,1,0:T(8,128)(2,1)} %get-tuple-element.60), calls=%async_computation | async-start | bytes 2359296 | tf_op jit(solution)/shard_map/all_to_all | solution.py:792
  51.0 7.4 %cot_hidden.1.refs_2_ = f32[1152,2048]{1,0:T(8,128)} custom-call(s32[2]{0:T(128)S(1)} %pad_add_fusion.where_ref.refs_0_, bf16[8,144,512]{2,1,0:T(8,128)(2,1)S(1)} %all-to-all-done.1.cot_ref.refs_1_, bf16[2,512,2048]{2,1,0:T(8,128)(2,1)} %refs_4_.3), custom_call_target="tpu_custom_call" | custom-call | flops 1000 | bytes 1000 | tf_op jit(solution)/shard_map/cot_hidden/pallas_call | solution.py:326
  58.4 21.6 %all-to-all-done.refs_0_ = bf16[8,144,512]{2,1,0:T(8,128)(2,1)S(1)} async-done(((bf16[8,144,512]{2,1,0:T(8,128)(2,1)}), bf16[8,144,512]{2,1,0:T(8,128)(2,1)S(1)}, u32[]{:S(2)}, u32[]{:S(2)}) %all-to-all-start) | async-done | bytes 1179680 | tf_op jit(solution)/shard_map/all_to_all | solution.py:792
  80.1 19.0 %experts.1 = (bf16[8,144,512]{2,1,0:T(8,128)(2,1)}, bf16[8,144,512]{2,1,0:T(8,128)(2,1)}, bf16[1152,2048]{1,0:T(8,128)(2,1)}, bf16[1152,2048]{1,0:T(8,128)(2,1)}...) custom-call(s32[2]{0:T(128)S(1)} %pad_add_fusion.where_ref.refs_0_, ...), custom_call_target="tpu_custom_call" | custom-call | flops 1000 | bytes 1000 | tf_op jit(solution)/shard_map/experts/pallas_call | solution.py:396
  99.1 3.6 %all-to-all-start.2 = ((bf16[8,144,512]{2,1,0:T(8,128)(2,1)}), bf16[8,144,512]{2,1,0:T(8,128)(2,1)S(1)}, u32[]{:S(2)}, u32[]{:S(2)}) async-start(bf16[8,144,512]{2,1,0:T(8,128)(2,1)} %get-tuple-element.64), calls=%async_computation.2 | async-start | bytes 2359296 | tf_op jit(solution)/shard_map/all_to_all | solution.py:792
  102.6 10.8 %expert_grads.1 = (bf16[2,2,128,1024]{3,2,1,0:T(8,128)(2,1)}, bf16[2,2,128,1024]{3,2,1,0:T(8,128)(2,1)S(1)}, bf16[2,2,128,1024]{3,2,1,0:T(8,128)(2,1)}, bf16[2,2,128,1024]{3,2,1,0:T(8,128)(2,1)S(1)}) custom-call(s32[2]{0:T(128)S(1)} %pad_add_fusion.where_ref.refs_0_, bf16[1152,2048]{1,0:T(8,128)(2,1)} %get-tuple-element.67.refs_1_, ...), custom_call_target="tpu_custom_call" | custom-call | flops 1000 | bytes 1000 | tf_op jit(solution)/shard_map/expert_grads/pallas_call | solution.py:454
  113.4 1.5 collective-permute-start.10
  114.9 1.5 collective-permute-start.11
  116.4 15.6 %all-to-all-done.2.refs_1_ = bf16[8,144,512]{2,1,0:T(8,128)(2,1)S(1)} async-done(((bf16[8,144,512]{2,1,0:T(8,128)(2,1)}), bf16[8,144,512]{2,1,0:T(8,128)(2,1)S(1)}, u32[]{:S(2)}, u32[]{:S(2)}) %all-to-all-start.2) | async-done | bytes 1179680 | tf_op jit(solution)/shard_map/all_to_all | solution.py:792
  132.0 4.3 %all-to-all-start.3 = ((bf16[8,144,512]{2,1,0:T(8,128)(2,1)}), bf16[8,144,512]{2,1,0:T(8,128)(2,1)}, u32[]{:S(2)}, u32[]{:S(2)}) async-start(bf16[8,144,512]{2,1,0:T(8,128)(2,1)} %get-tuple-element.65), calls=%async_computation.3 | async-start | bytes 2359296 | tf_op jit(solution)/shard_map/all_to_all | solution.py:792
  136.2 3.0 %collective-permute-done.10.come0_ref = bf16[2,2,128,1024]{3,2,1,0:T(8,128)(2,1)} collective-permute-done((bf16[2,2,128,1024]{3,2,1,0:T(8,128)(2,1)}, bf16[2,2,128,1024]{3,2,1,0:T(8,128)(2,1)}, u32[]{:S(2)}, u32[]{:S(2)}) %collective-permute-start.10) | collective-permute-done | bytes 1048608 | tf_op jit(solution)/shard_map/ppermute | solution.py:817
  139.2 1.2 collective-permute-done.11.come1_ref
  140.4 2.2 first_sums.1
  142.6 1.6 collective-permute-start.12
  144.8 16.2 %backward.1 = (bf16[1,512,512]{2,1,0:T(8,128)(2,1)}, bf16[4,4,72,512]{3,2,1,0:T(8,128)(2,1)}, bf16[4,4,72,512]{3,2,1,0:T(8,128)(2,1)}) custom-call(s32[2]{0:T(128)S(1)} %pad_add_fusion.where_ref.refs_0_, bf16[8,144,512]{2,1,0:T(8,128)(2,1)S(1)} %all-to-all-done.2.refs_1_, bf16[1,512,512]{2,1,0:T(8,128)(2,1)} %refs_2_.3, bf16[1,512,512]{2,1,0:T(8,128)(2,1)} %refs_3_.3, ...), custom_call_target="tpu_custom_call" | custom-call | flops 1000 | bytes 1000 | tf_op jit(solution)/shard_map/backward/pallas_call | solution.py:613
  161.3 1.0 copy-done.5
  162.3 1.5 collective-permute-start.15
  164.3 0.8 collective-permute-done.14.b_ref
  165.1 1.3 pair_sum.1
  166.4 4.7 %all-to-all-start.4 = ((bf16[4,4,72,512]{3,2,1,0:T(8,128)(2,1)}), bf16[4,4,72,512]{3,2,1,0:T(8,128)(2,1)S(1)}, u32[]{:S(2)}, u32[]{:S(2)}) async-start(bf16[4,4,72,512]{3,2,1,0:T(8,128)(2,1)} %pair_sum.1), calls=%async_computation.4 | async-start | bytes 2359296 | tf_op jit(solution)/shard_map/all_to_all | solution.py:852
  171.2 16.7 %collective-permute-done.15.refs_2_ = bf16[2,2,128,1024]{3,2,1,0:T(8,128)(2,1)S(1)} collective-permute-done((bf16[2,2,128,1024]{3,2,1,0:T(8,128)(2,1)S(1)}, bf16[2,2,128,1024]{3,2,1,0:T(8,128)(2,1)S(1)}, u32[]{:S(2)}, u32[]{:S(2)}) %collective-permute-start.15) | collective-permute-done | bytes 1048608 | tf_op jit(solution)/shard_map/ppermute | solution.py:817
  187.8 1.3 collective-permute-done.16.refs_3_
  189.2 0.8 slice_bitcast_fusion.1
  190.5 1.9 slice_bitcast_fusion
  192.4 0.7 collective-permute-start.21
  193.1 3.7 %combine.1 = bf16[1,512,512]{2,1,0:T(8,128)(2,1)} custom-call(bf16[8,144,512]{2,1,0:T(8,128)(2,1)} %all-to-all-done.3.out_ref, s32[2,512]{1,0:T(2,128)S(1)} %get-tuple-element.59.refs_3_.index_ref.refs_4_, f32[512,512]{1,0:T(8,128)} %get-tuple-element.66.resid_ref.refs_12_), custom_call_target="tpu_custom_call" | custom-call | flops 1000 | bytes 1000 | tf_op jit(solution)/shard_map/combine/pallas_call | solution.py:644
  196.8 3.2 %all-to-all-done.4.parts_ref = bf16[4,4,72,512]{3,2,1,0:T(8,128)(2,1)S(1)} async-done(((bf16[4,4,72,512]{3,2,1,0:T(8,128)(2,1)}), bf16[4,4,72,512]{3,2,1,0:T(8,128)(2,1)S(1)}, u32[]{:S(2)}, u32[]{:S(2)}) %all-to-all-start.4) | async-done | bytes 1179680 | tf_op jit(solution)/shard_map/all_to_all | solution.py:852
  200.0 0.9 lead_sum.2
  200.8 3.5 %all-to-all-start.5 = ((bf16[4,72,512]{2,1,0:T(8,128)(2,1)}), bf16[4,72,512]{2,1,0:T(8,128)(2,1)S(1)}, u32[]{:S(2)}, u32[]{:S(2)}) async-start(bf16[4,72,512]{2,1,0:T(8,128)(2,1)} %lead_sum.2), calls=%async_computation.5 | async-start | bytes 589824 | tf_op jit(solution)/shard_map/all_to_all | solution.py:864
  204.3 6.8 %widen.2 = (f32[2,512,2048]{2,1,0:T(8,128)}, f32[2,512,2048]{2,1,0:T(8,128)}) custom-call(s32[2]{0:T(128)S(1)} %pad_add_fusion.where_ref.refs_0_, bf16[2,2,128,1024]{3,2,1,0:T(8,128)(2,1)} %copy-done, bf16[2,2,128,1024]{3,2,1,0:T(8,128)(2,1)} %copy-done.2, bf16[2,2,128,1024]{3,2,1,0:T(8,128)(2,1)} %collective-permute-done.16.refs_3_, ...), custom_call_target="tpu_custom_call" | custom-call | flops 1000 | bytes 1000 | tf_op jit(solution)/shard_map/widen/pallas_call | solution.py:723
  211.8 10.4 %all-gather = bf16[576,512]{1,0:T(8,128)(2,1)S(1)} all-gather(bf16[72,512]{1,0:T(8,128)(2,1)S(1)} %lead_sum.3), channel_id=2, replica_groups=mesh['rep'=8,'shard'=4] {'rep'}, dimensions={0}, use_global_device_ids=true | all-gather | bytes 663552 | tf_op jit(solution)/shard_map/all_gather | solution.py:869
  222.2 1.0 finish.1
  223.2 0.8 copy-done.3
  224.0 0.8 copy-done.4
  224.9 3.7 %widen.3 = (f32[2,512,2048]{2,1,0:T(8,128)}, f32[2,512,2048]{2,1,0:T(8,128)}) custom-call(s32[2]{0:T(128)S(1)} %pad_add_fusion.where_ref.refs_0_, bf16[2,128,1024]{2,1,0:T(8,128)(2,1)} %collective-permute-done.20.refs_1_, bf16[2,128,1024]{2,1,0:T(8,128)(2,1)} %collective-permute-done.21.refs_2_, ...), custom_call_target="tpu_custom_call", output_to_operand_aliasing={{0}: (5, {}), {1}: (6, {})} | custom-call | flops 1000 | bytes 1000 | tf_op jit(solution)/shard_map/widen/pallas_call | solution.py:723
  (54 shorter events, 4.0 us)
Async XLA Ops:
  1.7 9.2 %collective-permute-start = (bf16[5,16,512]{2,1,0:T(8,128)(2,1)S(1)}, bf16[5,16,512]{2,1,0:T(8,128)(2,1)S(1)}, u32[]{:S(2)}, u32[]{:S(2)}) collective-permute-start(bf16[5,16,512]{2,1,0:T(8,128)(2,1)S(1)} %pack_weights.1), channel_id=1, source_target_pairs={{0,1},{1,0},{2,3},{3,2},{4,5},{5,4},{6,7},{7,6},{8,9},{9,8},{10,11... | collective-permute-start | bytes 245768 | tf_op jit(solution)/shard_map/ppermute | solution.py:158
  4.8 9.2 %collective-permute-start.1 = (bf16[5,16,512]{2,1,0:T(8,128)(2,1)S(1)}, bf16[5,16,512]{2,1,0:T(8,128)(2,1)S(1)}, u32[]{:S(2)}, u32[]{:S(2)}) collective-permute-start(bf16[5,16,512]{2,1,0:T(8,128)(2,1)S(1)} %pack_weights.1), channel_id=1, source_target_pairs={{0,2},{1,3},{2,0},{3,1},{4,6},{5,7},{6,4},{7,5},{8,10},{9,11},{10,... | collective-permute-start | bytes 245768 | tf_op jit(solution)/shard_map/ppermute | solution.py:158
  7.4 6.6 %collective-permute-start.2 = (bf16[5,16,512]{2,1,0:T(8,128)(2,1)S(1)}, bf16[5,16,512]{2,1,0:T(8,128)(2,1)S(1)}, u32[]{:S(2)}, u32[]{:S(2)}) collective-permute-start(bf16[5,16,512]{2,1,0:T(8,128)(2,1)S(1)} %pack_weights.1), channel_id=1, source_target_pairs={{0,3},{1,2},{2,1},{3,0},{4,7},{5,6},{6,5},{7,4},{8,11},{9,10},{10,... | collective-permute-start | bytes 245768 | tf_op jit(solution)/shard_map/ppermute | solution.py:158
  14.0 33.2 %all-to-all-start.1 = ((bf16[8,144,512]{2,1,0:T(8,128)(2,1)}), bf16[8,144,512]{2,1,0:T(8,128)(2,1)S(1)}, u32[]{:S(2)}, u32[]{:S(2)}) async-start(bf16[8,144,512]{2,1,0:T(8,128)(2,1)} %get-tuple-element.62), calls=%async_computation.1 | async-start | bytes 2359296 | tf_op jit(solution)/shard_map/all_to_all | solution.py:792
  17.8 7.8 %collective-permute-start.4 = (bf16[3,4,16,512]{3,2,1,0:T(8,128)(2,1)S(1)}, bf16[3,4,16,512]{3,2,1,0:T(8,128)(2,1)S(1)}, u32[]{:S(2)}, u32[]{:S(2)}) collective-permute-start(bf16[3,4,16,512]{3,2,1,0:T(8,128)(2,1)S(1)} %pad_maximum_fusion.refs_7_), channel_id=1, source_target_pairs={{0,8},{4,12},{8,0},{12,4},{16,24},{20,28},{24,16},{28,20},{1,9},{5... | collective-permute-start | bytes 589832 | tf_op jit(solution)/shard_map/ppermute | solution.py:164
  19.4 11.2 %collective-permute-start.6 = (bf16[3,4,16,512]{3,2,1,0:T(8,128)(2,1)S(1)}, bf16[3,4,16,512]{3,2,1,0:T(8,128)(2,1)S(1)}, u32[]{:S(2)}, u32[]{:S(2)}) collective-permute-start(bf16[3,4,16,512]{3,2,1,0:T(8,128)(2,1)S(1)} %pad_maximum_fusion.refs_7_), channel_id=1, source_target_pairs={{0,16},{4,20},{8,24},{12,28},{16,0},{20,4},{24,8},{28,12},{1,17},{... | collective-permute-start | bytes 589832 | tf_op jit(solution)/shard_map/ppermute | solution.py:164
  20.9 9.7 %collective-permute-start.8 = (bf16[3,4,16,512]{3,2,1,0:T(8,128)(2,1)S(1)}, bf16[3,4,16,512]{3,2,1,0:T(8,128)(2,1)S(1)}, u32[]{:S(2)}, u32[]{:S(2)}) collective-permute-start(bf16[3,4,16,512]{3,2,1,0:T(8,128)(2,1)S(1)} %pad_maximum_fusion.refs_7_), channel_id=1, source_target_pairs={{0,24},{4,28},{8,16},{12,20},{16,8},{20,12},{24,0},{28,4},{1,25},{... | collective-permute-start | bytes 589832 | tf_op jit(solution)/shard_map/ppermute | solution.py:164
  21.4 9.9 %collective-permute-start.3 = (bf16[3,4,16,512]{3,2,1,0:T(8,128)(2,1)S(1)}, bf16[3,4,16,512]{3,2,1,0:T(8,128)(2,1)S(1)}, u32[]{:S(2)}, u32[]{:S(2)}) collective-permute-start(bf16[3,4,16,512]{3,2,1,0:T(8,128)(2,1)S(1)} %pad_maximum_fusion.refs_7_), channel_id=1, source_target_pairs={{0,4},{4,0},{8,12},{12,8},{16,20},{20,16},{24,28},{28,24},{1,5},{5... | collective-permute-start | bytes 589832 | tf_op jit(solution)/shard_map/ppermute | solution.py:166
  25.6 5.7 %collective-permute-start.5 = (bf16[3,4,16,512]{3,2,1,0:T(8,128)(2,1)S(1)}, bf16[3,4,16,512]{3,2,1,0:T(8,128)(2,1)S(1)}, u32[]{:S(2)}, u32[]{:S(2)}) collective-permute-start(bf16[3,4,16,512]{3,2,1,0:T(8,128)(2,1)S(1)} %collective-permute-done.4.refs_9_), channel_id=1, source_target_pairs={{0,4},{4,0},{8,12},{12,8},{16,20},{20,16},{24,28},{28,24},{1,5},{5... | collective-permute-start | bytes 589832 | tf_op jit(solution)/shard_map/ppermute | solution.py:166
  30.6 1.4 collective-permute-start.7
  30.6 1.7 collective-permute-start.9
  47.2 32.9 %all-to-all-start = ((bf16[8,144,512]{2,1,0:T(8,128)(2,1)}), bf16[8,144,512]{2,1,0:T(8,128)(2,1)S(1)}, u32[]{:S(2)}, u32[]{:S(2)}) async-start(bf16[8,144,512]{2,1,0:T(8,128)(2,1)} %get-tuple-element.60), calls=%async_computation | async-start | bytes 2359296 | tf_op jit(solution)/shard_map/all_to_all | solution.py:792
  99.1 32.9 %all-to-all-start.2 = ((bf16[8,144,512]{2,1,0:T(8,128)(2,1)}), bf16[8,144,512]{2,1,0:T(8,128)(2,1)S(1)}, u32[]{:S(2)}, u32[]{:S(2)}) async-start(bf16[8,144,512]{2,1,0:T(8,128)(2,1)} %get-tuple-element.64), calls=%async_computation.2 | async-start | bytes 2359296 | tf_op jit(solution)/shard_map/all_to_all | solution.py:792
  113.4 25.8 %collective-permute-start.10 = (bf16[2,2,128,1024]{3,2,1,0:T(8,128)(2,1)}, bf16[2,2,128,1024]{3,2,1,0:T(8,128)(2,1)}, u32[]{:S(2)}, u32[]{:S(2)}) collective-permute-start(bf16[2,2,128,1024]{3,2,1,0:T(8,128)(2,1)} %get-tuple-element.72), channel_id=1, source_target_pairs={{0,8},{4,12},{8,0},{12,4},{16,24},{20,28},{24,16},{28,20},{1,9},{5... | collective-permute-start | bytes 3145736 | tf_op jit(solution)/shard_map/ppermute | solution.py:817
  114.9 25.5 %collective-permute-start.11 = (bf16[2,2,128,1024]{3,2,1,0:T(8,128)(2,1)}, bf16[2,2,128,1024]{3,2,1,0:T(8,128)(2,1)}, u32[]{:S(2)}, u32[]{:S(2)}) collective-permute-start(bf16[2,2,128,1024]{3,2,1,0:T(8,128)(2,1)} %get-tuple-element.74), channel_id=1, source_target_pairs={{0,16},{4,20},{8,24},{12,28},{16,0},{20,4},{24,8},{28,12},{1,17},{... | collective-permute-start | bytes 3145736 | tf_op jit(solution)/shard_map/ppermute | solution.py:817
  132.0 34.4 %all-to-all-start.3 = ((bf16[8,144,512]{2,1,0:T(8,128)(2,1)}), bf16[8,144,512]{2,1,0:T(8,128)(2,1)}, u32[]{:S(2)}, u32[]{:S(2)}) async-start(bf16[8,144,512]{2,1,0:T(8,128)(2,1)} %get-tuple-element.65), calls=%async_computation.3 | async-start | bytes 2359296 | tf_op jit(solution)/shard_map/all_to_all | solution.py:792
  142.6 18.3 %collective-permute-start.12 = (bf16[2,128,1024]{2,1,0:T(8,128)(2,1)S(1)}, bf16[2,128,1024]{2,1,0:T(8,128)(2,1)S(1)}, u32[]{:S(2)}, u32[]{:S(2)}) collective-permute-start(bf16[2,128,1024]{2,1,0:T(8,128)(2,1)S(1)} %get-tuple-element.88), channel_id=1, source_target_pairs={{0,16},{4,20},{8,24},{12,28},{16,0},{20,4},{24,8},{28,12},{1,17},{... | collective-permute-start | bytes 1572872 | tf_op jit(solution)/shard_map/ppermute | solution.py:817
  144.2 16.8 %collective-permute-start.13 = (bf16[2,128,1024]{2,1,0:T(8,128)(2,1)S(1)}, bf16[2,128,1024]{2,1,0:T(8,128)(2,1)S(1)}, u32[]{:S(2)}, u32[]{:S(2)}) collective-permute-start(bf16[2,128,1024]{2,1,0:T(8,128)(2,1)S(1)} %get-tuple-element.89), channel_id=1, source_target_pairs={{0,8},{4,12},{8,0},{12,4},{16,24},{20,28},{24,16},{28,20},{1,9},{5... | collective-permute-start | bytes 1572872 | tf_op jit(solution)/shard_map/ppermute | solution.py:817
  161.0 1.3 copy-start.5
  161.0 4.1 %copy-start.1 = (bf16[4,4,72,512]{3,2,1,0:T(8,128)(2,1)S(1)}, bf16[4,4,72,512]{3,2,1,0:T(8,128)(2,1)}, u32[]{:S(2)}) copy-start(bf16[4,4,72,512]{3,2,1,0:T(8,128)(2,1)} %get-tuple-element.90.a_ref) | copy-start | bytes 3538948
  162.3 8.9 %copy-start = (bf16[2,2,128,1024]{3,2,1,0:T(8,128)(2,1)}, bf16[2,2,128,1024]{3,2,1,0:T(8,128)(2,1)S(1)}, u32[]{:S(2)}) copy-start(bf16[2,2,128,1024]{3,2,1,0:T(8,128)(2,1)S(1)} %second_sums.1.refs_1_) | copy-start | bytes 3145732
  162.3 2.8 %collective-permute-start.14 = (bf16[4,4,72,512]{3,2,1,0:T(8,128)(2,1)S(1)}, bf16[4,4,72,512]{3,2,1,0:T(8,128)(2,1)S(1)}, u32[]{:S(2)}, u32[]{:S(2)}) collective-permute-start(bf16[4,4,72,512]{3,2,1,0:T(8,128)(2,1)S(1)} %copy-done.5), channel_id=1, source_target_pairs={{0,4},{4,0},{8,12},{12,8},{16,20},{20,16},{24,28},{28,24},{1,5},{5... | collective-permute-start | bytes 3538952 | tf_op jit(solution)/shard_map/ppermute | solution.py:817
  162.3 25.6 %collective-permute-start.15 = (bf16[2,2,128,1024]{3,2,1,0:T(8,128)(2,1)S(1)}, bf16[2,2,128,1024]{3,2,1,0:T(8,128)(2,1)S(1)}, u32[]{:S(2)}, u32[]{:S(2)}) collective-permute-start(bf16[2,2,128,1024]{3,2,1,0:T(8,128)(2,1)S(1)} %second_sums.1.refs_1_), channel_id=1, source_target_pairs={{0,8},{4,12},{8,0},{12,4},{16,24},{20,28},{24,16},{28,20},{1,9},{5... | collective-permute-start | bytes 3145736 | tf_op jit(solution)/shard_map/ppermute | solution.py:817
  163.8 25.4 %collective-permute-start.16 = (bf16[2,2,128,1024]{3,2,1,0:T(8,128)(2,1)S(1)}, bf16[2,2,128,1024]{3,2,1,0:T(8,128)(2,1)}, u32[]{:S(2)}, u32[]{:S(2)}) collective-permute-start(bf16[2,2,128,1024]{3,2,1,0:T(8,128)(2,1)S(1)} %second_sums.1.refs_1_), channel_id=1, source_target_pairs={{0,16},{4,20},{8,24},{12,28},{16,0},{20,4},{24,8},{28,12},{1,17},{... | collective-permute-start | bytes 3145736 | tf_op jit(solution)/shard_map/ppermute | solution.py:817
  166.4 33.6 %all-to-all-start.4 = ((bf16[4,4,72,512]{3,2,1,0:T(8,128)(2,1)}), bf16[4,4,72,512]{3,2,1,0:T(8,128)(2,1)S(1)}, u32[]{:S(2)}, u32[]{:S(2)}) async-start(bf16[4,4,72,512]{3,2,1,0:T(8,128)(2,1)} %pair_sum.1), calls=%async_computation.4 | async-start | bytes 2359296 | tf_op jit(solution)/shard_map/all_to_all | solution.py:852
  171.1 33.2 %collective-permute-start.17 = (bf16[2,2,128,1024]{3,2,1,0:T(8,128)(2,1)S(1)}, bf16[2,2,128,1024]{3,2,1,0:T(8,128)(2,1)}, u32[]{:S(2)}, u32[]{:S(2)}) collective-permute-start(bf16[2,2,128,1024]{3,2,1,0:T(8,128)(2,1)S(1)} %second_sums.1.refs_1_), channel_id=1, source_target_pairs={{0,4},{4,0},{8,12},{12,8},{16,20},{20,16},{24,28},{28,24},{1,5},{5... | collective-permute-start | bytes 3145736 | tf_op jit(solution)/shard_map/ppermute | solution.py:817
  187.8 8.9 %copy-start.2 = (bf16[2,2,128,1024]{3,2,1,0:T(8,128)(2,1)}, bf16[2,2,128,1024]{3,2,1,0:T(8,128)(2,1)S(1)}, u32[]{:S(2)}) copy-start(bf16[2,2,128,1024]{3,2,1,0:T(8,128)(2,1)S(1)} %collective-permute-done.15.refs_2_) | copy-start | bytes 3145732
  187.8 16.5 %collective-permute-start.18 = (bf16[2,2,128,1024]{3,2,1,0:T(8,128)(2,1)S(1)}, bf16[2,2,128,1024]{3,2,1,0:T(8,128)(2,1)}, u32[]{:S(2)}, u32[]{:S(2)}) collective-permute-start(bf16[2,2,128,1024]{3,2,1,0:T(8,128)(2,1)S(1)} %collective-permute-done.15.refs_2_), channel_id=1, source_target_pairs={{0,4},{4,0},{8,12},{12,8},{16,20},{20,16},{24,28},{28,24},{1,5},{5... | collective-permute-start | bytes 3145736 | tf_op jit(solution)/shard_map/ppermute | solution.py:817
  189.2 15.2 %collective-permute-start.19 = (bf16[2,2,128,1024]{3,2,1,0:T(8,128)(2,1)}, bf16[2,2,128,1024]{3,2,1,0:T(8,128)(2,1)}, u32[]{:S(2)}, u32[]{:S(2)}) collective-permute-start(bf16[2,2,128,1024]{3,2,1,0:T(8,128)(2,1)} %collective-permute-done.16.refs_3_), channel_id=1, source_target_pairs={{0,4},{4,0},{8,12},{12,8},{16,20},{20,16},{24,28},{28,24},{1,5},{5... | collective-permute-start | bytes 3145736 | tf_op jit(solution)/shard_map/ppermute | solution.py:817
  190.0 21.2 %collective-permute-start.20 = (bf16[2,128,1024]{2,1,0:T(8,128)(2,1)}, bf16[2,128,1024]{2,1,0:T(8,128)(2,1)}, u32[]{:S(2)}, u32[]{:S(2)}) collective-permute-start(bf16[2,128,1024]{2,1,0:T(8,128)(2,1)} %slice_bitcast_fusion.1), channel_id=1, source_target_pairs={{0,16},{4,20},{8,24},{12,28},{16,0},{20,4},{24,8},{28,12},{1,17},{... | collective-permute-start | bytes 1572872 | tf_op jit(solution)/shard_map/ppermute | solution.py:817
  192.4 18.8 %collective-permute-start.21 = (bf16[2,128,1024]{2,1,0:T(8,128)(2,1)}, bf16[2,128,1024]{2,1,0:T(8,128)(2,1)}, u32[]{:S(2)}, u32[]{:S(2)}) collective-permute-start(bf16[2,128,1024]{2,1,0:T(8,128)(2,1)} %slice_bitcast_fusion), channel_id=1, source_target_pairs={{0,8},{4,12},{8,0},{12,4},{16,24},{20,28},{24,16},{28,20},{1,9},{5... | collective-permute-start | bytes 1572872 | tf_op jit(solution)/shard_map/ppermute | solution.py:817
  200.8 10.3 %all-to-all-start.5 = ((bf16[4,72,512]{2,1,0:T(8,128)(2,1)}), bf16[4,72,512]{2,1,0:T(8,128)(2,1)S(1)}, u32[]{:S(2)}, u32[]{:S(2)}) async-start(bf16[4,72,512]{2,1,0:T(8,128)(2,1)} %lead_sum.2), calls=%async_computation.5 | async-start | bytes 589824 | tf_op jit(solution)/shard_map/all_to_all | solution.py:864
  211.2 12.0 %collective-permute-start.22 = (bf16[2,128,1024]{2,1,0:T(8,128)(2,1)}, bf16[2,128,1024]{2,1,0:T(8,128)(2,1)S(1)}, u32[]{:S(2)}, u32[]{:S(2)}) collective-permute-start(bf16[2,128,1024]{2,1,0:T(8,128)(2,1)} %collective-permute-done.20.refs_1_), channel_id=1, source_target_pairs={{0,4},{4,0},{8,12},{12,8},{16,20},{20,16},{24,28},{28,24},{1,5},{5... | collective-permute-start | bytes 1572872 | tf_op jit(solution)/shard_map/ppermute | solution.py:817
  211.3 11.9 %collective-permute-start.23 = (bf16[2,128,1024]{2,1,0:T(8,128)(2,1)}, bf16[2,128,1024]{2,1,0:T(8,128)(2,1)S(1)}, u32[]{:S(2)}, u32[]{:S(2)}) collective-permute-start(bf16[2,128,1024]{2,1,0:T(8,128)(2,1)} %collective-permute-done.21.refs_2_), channel_id=1, source_target_pairs={{0,4},{4,0},{8,12},{12,8},{16,20},{20,16},{24,28},{28,24},{1,5},{5... | collective-permute-start | bytes 1572872 | tf_op jit(solution)/shard_map/ppermute | solution.py:817
  223.2 0.8 copy-start.3
  224.0 0.8 copy-start.4

commit v2 on v1

--- a/solution.py
+++ b/solution.py
@@ -9,14 +9,13 @@
 HEAD_DIM = 64
 EXPERTS = 8
 CAPACITY = 135
-ROWS = 144
-SLOTS = 136
+ROWS = 136
 EPS = 1e-06
 F32 = jnp.float32
 BF = jnp.bfloat16
 AXES = ("rep", "shard")
 FF_STEP = 512
-KEPT = 7
+KEPT = 5
 SMALL = pl.CostEstimate(flops=1000, bytes_accessed=1000, transcendentals=0)
 GELU_A = 0.7978845608028654
 GELU_B = 0.044715
@@ -65,6 +64,29 @@
     return jnp.where(
         row == 0, parts[0], jnp.where(row == 1, parts[1], jnp.where(row == 2, parts[2], 0.0))
     )
+
+
+def side_row(pieces, width):
+    wide = jnp.concatenate([pieces, jnp.zeros((8, width - ROWS), F32)], axis=1)
+    row = iota((8, width), 0)
+    moved = jnp.where(
+        row == 0,
+        wide,
+        jnp.where(row == 1, pltpu.roll(wide, ROWS, 1), pltpu.roll(wide, 2 * ROWS, 1)),
+    )
+    return jnp.sum(jnp.where(row < 3, moved, 0.0), axis=0, keepdims=True)
+
+
+def side_parts(side):
+    width = side.shape[1]
+    wide = jnp.broadcast_to(side, (8, width))
+    row = iota((8, width), 0)
+    back = jnp.where(
+        row == 0,
+        wide,
+        jnp.where(row == 1, pltpu.roll(wide, width - ROWS, 1), pltpu.roll(wide, width - 2 * ROWS, 1)),
+    )
+    return jnp.where(row < 3, back, 0.0)[:, 0:ROWS]
 
 
 def far(value):
@@ -198,10 +220,20 @@
         ((HEADS, count, count), BF),
         ((3, count, width), BF),
         ((count, width), BF),
-        ((count, width), BF),
         ((count, width), F32),
-        ((count, width), BF),
-    )
+    )
+
+
+def kept_copies(sources, targets, sem):
+    copies = {
+        i: pltpu.make_async_copy(sources[i], targets[i], sem.at[i]) for i in range(KEPT) if i != 1
+    }
+    for pair in range(HEADS // 2):
+        heads = pl.ds(2 * pair, 2)
+        copies[1, pair] = pltpu.make_async_copy(
+            sources[1].at[heads], targets[1].at[heads], sem.at[KEPT + pair]
+        )
+    return copies
 
 
 def forward_body(fast, n_pieces, *refs):
@@ -213,13 +245,8 @@
         x_ref, seg_ref, index_ref, qkv_ref, out_ref, router_ref, gains_ref = refs[:7]
         refs = refs[7:]
     sent_ref, small_ref, gate_ref, *kept = refs[: 3 + KEPT]
-    full_ref, weights_ref, proj_ref, n1_ref, mixed_ref, resid_ref, n2_ref = held = refs[3 + KEPT : -1]
-    sem = refs[-1]
-
-    def keep(*which):
-        for i in which:
-            pltpu.make_async_copy(held[i], kept[i], sem.at[i]).start()
-
+    full_ref, weights_ref, proj_ref, mixed_ref, resid_ref = held = refs[3 + KEPT : -1]
+    copies = kept_copies(held, kept, refs[-1])
     if fast:
         fill_weights(
             where_ref[0], where_ref[1], qkv_ref, out_ref, smalls_ref, piece_refs, full_ref, small_ref
@@ -235,16 +262,15 @@
             ],
             axis=0,
         ).astype(BF)
-    keep(0)
+    copies[0].start()
     x = x_ref[0].astype(F32)
     count, width = x.shape
     small = small_ref[...].astype(F32)
     unit1, _ = unit_of(x)
     n1 = (unit1 * small[8:9, :]).astype(BF)
-    n1_ref[...] = n1
     for s in range(3):
         proj_ref[s] = dot_nn(n1, full_ref[s]).astype(BF)
-    keep(2, 3)
+    copies[2].start()
     document = jnp.where(iota((8, count), 0) == seg_ref[...], 1.0, 0.0).astype(BF)
     bias = jnp.where(dot_tn(document, document) > 0.5, 0.0, -1e30)
     masks = head_masks(count)
@@ -261,15 +287,14 @@
             weights = (terms * (1.0 / total)).astype(BF)
             weights_ref[2 * pair + half] = weights
             halves.append(dot_nn(weights, v))
+        copies[1, pair].start()
         mixed_ref[:, lanes] = jnp.where(masks[0], halves[0], halves[1]).astype(BF)
-    keep(1, 4)
+    copies[3].start()
     resid = x + dot_nn(mixed_ref[...], full_ref[3])
     resid_ref[...] = resid
-    keep(5)
+    copies[4].start()
     unit2, _ = unit_of(resid)
     n2 = (unit2 * small[9:10, :]).astype(BF)
-    n2_ref[...] = n2
-    keep(6)
     logits = dot_nt(small_ref[...], n2)[0:EXPERTS]
     terms = jnp.exp(logits - jnp.max(logits, axis=0, keepdims=True))
     gates = terms / jnp.sum(terms, axis=0, keepdims=True)
@@ -280,11 +305,11 @@
         pick = (row == index[0:1, :]) | (row == index[1:2, :])
         pick = jnp.where(pick, 1.0, 0.0).astype(BF)
         rows = dot_nn(pick, n2)
-        side = dot_nt(piece_rows(gates[e : e + 1, :]).astype(BF), pick)
-        side = jnp.concatenate([side, jnp.zeros((8, width - ROWS), F32)], axis=1)
-        sent_ref[e] = jnp.concatenate([rows[0:SLOTS], side], axis=0).astype(BF)
-    for i in range(KEPT):
-        pltpu.make_async_copy(held[i], kept[i], sem.at[i]).wait()
+        side = side_row(dot_nt(piece_rows(gates[e : e + 1, :]).astype(BF), pick), width)
+        last = iota((ROWS, 1), 0) == CAPACITY
+        sent_ref[e] = jnp.where(last, side, rows).astype(BF)
+    for copy in copies.values():
+        copy.wait()
 
 
 def forward(fast, where, x, seg, index, weights_in, pieces):
@@ -306,7 +331,10 @@
         out_shape=(*shown, *(pltpu.HBM(*k) for k in kept)),
         in_specs=specs,
         out_specs=(*vmem(3), *([pl.BlockSpec(memory_space=pltpu.HBM)] * KEPT)),
-        scratch_shapes=[*(pltpu.VMEM(*k) for k in kept), pltpu.SemaphoreType.DMA((KEPT,))],
+        scratch_shapes=[
+            *(pltpu.VMEM(*k) for k in kept),
+            pltpu.SemaphoreType.DMA((KEPT + HEADS // 2,)),
+        ],
         compiler_params=params(40),
         cost_estimate=SMALL,
         name="forward",
@@ -314,7 +342,7 @@
 
 
 def cot_hidden_body(where_ref, cot_ref, w_out_ref, through_ref):
-    rows = jnp.concatenate([cot_ref[0], cot_ref[1]], axis=0)
+    rows = jnp.concatenate([cot_ref[g].astype(F32) for g in range(2)], axis=0).astype(BF)
     for start in range(0, w_out_ref.shape[2], FF_STEP):
         cols = slice(start, start + FF_STEP)
         through_ref[:, cols] = dot_nn(rows, w_out_ref[0, :, cols])
@@ -347,14 +375,15 @@
     eye = jnp.where(iota((ROWS, ROWS), 0) == iota((ROWS, ROWS), 1), 1.0, 0.0).astype(BF)
     gates, rows_all, gso_all = [], [], []
     for g in range(2):
-        rows = n2_ref[g]
-        side = rows.astype(F32)[SLOTS:, 0:ROWS].astype(BF)
-        gate = jnp.sum(dot_nt(eye, side), axis=1, keepdims=True)
+        rows = n2_ref[g].astype(F32)
+        parts = side_parts(rows[CAPACITY : CAPACITY + 1]).astype(BF)
+        gate = jnp.sum(dot_nt(eye, parts), axis=1, keepdims=True)
         gates.append(gate)
-        rows_all.append(jnp.where(row < SLOTS, rows, BF(0)))
-        gso_all.append((gate * cot_ref[g].astype(F32)).astype(BF))
-    rows, gate_col = jnp.concatenate(rows_all, axis=0), jnp.concatenate(gates, axis=0)
-    rows_ref[span], gso_ref[span] = rows, jnp.concatenate(gso_all, axis=0)
+        rows_all.append(jnp.where(row < CAPACITY, rows, 0.0))
+        gso_all.append(gate * cot_ref[g].astype(F32))
+    rows = jnp.concatenate(rows_all, axis=0).astype(BF)
+    gate_col = jnp.concatenate(gates, axis=0)
+    rows_ref[span], gso_ref[span] = rows, jnp.concatenate(gso_all, axis=0).astype(BF)
     for start in range(0, w_in_ref.shape[2], FF_STEP):
         cols = slice(start, start + FF_STEP)
         u = dot_nn(rows, w_in_ref[0, :, cols])
@@ -376,9 +405,8 @@
         high = product.astype(BF)
         low = (product - high.astype(F32)).astype(BF)
         inner = dot_nt(ones, high) + dot_nt(ones, low)
-        side = piece_rows(inner[0:1, :])
-        side = jnp.concatenate([side, jnp.zeros((8, out.shape[1] - ROWS), F32)], axis=1)
-        back_ref[g] = jnp.concatenate([grad_in[part][0:SLOTS], side], axis=0).astype(BF)
+        side = side_row(piece_rows(inner[0:1, :]), out.shape[1])
+        back_ref[g] = jnp.where(row == CAPACITY, side, grad_in[part]).astype(BF)
 
 
 def experts_body(where_ref, *refs):
@@ -478,8 +506,8 @@
     for z in range(shards_n):
         for r in range(reps):
             start = z * depth + r * rows
-            span = slice(which * rows, (which + 1) * rows)
-            pack_ref[r % 2, z, r // 2, span, :] = grad[start : start + rows]
+            spot = ((r // 2) * 4 + which) * rows
+            pack_ref[r % 2, z, spot : spot + rows, :] = grad[start : start + rows]
 
 
 def backward_body(fast, reps, shards_n, where_ref, *refs):
@@ -491,15 +519,11 @@
     else:
         grad_x_ref, pack_ref, sums_ref, gp_ref = refs[6 + KEPT : 10 + KEPT]
         refs = refs[10 + KEPT :]
-    full_ref, weights_ref, proj_ref, n1_ref, mixed_ref, resid_ref, n2_ref = held = refs[:-1]
+    full_ref, weights_ref, proj_ref, mixed_ref, resid_ref = held = refs[:-1]
     sem = refs[-1]
-    for i in (5, 6, 4, 0, 2, 1, 3):
-        pltpu.make_async_copy(kept[i], held[i], sem.at[i]).start()
-
-    def need(*which):
-        for i in which:
-            pltpu.make_async_copy(kept[i], held[i], sem.at[i]).wait()
-
+    fetch = kept_copies(kept, held, sem)
+    for which in (4, 0, 3, 2, *((1, pair) for pair in range(HEADS // 2))):
+        fetch[which].start()
     count, width = resid_ref.shape
     small = small_ref[...].astype(F32)
     index = index_ref[...]
@@ -511,7 +535,7 @@
         pick = (row == index[0:1, :]) | (row == index[1:2, :])
         pick = jnp.where(pick, 1.0, 0.0).astype(BF)
         back = back_ref[e]
-        side = back.astype(F32)[SLOTS:, 0:ROWS].astype(BF)
+        side = side_parts(back.astype(F32)[CAPACITY : CAPACITY + 1]).astype(BF)
         rows_h.append(jnp.sum(dot_nn(side, pick), axis=0, keepdims=True))
         grad_n2 = grad_n2 + dot_tn(pick, back)
     inner = jnp.concatenate(rows_h, axis=0)
@@ -520,9 +544,10 @@
         [grad_logits.astype(F32), jnp.zeros((8, count), F32)], axis=0
     ).astype(BF)
     grad_n2 = grad_n2 + dot_tn(wide_logits, small_ref[...])
-    need(5, 6)
-    grad_router = dot_nn(wide_logits, n2_ref[...])[0:EXPERTS]
+    fetch[4].wait()
     unit2, inv2 = unit_of(resid_ref[...])
+    n2 = (unit2 * small[9:10, :]).astype(BF)
+    grad_router = dot_nn(wide_logits, n2)[0:EXPERTS]
     grad_gain2 = jnp.sum(grad_n2 * unit2, axis=0, keepdims=True)
     a = grad_n2 * small[9:10, :]
     grad_resid = cot_ref[0].astype(F32) + inv2 * (
@@ -531,16 +556,18 @@
         - unit2 * jnp.mean(a * unit2, axis=-1, keepdims=True)
     )
     branch = grad_resid.astype(BF)
-    need(4, 0)
+    fetch[0].wait()
+    fetch[3].wait()
     place_grads(fast, reps, shards_n, pack_ref, 3, dot_tn(mixed_ref[...], branch))
     grad_mixed = dot_nt(branch, full_ref[3]).astype(BF)
-    need(2, 1)
+    fetch[2].wait()
     masks = head_masks(count)
     factor = HEAD_DIM**-0.5
     for pair in range(HEADS // 2):
         lanes = slice(pair * 2 * HEAD_DIM, (pair + 1) * 2 * HEAD_DIM)
         q, k, v = proj_ref[0, :, lanes], proj_ref[1, :, lanes], proj_ref[2, :, lanes]
         gm = grad_mixed[:, lanes]
+        fetch[1, pair].wait()
         parts = []
         for half in range(2):
             weights = weights_ref[2 * pair + half]
@@ -554,14 +581,13 @@
         for s in range(3):
             both = jnp.where(masks[0], parts[0][s], parts[1][s])
             gp_ref[s, :, lanes] = (both * factor if s < 2 else both).astype(BF)
-    need(3)
-    n1 = n1_ref[...]
+    unit1, inv1 = unit_of(x_ref[0].astype(F32))
+    n1 = (unit1 * small[8:9, :]).astype(BF)
     grad_n1 = jnp.zeros((count, width), F32)
     for s in range(3):
         grads = gp_ref[s]
         place_grads(fast, reps, shards_n, pack_ref, s, dot_tn(n1, grads))
         grad_n1 = grad_n1 + dot_nt(grads, full_ref[s])
-    unit1, inv1 = unit_of(x_ref[0].astype(F32))
     grad_gain1 = jnp.sum(grad_n1 * unit1, axis=0, keepdims=True)
     b = grad_n1 * small[8:9, :]
     grad_x = grad_resid + inv1 * (
@@ -579,11 +605,10 @@
     depth = width // shards_n
     rows = depth // reps
     for z in range(shards_n):
-        for r in range(reps):
-            two = sums[2 * r : 2 * r + 2, z * depth : (z + 1) * depth]
-            two = jnp.concatenate([two, jnp.zeros((6, depth), F32)], axis=0)
-            two = jnp.concatenate([two, jnp.zeros((8, width - depth), F32)], axis=1)
-            pack_ref[r % 2, z, r // 2, 4 * rows :, :] = two.astype(BF)
+        for half in range(2):
+            eight = sums[8 * half : 8 * half + 8, z * depth : (z + 1) * depth]
+            eight = jnp.concatenate([eight, jnp.zeros((8, width - depth), F32)], axis=1)
+            pack_ref[half, z, 2 * reps * rows :, :] = eight.astype(BF)
     copies = [
         pltpu.make_async_copy(pack_ref.at[core ^ i], (mine_ref, twin_ref)[i], sem.at[i])
         for i in range(2)
@@ -600,7 +625,7 @@
     outs = [jax.ShapeDtypeStruct(x.shape, BF)]
     scratch = [pltpu.VMEM((3, count, width), BF)]
     if fast:
-        part = (shards_n, reps // 2, 4 * (width // shards_n // reps) + 8, width)
+        part = (shards_n, 2 * reps * (width // shards_n // reps) + 8, width)
         outs += [pltpu.HBM(part, BF)] * 2
         out_specs = vmem(1) + [pl.BlockSpec(memory_space=pltpu.HBM)] * 2
         scratch = [pltpu.VMEM((2, *part), BF)] + scratch
@@ -620,7 +645,7 @@
         scratch_shapes=[
             *scratch,
             *(pltpu.VMEM(*k) for k in kept_shapes(count, width)),
-            pltpu.SemaphoreType.DMA((KEPT,)),
+            pltpu.SemaphoreType.DMA((KEPT + HEADS // 2,)),
         ],
         compiler_params=params(40),
         cost_estimate=SMALL,
@@ -741,17 +766,20 @@
 def finish_body(rows, parts_ref, qkv_ref, out_ref, router_ref, gains_ref):
     reps = parts_ref.shape[0]
     depth = out_ref.shape[0]
-    smalls = []
     for r in range(reps):
         for s in range(3):
             qkv_ref[s, r * rows : (r + 1) * rows, :] = parts_ref[
                 r, s * rows : (s + 1) * rows, :
             ].astype(F32)
         out_ref[r * rows : (r + 1) * rows, :] = parts_ref[r, 3 * rows : 4 * rows, :].astype(F32)
-        smalls.append(parts_ref[r].astype(F32)[4 * rows : 4 * rows + 2, 0:depth])
-    small = jnp.concatenate(smalls, axis=0)
-    router_ref[...] = small[0:EXPERTS]
-    gains_ref[...] = small[EXPERTS : EXPERTS + 2]
+    smalls = []
+    for half in range(2):
+        total = jnp.zeros((8, depth), F32)
+        for peer in range(reps // 2):
+            total = total + parts_ref[2 * peer + half].astype(F32)[4 * rows :, 0:depth]
+        smalls.append(total)
+    router_ref[...] = smalls[0]
+    gains_ref[...] = smalls[1][0:2]
 
 
 def finish(parts, rows):
@@ -843,15 +871,17 @@
         where,
         [back_in, tokens, cotangent, index, small, gates, *kept],
     )
-    result = combine(out_in, index, kept[5])
+    result = combine(out_in, index, kept[4])
     if fast:
         mine, twin, *arrived = lax.optimization_barrier((*packs, *arrived))
         total = plain(second_sums, [jax.ShapeDtypeStruct(keep.shape, BF)], keep, *arrived)
         twin = after(twin, total)
         chip = plain(pair_sum, [jax.ShapeDtypeStruct(mine.shape, BF)], mine, peer(twin, 1))
-        line = lax.all_to_all(chip, "shard", 0, 0, tiled=True)
-        line = after(line, result)
+        line = lax.all_to_all(after(chip, out_in), "shard", 0, 0, tiled=True)
         line = plain(lead_sum, [jax.ShapeDtypeStruct(line.shape[1:], BF)], line)
+        tall = 2 * depth
+        own_small = line[tall:]
+        line = line[:tall].reshape(peers, tall // peers, width)
         early = [total] + [peer(total, k * owned) for k in (1, 2)]
         late = [
             peer(early[axes[half][0] // owned][half], 3 * owned - axes[half][0]) for half in range(2)
@@ -864,13 +894,17 @@
         plane = lax.all_to_all(line, "rep", 0, 0, axis_index_groups=plane_groups, tiled=True)
         plane, *so_far = lax.optimization_barrier((plane, *so_far))
         share = plain(lead_sum, [jax.ShapeDtypeStruct(plane.shape[1:], BF)], plane)
+        share = jnp.concatenate([share, own_small], axis=0)
         share, *late = lax.optimization_barrier((share, *late))
         late += [peer(value, 1) for value in late]
-        parts = lax.all_gather(share, "rep", axis=0, tiled=False)
+        parts = lax.all_to_all(
+            jnp.broadcast_to(share, (reps, *share.shape)), "rep", 0, 0, tiled=True
+        )
+        places = [(other, 3, half) for other in range(2) for half in range(2)]
+        grad_w_in, grad_w_out = widen(where, places, late, shape, so_far)
+        parts = after(parts, grad_w_in, result)
         grad_qkv, grad_out, grad_router, grad_gains = finish(parts, depth // reps)
         grad_router = grad_router.T
-        places = [(other, 3, half) for other in range(2) for half in range(2)]
-        grad_w_in, grad_w_out = widen(where, places, late, shape, so_far)
     else:
         share = lax.psum_scatter(grads[0], "rep", scatter_dimension=1, tiled=True)
         every = lax.all_gather(share, "rep", axis=1, tiled=True).astype(F32)

time: 230 us -> 225 us (0.978)
  blocking collectives: 10.4 us -> 0 us
  starting transfers between devices: 42.2 us -> 47.7 us
  local copies, waits for them, and re-layouts: 5.36 us -> 8.87 us
  Pallas kernels: 90.8 us -> 87.7 us
    all_gather x1 -> x0, blocking collectives: 10.4 us -> none  [shards(): parts = lax.all_gather(share, 'rep', axis=0, tiled=False)]
    all_to_all x1 -> x2, starting transfers between devices: 4.74 us -> 8.27 us  [the longest x1 4.73 us: shards(): line = lax.all_to_all(after(chip, out_in), 'shard', 0, 0, tiled=True)]
    pallas_call x1, Pallas kernels: 13 us -> 10.4 us  [forward(): pl.pallas_call(body, out_shape=(*shown, *(pltpu.HBM(*k) for k in kept)),...]
  transfers between devices with their start and end apart: 30 -> 31, of which waited for: 14 -> 17; matrix products, arithmetic and copies ran while one was open for 1% -> 2% of each run, Pallas kernels for 29% -> 30%
where the time goes in v2:
time: 225 us; the launch traced here: 224 us
  Pallas kernels  87.7 us (39%)
  waiting for transfers between devices  79.1 us (35%)
  starting transfers between devices  47.7 us (21%)
  local copies, waits for them, and re-layouts  8.87 us (4%)
    all_to_all x4, waiting for transfers between devices, to_experts(): lax.all_to_all(rows, AXES, 0, 0, axis_index_groups=column, tiled=True)  38 us
    ppermute x14, waiting for transfers between devices, peer(): return lax.ppermute(value, 'rep', [(i, i ^ k) for i in range(reps)])  23.5 us
    pallas_call x1, Pallas kernels, experts(): pl.pallas_call(experts_body, out_shape=[pltpu.HBM((groups, ROWS, width),...  18.9 us
    pallas_call x1, Pallas kernels, backward(): pl.pallas_call(lambda *refs: backward_body(fast, reps, shards_n, *refs),...  16.9 us
    all_to_all x4, starting transfers between devices, to_experts(): lax.all_to_all(rows, AXES, 0, 0, axis_index_groups=column, tiled=True)  15.5 us
    ppermute x14, starting transfers between devices, peer(): return lax.ppermute(value, 'rep', [(i, i ^ k) for i in range(reps)])  10.7 us
    pallas_call x1, Pallas kernels, expert_grads(): pl.pallas_call(lambda *refs: expert_grads_body(split, *refs), out_shape=g...  10.7 us
    pallas_call x2, Pallas kernels, widen(): pl.pallas_call(lambda *refs: widen_body(places, aliased, *refs), out_shap...  10.5 us
  transfers between devices with their start and end apart: 31, of which 17 were waited for; matrix products, arithmetic and copies ran while one was open for 2% of the time, Pallas kernels for 30%

profile of v2, /device:TPU:0, one launch (start us, length us, event | category | flops | bytes accessed | tf_op | source)
XLA Modules:
  0.0 224.4 jit_solution(14456642446516876666)
XLA Ops:
  0.6 1.1 pack_weights.1
  1.7 5.1 %collective-permute-start.2 = (bf16[5,16,512]{2,1,0:T(8,128)(2,1)S(1)}, bf16[5,16,512]{2,1,0:T(8,128)(2,1)S(1)}, u32[]{:S(2)}, u32[]{:S(2)}) collective-permute-start(bf16[5,16,512]{2,1,0:T(8,128)(2,1)S(1)} %pack_weights.1), channel_id=1, source_target_pairs={{0,3},{1,2},{2,1},{3,0},{4,7},{5,6},{6,5},{7,4},{8,11},{9,10},{10,... | collective-permute-start | bytes 245768 | tf_op jit(solution)/shard_map/ppermute | solution.py:180
  7.5 3.5 %route.1 = (s32[2,512]{1,0:T(2,128)S(1)}, bf16[8,136,512]{2,1,0:T(8,128)(2,1)}) custom-call(s32[2,512]{1,0:T(2,128)} %bitcast.20, s32[1,512]{1,0:T(1,128)} %prio_ref.1, bf16[1,512,512]{2,1,0:T(8,128)(2,1)} %refs_3_.3), custom_call_target="tpu_custom_call" | custom-call | flops 1000 | bytes 1000 | tf_op jit(solution)/shard_map/route/pallas_call | solution.py:135
  10.9 2.8 %collective-permute-done.1 = bf16[5,16,512]{2,1,0:T(8,128)(2,1)S(1)} collective-permute-done((bf16[5,16,512]{2,1,0:T(8,128)(2,1)S(1)}, bf16[5,16,512]{2,1,0:T(8,128)(2,1)S(1)}, u32[]{:S(2)}, u32[]{:S(2)}) %collective-permute-start.1) | collective-permute-done | bytes 81952 | tf_op jit(solution)/shard_map/ppermute | solution.py:180
  13.7 4.0 %all-to-all-start.1 = ((bf16[8,136,512]{2,1,0:T(8,128)(2,1)}), bf16[8,136,512]{2,1,0:T(8,128)(2,1)S(1)}, u32[]{:S(2)}, u32[]{:S(2)}) async-start(bf16[8,136,512]{2,1,0:T(8,128)(2,1)} %get-tuple-element.61), calls=%async_computation.1 | async-start | bytes 2228224 | tf_op jit(solution)/shard_map/all_to_all | solution.py:820
  17.7 2.5 %collective-permute-start.8 = (bf16[3,4,16,512]{3,2,1,0:T(8,128)(2,1)S(1)}, bf16[3,4,16,512]{3,2,1,0:T(8,128)(2,1)S(1)}, u32[]{:S(2)}, u32[]{:S(2)}) collective-permute-start(bf16[3,4,16,512]{3,2,1,0:T(8,128)(2,1)S(1)} %pad_maximum_fusion.refs_7_), channel_id=1, source_target_pairs={{0,24},{4,28},{8,16},{12,20},{16,8},{20,12},{24,0},{28,4},{1,25},{... | collective-permute-start | bytes 589832 | tf_op jit(solution)/shard_map/ppermute | solution.py:186
  21.3 5.1 %collective-permute-done.8.refs_13_ = bf16[3,4,16,512]{3,2,1,0:T(8,128)(2,1)S(1)} collective-permute-done((bf16[3,4,16,512]{3,2,1,0:T(8,128)(2,1)S(1)}, bf16[3,4,16,512]{3,2,1,0:T(8,128)(2,1)S(1)}, u32[]{:S(2)}, u32[]{:S(2)}) %collective-permute-start.8) | collective-permute-done | bytes 196640 | tf_op jit(solution)/shard_map/ppermute | solution.py:186
  26.4 3.8 %collective-permute-done.6.refs_11_ = bf16[3,4,16,512]{3,2,1,0:T(8,128)(2,1)S(1)} collective-permute-done((bf16[3,4,16,512]{3,2,1,0:T(8,128)(2,1)S(1)}, bf16[3,4,16,512]{3,2,1,0:T(8,128)(2,1)S(1)}, u32[]{:S(2)}, u32[]{:S(2)}) %collective-permute-start.6) | collective-permute-done | bytes 196640 | tf_op jit(solution)/shard_map/ppermute | solution.py:186
  30.9 0.8 collective-permute-done.7.refs_12_
  32.0 10.4 %forward.1 = (bf16[8,136,512]{2,1,0:T(8,128)(2,1)}, bf16[16,512]{1,0:T(8,128)(2,1)S(1)}, f32[8,512]{1,0:T(8,128)S(1)}, bf16[4,512,512]{2,1,0:T(8,128)(2,1)}, bf1...) custom-call(s32[2]{0:T(128)S(1)} %pad_add_fusion.1.refs_0_, ...), custom_call_target="tpu_custom_call" | custom-call | flops 1000 | bytes 1000 | tf_op jit(solution)/shard_map/forward/pallas_call | solution.py:329
  42.4 3.3 %all-to-all-done.1.cot_ref.refs_1_ = bf16[8,136,512]{2,1,0:T(8,128)(2,1)S(1)} async-done(((bf16[8,136,512]{2,1,0:T(8,128)(2,1)}), bf16[8,136,512]{2,1,0:T(8,128)(2,1)S(1)}, u32[]{:S(2)}, u32[]{:S(2)}) %all-to-all-start.1) | async-done | bytes 1114144 | tf_op jit(solution)/shard_map/all_to_all | solution.py:820
  45.7 3.7 %all-to-all-start = ((bf16[8,136,512]{2,1,0:T(8,128)(2,1)}), bf16[8,136,512]{2,1,0:T(8,128)(2,1)S(1)}, u32[]{:S(2)}, u32[]{:S(2)}) async-start(bf16[8,136,512]{2,1,0:T(8,128)(2,1)} %get-tuple-element.59), calls=%async_computation | async-start | bytes 2228224 | tf_op jit(solution)/shard_map/all_to_all | solution.py:820
  49.5 7.2 %cot_hidden.1.refs_2_ = f32[1088,2048]{1,0:T(8,128)} custom-call(s32[2]{0:T(128)S(1)} %pad_add_fusion.where_ref.refs_0_, bf16[8,136,512]{2,1,0:T(8,128)(2,1)S(1)} %all-to-all-done.1.cot_ref.refs_1_, bf16[2,512,2048]{2,1,0:T(8,128)(2,1)} %refs_4_.3), custom_call_target="tpu_custom_call" | custom-call | flops 1000 | bytes 1000 | tf_op jit(solution)/shard_map/cot_hidden/pallas_call | solution.py:354
  56.8 20.4 %all-to-all-done.refs_0_ = bf16[8,136,512]{2,1,0:T(8,128)(2,1)S(1)} async-done(((bf16[8,136,512]{2,1,0:T(8,128)(2,1)}), bf16[8,136,512]{2,1,0:T(8,128)(2,1)S(1)}, u32[]{:S(2)}, u32[]{:S(2)}) %all-to-all-start) | async-done | bytes 1114144 | tf_op jit(solution)/shard_map/all_to_all | solution.py:820
  77.2 18.9 %experts.1 = (bf16[8,136,512]{2,1,0:T(8,128)(2,1)}, bf16[8,136,512]{2,1,0:T(8,128)(2,1)}, bf16[1088,2048]{1,0:T(8,128)(2,1)}, bf16[1088,2048]{1,0:T(8,128)(2,1)}...) custom-call(s32[2]{0:T(128)S(1)} %pad_add_fusion.where_ref.refs_0_, ...), custom_call_target="tpu_custom_call" | custom-call | flops 1000 | bytes 1000 | tf_op jit(solution)/shard_map/experts/pallas_call | solution.py:424
  96.1 3.6 %all-to-all-start.2 = ((bf16[8,136,512]{2,1,0:T(8,128)(2,1)}), bf16[8,136,512]{2,1,0:T(8,128)(2,1)S(1)}, u32[]{:S(2)}, u32[]{:S(2)}) async-start(bf16[8,136,512]{2,1,0:T(8,128)(2,1)} %get-tuple-element.63), calls=%async_computation.2 | async-start | bytes 2228224 | tf_op jit(solution)/shard_map/all_to_all | solution.py:820
  99.7 10.7 %expert_grads.1 = (bf16[2,2,128,1024]{3,2,1,0:T(8,128)(2,1)}, bf16[2,2,128,1024]{3,2,1,0:T(8,128)(2,1)S(1)}, bf16[2,2,128,1024]{3,2,1,0:T(8,128)(2,1)}, bf16[2,2,128,1024]{3,2,1,0:T(8,128)(2,1)S(1)}) custom-call(s32[2]{0:T(128)S(1)} %pad_add_fusion.where_ref.refs_0_, bf16[1088,2048]{1,0:T(8,128)(2,1)} %get-tuple-element.66.refs_1_, ...), custom_call_target="tpu_custom_call" | custom-call | flops 1000 | bytes 1000 | tf_op jit(solution)/shard_map/expert_grads/pallas_call | solution.py:482
  110.3 1.5 collective-permute-start.10
  111.8 1.5 collective-permute-start.11
  113.3 14.3 %all-to-all-done.2.refs_1_ = bf16[8,136,512]{2,1,0:T(8,128)(2,1)S(1)} async-done(((bf16[8,136,512]{2,1,0:T(8,128)(2,1)}), bf16[8,136,512]{2,1,0:T(8,128)(2,1)S(1)}, u32[]{:S(2)}, u32[]{:S(2)}) %all-to-all-start.2) | async-done | bytes 1114144 | tf_op jit(solution)/shard_map/all_to_all | solution.py:820
  127.6 4.2 %all-to-all-start.3 = ((bf16[8,136,512]{2,1,0:T(8,128)(2,1)}), bf16[8,136,512]{2,1,0:T(8,128)(2,1)}, u32[]{:S(2)}, u32[]{:S(2)}) async-start(bf16[8,136,512]{2,1,0:T(8,128)(2,1)} %get-tuple-element.64), calls=%async_computation.3 | async-start | bytes 2228224 | tf_op jit(solution)/shard_map/all_to_all | solution.py:820
  131.8 4.3 %collective-permute-done.10.come0_ref = bf16[2,2,128,1024]{3,2,1,0:T(8,128)(2,1)} collective-permute-done((bf16[2,2,128,1024]{3,2,1,0:T(8,128)(2,1)}, bf16[2,2,128,1024]{3,2,1,0:T(8,128)(2,1)}, u32[]{:S(2)}, u32[]{:S(2)}) %collective-permute-start.10) | collective-permute-done | bytes 1048608 | tf_op jit(solution)/shard_map/ppermute | solution.py:845
  136.1 1.2 collective-permute-done.11.come1_ref
  137.3 2.2 first_sums.1
  139.5 1.6 collective-permute-start.12
  141.7 16.9 %backward.1 = (bf16[1,512,512]{2,1,0:T(8,128)(2,1)}, bf16[4,264,512]{2,1,0:T(8,128)(2,1)}, bf16[4,264,512]{2,1,0:T(8,128)(2,1)}) custom-call(s32[2]{0:T(128)S(1)} %pad_add_fusion.where_ref.refs_0_, bf16[8,136,512]{2,1,0:T(8,128)(2,1)S(1)} %all-to-all-done.2.refs_1_, bf16[1,512,512]{2,1,0:T(8,128)(2,1)} %refs_2_.3, bf16[1,512,512]{2,1,0:T(8,128)(2,1)} %refs_3_.3, ...), custom_call_target="tpu_custom_call" | custom-call | flops 1000 | bytes 1000 | tf_op jit(solution)/shard_map/backward/pallas_call | solution.py:638
  158.8 1.0 copy-done.5
  160.3 1.5 collective-permute-start.15
  162.5 1.2 pair_sum.1
  163.8 4.7 %all-to-all-start.4 = ((bf16[4,264,512]{2,1,0:T(8,128)(2,1)}), bf16[4,264,512]{2,1,0:T(8,128)(2,1)S(1)}, u32[]{:S(2)}, u32[]{:S(2)}) async-start(bf16[4,264,512]{2,1,0:T(8,128)(2,1)} %pair_sum.1), calls=%async_computation.4 | async-start | bytes 2162688 | tf_op jit(solution)/shard_map/all_to_all | solution.py:880
  168.5 17.0 %collective-permute-done.16.refs_3_ = bf16[2,2,128,1024]{3,2,1,0:T(8,128)(2,1)} collective-permute-done((bf16[2,2,128,1024]{3,2,1,0:T(8,128)(2,1)S(1)}, bf16[2,2,128,1024]{3,2,1,0:T(8,128)(2,1)}, u32[]{:S(2)}, u32[]{:S(2)}) %collective-permute-start.16) | collective-permute-done | bytes 1048608 | tf_op jit(solution)/shard_map/ppermute | solution.py:845
  186.0 1.9 slice_bitcast_fusion
  187.9 1.5 collective-permute-start.21
  189.4 1.9 slice_bitcast_fusion.1
  191.2 1.2 collective-permute-start.20
  192.5 2.7 %all-to-all-done.4.parts_ref = bf16[4,264,512]{2,1,0:T(8,128)(2,1)S(1)} async-done(((bf16[4,264,512]{2,1,0:T(8,128)(2,1)}), bf16[4,264,512]{2,1,0:T(8,128)(2,1)S(1)}, u32[]{:S(2)}, u32[]{:S(2)}) %all-to-all-start.4) | async-done | bytes 1081376 | tf_op jit(solution)/shard_map/all_to_all | solution.py:880
  195.4 0.7 slice.51
  196.1 3.4 %all-to-all-start.5 = ((bf16[4,64,512]{2,1,0:T(8,128)(2,1)}), bf16[4,64,512]{2,1,0:T(8,128)(2,1)S(1)}, u32[]{:S(2)}, u32[]{:S(2)}) async-start(bf16[4,64,512]{2,1,0:T(8,128)(2,1)} %bitcast.10), calls=%async_computation.5 | async-start | bytes 524288 | tf_op jit(solution)/shard_map/all_to_all | solution.py:894
  199.5 1.0 copy-done.2
  200.5 6.8 %widen.2 = (f32[2,512,2048]{2,1,0:T(8,128)}, f32[2,512,2048]{2,1,0:T(8,128)}) custom-call(s32[2]{0:T(128)S(1)} %pad_add_fusion.where_ref.refs_0_, bf16[2,2,128,1024]{3,2,1,0:T(8,128)(2,1)} %copy-done, bf16[2,2,128,1024]{3,2,1,0:T(8,128)(2,1)} %collective-permute-done.15.refs_2_, bf16[2,2,128,1024]{3,2,1,0:T(8,128)(2,1)} %collective-permute-done.16.refs_3_, ...), custom_call_target="tpu_custom_call" | custom-call | flops 1000 | bytes 1000 | tf_op jit(solution)/shard_map/widen/pallas_call | solution.py:748
  208.7 0.9 broadcast_in_dim.3
  209.5 3.5 %all-to-all-start.6 = ((bf16[8,72,512]{2,1,0:T(8,128)(2,1)}), bf16[8,72,512]{2,1,0:T(8,128)(2,1)S(1)}, u32[]{:S(2)}, u32[]{:S(2)}) async-start(bf16[8,72,512]{2,1,0:T(8,128)(2,1)} %broadcast_in_dim.3), calls=%async_computation.6 | async-start | bytes 1179648 | tf_op jit(solution)/shard_map/all_to_all | solution.py:900
  213.1 3.7 %combine.1 = bf16[1,512,512]{2,1,0:T(8,128)(2,1)} custom-call(bf16[8,136,512]{2,1,0:T(8,128)(2,1)} %all-to-all-done.3.out_ref, s32[2,512]{1,0:T(2,128)S(1)} %get-tuple-element.58.refs_3_.index_ref.refs_4_, f32[512,512]{1,0:T(8,128)} %get-tuple-element.65.resid_ref.refs_11_), custom_call_target="tpu_custom_call" | custom-call | flops 1000 | bytes 1000 | tf_op jit(solution)/shard_map/combine/pallas_call | solution.py:669
  216.8 0.8 copy-done.3
  217.5 0.8 copy-done.4
  218.4 3.7 %widen.3 = (f32[2,512,2048]{2,1,0:T(8,128)}, f32[2,512,2048]{2,1,0:T(8,128)}) custom-call(s32[2]{0:T(128)S(1)} %pad_add_fusion.where_ref.refs_0_, bf16[2,128,1024]{2,1,0:T(8,128)(2,1)} %collective-permute-done.20.refs_1_, bf16[2,128,1024]{2,1,0:T(8,128)(2,1)} %collective-permute-done.21.refs_2_, ...), custom_call_target="tpu_custom_call", output_to_operand_aliasing={{0}: (5, {}), {1}: (6, {})} | custom-call | flops 1000 | bytes 1000 | tf_op jit(solution)/shard_map/widen/pallas_call | solution.py:748
  222.1 1.4 all-to-all-done.6.refs_0_
  223.5 1.0 finish.1
  (59 shorter events, 6.7 us)
Async XLA Ops:
  1.7 9.2 %collective-permute-start.2 = (bf16[5,16,512]{2,1,0:T(8,128)(2,1)S(1)}, bf16[5,16,512]{2,1,0:T(8,128)(2,1)S(1)}, u32[]{:S(2)}, u32[]{:S(2)}) collective-permute-start(bf16[5,16,512]{2,1,0:T(8,128)(2,1)S(1)} %pack_weights.1), channel_id=1, source_target_pairs={{0,3},{1,2},{2,1},{3,0},{4,7},{5,6},{6,5},{7,4},{8,11},{9,10},{10,... | collective-permute-start | bytes 245768 | tf_op jit(solution)/shard_map/ppermute | solution.py:180
  6.8 6.9 %collective-permute-start.1 = (bf16[5,16,512]{2,1,0:T(8,128)(2,1)S(1)}, bf16[5,16,512]{2,1,0:T(8,128)(2,1)S(1)}, u32[]{:S(2)}, u32[]{:S(2)}) collective-permute-start(bf16[5,16,512]{2,1,0:T(8,128)(2,1)S(1)} %pack_weights.1), channel_id=1, source_target_pairs={{0,2},{1,3},{2,0},{3,1},{4,6},{5,7},{6,4},{7,5},{8,10},{9,11},{10,... | collective-permute-start | bytes 245768 | tf_op jit(solution)/shard_map/ppermute | solution.py:180
  6.8 6.9 %collective-permute-start = (bf16[5,16,512]{2,1,0:T(8,128)(2,1)S(1)}, bf16[5,16,512]{2,1,0:T(8,128)(2,1)S(1)}, u32[]{:S(2)}, u32[]{:S(2)}) collective-permute-start(bf16[5,16,512]{2,1,0:T(8,128)(2,1)S(1)} %pack_weights.1), channel_id=1, source_target_pairs={{0,1},{1,0},{2,3},{3,2},{4,5},{5,4},{6,7},{7,6},{8,9},{9,8},{10,11... | collective-permute-start | bytes 245768 | tf_op jit(solution)/shard_map/ppermute | solution.py:180
  13.7 32.0 %all-to-all-start.1 = ((bf16[8,136,512]{2,1,0:T(8,128)(2,1)}), bf16[8,136,512]{2,1,0:T(8,128)(2,1)S(1)}, u32[]{:S(2)}, u32[]{:S(2)}) async-start(bf16[8,136,512]{2,1,0:T(8,128)(2,1)} %get-tuple-element.61), calls=%async_computation.1 | async-start | bytes 2228224 | tf_op jit(solution)/shard_map/all_to_all | solution.py:820
  17.7 8.7 %collective-permute-start.8 = (bf16[3,4,16,512]{3,2,1,0:T(8,128)(2,1)S(1)}, bf16[3,4,16,512]{3,2,1,0:T(8,128)(2,1)S(1)}, u32[]{:S(2)}, u32[]{:S(2)}) collective-permute-start(bf16[3,4,16,512]{3,2,1,0:T(8,128)(2,1)S(1)} %pad_maximum_fusion.refs_7_), channel_id=1, source_target_pairs={{0,24},{4,28},{8,16},{12,20},{16,8},{20,12},{24,0},{28,4},{1,25},{... | collective-permute-start | bytes 589832 | tf_op jit(solution)/shard_map/ppermute | solution.py:186
  20.3 10.0 %collective-permute-start.6 = (bf16[3,4,16,512]{3,2,1,0:T(8,128)(2,1)S(1)}, bf16[3,4,16,512]{3,2,1,0:T(8,128)(2,1)S(1)}, u32[]{:S(2)}, u32[]{:S(2)}) collective-permute-start(bf16[3,4,16,512]{3,2,1,0:T(8,128)(2,1)S(1)} %pad_maximum_fusion.refs_7_), channel_id=1, source_target_pairs={{0,16},{4,20},{8,24},{12,28},{16,0},{20,4},{24,8},{28,12},{1,17},{... | collective-permute-start | bytes 589832 | tf_op jit(solution)/shard_map/ppermute | solution.py:186
  20.8 9.6 %collective-permute-start.4 = (bf16[3,4,16,512]{3,2,1,0:T(8,128)(2,1)S(1)}, bf16[3,4,16,512]{3,2,1,0:T(8,128)(2,1)S(1)}, u32[]{:S(2)}, u32[]{:S(2)}) collective-permute-start(bf16[3,4,16,512]{3,2,1,0:T(8,128)(2,1)S(1)} %pad_maximum_fusion.refs_7_), channel_id=1, source_target_pairs={{0,8},{4,12},{8,0},{12,4},{16,24},{20,28},{24,16},{28,20},{1,9},{5... | collective-permute-start | bytes 589832 | tf_op jit(solution)/shard_map/ppermute | solution.py:186
  21.3 9.5 %collective-permute-start.3 = (bf16[3,4,16,512]{3,2,1,0:T(8,128)(2,1)S(1)}, bf16[3,4,16,512]{3,2,1,0:T(8,128)(2,1)S(1)}, u32[]{:S(2)}, u32[]{:S(2)}) collective-permute-start(bf16[3,4,16,512]{3,2,1,0:T(8,128)(2,1)S(1)} %pad_maximum_fusion.refs_7_), channel_id=1, source_target_pairs={{0,4},{4,0},{8,12},{12,8},{16,20},{20,16},{24,28},{28,24},{1,5},{5... | collective-permute-start | bytes 589832 | tf_op jit(solution)/shard_map/ppermute | solution.py:188
  26.4 4.4 %collective-permute-start.9 = (bf16[3,4,16,512]{3,2,1,0:T(8,128)(2,1)S(1)}, bf16[3,4,16,512]{3,2,1,0:T(8,128)(2,1)S(1)}, u32[]{:S(2)}, u32[]{:S(2)}) collective-permute-start(bf16[3,4,16,512]{3,2,1,0:T(8,128)(2,1)S(1)} %collective-permute-done.8.refs_13_), channel_id=1, source_target_pairs={{0,4},{4,0},{8,12},{12,8},{16,20},{20,16},{24,28},{28,24},{1,5},{5... | collective-permute-start | bytes 589832 | tf_op jit(solution)/shard_map/ppermute | solution.py:188
  30.2 1.4 collective-permute-start.7
  30.3 1.6 collective-permute-start.5
  45.7 31.5 %all-to-all-start = ((bf16[8,136,512]{2,1,0:T(8,128)(2,1)}), bf16[8,136,512]{2,1,0:T(8,128)(2,1)S(1)}, u32[]{:S(2)}, u32[]{:S(2)}) async-start(bf16[8,136,512]{2,1,0:T(8,128)(2,1)} %get-tuple-element.59), calls=%async_computation | async-start | bytes 2228224 | tf_op jit(solution)/shard_map/all_to_all | solution.py:820
  96.1 31.5 %all-to-all-start.2 = ((bf16[8,136,512]{2,1,0:T(8,128)(2,1)}), bf16[8,136,512]{2,1,0:T(8,128)(2,1)S(1)}, u32[]{:S(2)}, u32[]{:S(2)}) async-start(bf16[8,136,512]{2,1,0:T(8,128)(2,1)} %get-tuple-element.63), calls=%async_computation.2 | async-start | bytes 2228224 | tf_op jit(solution)/shard_map/all_to_all | solution.py:820
  110.3 25.8 %collective-permute-start.10 = (bf16[2,2,128,1024]{3,2,1,0:T(8,128)(2,1)}, bf16[2,2,128,1024]{3,2,1,0:T(8,128)(2,1)}, u32[]{:S(2)}, u32[]{:S(2)}) collective-permute-start(bf16[2,2,128,1024]{3,2,1,0:T(8,128)(2,1)} %get-tuple-element.71), channel_id=1, source_target_pairs={{0,8},{4,12},{8,0},{12,4},{16,24},{20,28},{24,16},{28,20},{1,9},{5... | collective-permute-start | bytes 3145736 | tf_op jit(solution)/shard_map/ppermute | solution.py:845
  111.8 25.5 %collective-permute-start.11 = (bf16[2,2,128,1024]{3,2,1,0:T(8,128)(2,1)}, bf16[2,2,128,1024]{3,2,1,0:T(8,128)(2,1)}, u32[]{:S(2)}, u32[]{:S(2)}) collective-permute-start(bf16[2,2,128,1024]{3,2,1,0:T(8,128)(2,1)} %get-tuple-element.73), channel_id=1, source_target_pairs={{0,16},{4,20},{8,24},{12,28},{16,0},{20,4},{24,8},{28,12},{1,17},{... | collective-permute-start | bytes 3145736 | tf_op jit(solution)/shard_map/ppermute | solution.py:845
  127.6 36.2 %all-to-all-start.3 = ((bf16[8,136,512]{2,1,0:T(8,128)(2,1)}), bf16[8,136,512]{2,1,0:T(8,128)(2,1)}, u32[]{:S(2)}, u32[]{:S(2)}) async-start(bf16[8,136,512]{2,1,0:T(8,128)(2,1)} %get-tuple-element.64), calls=%async_computation.3 | async-start | bytes 2228224 | tf_op jit(solution)/shard_map/all_to_all | solution.py:820
  139.5 19.0 %collective-permute-start.12 = (bf16[2,128,1024]{2,1,0:T(8,128)(2,1)S(1)}, bf16[2,128,1024]{2,1,0:T(8,128)(2,1)S(1)}, u32[]{:S(2)}, u32[]{:S(2)}) collective-permute-start(bf16[2,128,1024]{2,1,0:T(8,128)(2,1)S(1)} %get-tuple-element.85), channel_id=1, source_target_pairs={{0,16},{4,20},{8,24},{12,28},{16,0},{20,4},{24,8},{28,12},{1,17},{... | collective-permute-start | bytes 1572872 | tf_op jit(solution)/shard_map/ppermute | solution.py:845
  141.1 17.4 %collective-permute-start.13 = (bf16[2,128,1024]{2,1,0:T(8,128)(2,1)S(1)}, bf16[2,128,1024]{2,1,0:T(8,128)(2,1)S(1)}, u32[]{:S(2)}, u32[]{:S(2)}) collective-permute-start(bf16[2,128,1024]{2,1,0:T(8,128)(2,1)S(1)} %get-tuple-element.86), channel_id=1, source_target_pairs={{0,8},{4,12},{8,0},{12,4},{16,24},{20,28},{24,16},{28,20},{1,9},{5... | collective-permute-start | bytes 1572872 | tf_op jit(solution)/shard_map/ppermute | solution.py:845
  158.6 1.2 copy-start.5
  158.6 3.9 %copy-start.1 = (bf16[4,264,512]{2,1,0:T(8,128)(2,1)S(1)}, bf16[4,264,512]{2,1,0:T(8,128)(2,1)}, u32[]{:S(2)}) copy-start(bf16[4,264,512]{2,1,0:T(8,128)(2,1)} %get-tuple-element.87.a_ref) | copy-start | bytes 3244036
  159.8 8.7 %copy-start = (bf16[2,2,128,1024]{3,2,1,0:T(8,128)(2,1)}, bf16[2,2,128,1024]{3,2,1,0:T(8,128)(2,1)S(1)}, u32[]{:S(2)}) copy-start(bf16[2,2,128,1024]{3,2,1,0:T(8,128)(2,1)S(1)} %second_sums.1.refs_1_) | copy-start | bytes 3145732
  159.8 2.7 %collective-permute-start.14 = (bf16[4,264,512]{2,1,0:T(8,128)(2,1)S(1)}, bf16[4,264,512]{2,1,0:T(8,128)(2,1)S(1)}, u32[]{:S(2)}, u32[]{:S(2)}) collective-permute-start(bf16[4,264,512]{2,1,0:T(8,128)(2,1)S(1)} %copy-done.5), channel_id=1, source_target_pairs={{0,4},{4,0},{8,12},{12,8},{16,20},{20,16},{24,28},{28,24},{1,5},{5... | collective-permute-start | bytes 3244040 | tf_op jit(solution)/shard_map/ppermute | solution.py:845
  159.8 25.7 %collective-permute-start.16 = (bf16[2,2,128,1024]{3,2,1,0:T(8,128)(2,1)S(1)}, bf16[2,2,128,1024]{3,2,1,0:T(8,128)(2,1)}, u32[]{:S(2)}, u32[]{:S(2)}) collective-permute-start(bf16[2,2,128,1024]{3,2,1,0:T(8,128)(2,1)S(1)} %second_sums.1.refs_1_), channel_id=1, source_target_pairs={{0,16},{4,20},{8,24},{12,28},{16,0},{20,4},{24,8},{28,12},{1,17},{... | collective-permute-start | bytes 3145736 | tf_op jit(solution)/shard_map/ppermute | solution.py:845
  160.3 25.4 %collective-permute-start.15 = (bf16[2,2,128,1024]{3,2,1,0:T(8,128)(2,1)S(1)}, bf16[2,2,128,1024]{3,2,1,0:T(8,128)(2,1)}, u32[]{:S(2)}, u32[]{:S(2)}) collective-permute-start(bf16[2,2,128,1024]{3,2,1,0:T(8,128)(2,1)S(1)} %second_sums.1.refs_1_), channel_id=1, source_target_pairs={{0,8},{4,12},{8,0},{12,4},{16,24},{20,28},{24,16},{28,20},{1,9},{5... | collective-permute-start | bytes 3145736 | tf_op jit(solution)/shard_map/ppermute | solution.py:845
  163.8 31.5 %all-to-all-start.4 = ((bf16[4,264,512]{2,1,0:T(8,128)(2,1)}), bf16[4,264,512]{2,1,0:T(8,128)(2,1)S(1)}, u32[]{:S(2)}, u32[]{:S(2)}) async-start(bf16[4,264,512]{2,1,0:T(8,128)(2,1)} %pair_sum.1), calls=%async_computation.4 | async-start | bytes 2162688 | tf_op jit(solution)/shard_map/all_to_all | solution.py:880
  168.5 31.0 %collective-permute-start.17 = (bf16[2,2,128,1024]{3,2,1,0:T(8,128)(2,1)S(1)}, bf16[2,2,128,1024]{3,2,1,0:T(8,128)(2,1)S(1)}, u32[]{:S(2)}, u32[]{:S(2)}) collective-permute-start(bf16[2,2,128,1024]{3,2,1,0:T(8,128)(2,1)S(1)} %second_sums.1.refs_1_), channel_id=1, source_target_pairs={{0,4},{4,0},{8,12},{12,8},{16,20},{20,16},{24,28},{28,24},{1,5},{5... | collective-permute-start | bytes 3145736 | tf_op jit(solution)/shard_map/ppermute | solution.py:845
  185.5 14.0 %collective-permute-start.19 = (bf16[2,2,128,1024]{3,2,1,0:T(8,128)(2,1)}, bf16[2,2,128,1024]{3,2,1,0:T(8,128)(2,1)}, u32[]{:S(2)}, u32[]{:S(2)}) collective-permute-start(bf16[2,2,128,1024]{3,2,1,0:T(8,128)(2,1)} %collective-permute-done.16.refs_3_), channel_id=1, source_target_pairs={{0,4},{4,0},{8,12},{12,8},{16,20},{20,16},{24,28},{28,24},{1,5},{5... | collective-permute-start | bytes 3145736 | tf_op jit(solution)/shard_map/ppermute | solution.py:845
  185.7 13.8 %collective-permute-start.18 = (bf16[2,2,128,1024]{3,2,1,0:T(8,128)(2,1)}, bf16[2,2,128,1024]{3,2,1,0:T(8,128)(2,1)}, u32[]{:S(2)}, u32[]{:S(2)}) collective-permute-start(bf16[2,2,128,1024]{3,2,1,0:T(8,128)(2,1)} %collective-permute-done.15.refs_2_), channel_id=1, source_target_pairs={{0,4},{4,0},{8,12},{12,8},{16,20},{20,16},{24,28},{28,24},{1,5},{5... | collective-permute-start | bytes 3145736 | tf_op jit(solution)/shard_map/ppermute | solution.py:845
  187.9 20.2 %collective-permute-start.21 = (bf16[2,128,1024]{2,1,0:T(8,128)(2,1)}, bf16[2,128,1024]{2,1,0:T(8,128)(2,1)}, u32[]{:S(2)}, u32[]{:S(2)}) collective-permute-start(bf16[2,128,1024]{2,1,0:T(8,128)(2,1)} %slice_bitcast_fusion), channel_id=1, source_target_pairs={{0,8},{4,12},{8,0},{12,4},{16,24},{20,28},{24,16},{28,20},{1,9},{5... | collective-permute-start | bytes 1572872 | tf_op jit(solution)/shard_map/ppermute | solution.py:845
  191.2 16.9 %collective-permute-start.20 = (bf16[2,128,1024]{2,1,0:T(8,128)(2,1)}, bf16[2,128,1024]{2,1,0:T(8,128)(2,1)}, u32[]{:S(2)}, u32[]{:S(2)}) collective-permute-start(bf16[2,128,1024]{2,1,0:T(8,128)(2,1)} %slice_bitcast_fusion.1), channel_id=1, source_target_pairs={{0,16},{4,20},{8,24},{12,28},{16,0},{20,4},{24,8},{28,12},{1,17},{... | collective-permute-start | bytes 1572872 | tf_op jit(solution)/shard_map/ppermute | solution.py:845
  196.1 11.9 %all-to-all-start.5 = ((bf16[4,64,512]{2,1,0:T(8,128)(2,1)}), bf16[4,64,512]{2,1,0:T(8,128)(2,1)S(1)}, u32[]{:S(2)}, u32[]{:S(2)}) async-start(bf16[4,64,512]{2,1,0:T(8,128)(2,1)} %bitcast.10), calls=%async_computation.5 | async-start | bytes 524288 | tf_op jit(solution)/shard_map/all_to_all | solution.py:894
  199.5 1.0 copy-start.2
  208.1 8.6 %collective-permute-start.22 = (bf16[2,128,1024]{2,1,0:T(8,128)(2,1)}, bf16[2,128,1024]{2,1,0:T(8,128)(2,1)S(1)}, u32[]{:S(2)}, u32[]{:S(2)}) collective-permute-start(bf16[2,128,1024]{2,1,0:T(8,128)(2,1)} %collective-permute-done.20.refs_1_), channel_id=1, source_target_pairs={{0,4},{4,0},{8,12},{12,8},{16,20},{20,16},{24,28},{28,24},{1,5},{5... | collective-permute-start | bytes 1572872 | tf_op jit(solution)/shard_map/ppermute | solution.py:845
  208.2 8.6 %collective-permute-start.23 = (bf16[2,128,1024]{2,1,0:T(8,128)(2,1)}, bf16[2,128,1024]{2,1,0:T(8,128)(2,1)S(1)}, u32[]{:S(2)}, u32[]{:S(2)}) collective-permute-start(bf16[2,128,1024]{2,1,0:T(8,128)(2,1)} %collective-permute-done.21.refs_2_), channel_id=1, source_target_pairs={{0,4},{4,0},{8,12},{12,8},{16,20},{20,16},{24,28},{28,24},{1,5},{5... | collective-permute-start | bytes 1572872 | tf_op jit(solution)/shard_map/ppermute | solution.py:845
  209.5 13.9 %all-to-all-start.6 = ((bf16[8,72,512]{2,1,0:T(8,128)(2,1)}), bf16[8,72,512]{2,1,0:T(8,128)(2,1)S(1)}, u32[]{:S(2)}, u32[]{:S(2)}) async-start(bf16[8,72,512]{2,1,0:T(8,128)(2,1)} %broadcast_in_dim.3), calls=%async_computation.6 | async-start | bytes 1179648 | tf_op jit(solution)/shard_map/all_to_all | solution.py:900
  216.7 0.8 copy-start.3
  217.5 0.8 copy-start.4

commit v3 on v2

--- a/solution.py
+++ b/solution.py
@@ -280,13 +280,13 @@
         q = q * BF(HEAD_DIM**-0.5)
         halves = []
         for half in range(2):
-            scores = dot_nt(jnp.where(masks[half], q, BF(0)), k) + bias
-            top = jnp.max(scores, axis=-1, keepdims=True)
+            scores = dot_nt(k, jnp.where(masks[half], q, BF(0))) + bias
+            top = jnp.max(scores, axis=0, keepdims=True)
             terms = jnp.exp(scores - top)
-            total = jnp.sum(terms, axis=-1, keepdims=True)
+            total = jnp.sum(terms, axis=0, keepdims=True)
             weights = (terms * (1.0 / total)).astype(BF)
             weights_ref[2 * pair + half] = weights
-            halves.append(dot_nn(weights, v))
+            halves.append(dot_tn(weights, v))
         copies[1, pair].start()
         mixed_ref[:, lanes] = jnp.where(masks[0], halves[0], halves[1]).astype(BF)
     copies[3].start()
@@ -510,20 +510,17 @@
             pack_ref[r % 2, z, spot : spot + rows, :] = grad[start : start + rows]
 
 
-def backward_body(fast, reps, shards_n, where_ref, *refs):
-    core = where_ref[0]
-    back_ref, x_ref, cot_ref, index_ref, small_ref, gate_ref, *kept = refs[: 6 + KEPT]
-    if fast:
-        grad_x_ref, mine_ref, twin_ref, pack_ref, gp_ref = refs[6 + KEPT : 11 + KEPT]
-        refs = refs[11 + KEPT :]
-    else:
-        grad_x_ref, pack_ref, sums_ref, gp_ref = refs[6 + KEPT : 10 + KEPT]
-        refs = refs[10 + KEPT :]
-    full_ref, weights_ref, proj_ref, mixed_ref, resid_ref = held = refs[:-1]
-    sem = refs[-1]
-    fetch = kept_copies(kept, held, sem)
-    for which in (4, 0, 3, 2, *((1, pair) for pair in range(HEADS // 2))):
-        fetch[which].start()
+def tokens_back_body(back_ref, cot_ref, index_ref, small_ref, gate_ref, *refs):
+    full_far, mixed_far, resid_far, grad_resid_ref, grad_mixed_ref, grad_out_ref, sums_ref = refs[:7]
+    out_weight_ref, mixed_ref, resid_ref, sem = refs[7:]
+    fetch = [
+        pltpu.make_async_copy(source, target, sem.at[i])
+        for i, (source, target) in enumerate(
+            ((resid_far, resid_ref), (full_far.at[3], out_weight_ref), (mixed_far, mixed_ref))
+        )
+    ]
+    for copy in fetch:
+        copy.start()
     count, width = resid_ref.shape
     small = small_ref[...].astype(F32)
     index = index_ref[...]
@@ -544,113 +541,196 @@
         [grad_logits.astype(F32), jnp.zeros((8, count), F32)], axis=0
     ).astype(BF)
     grad_n2 = grad_n2 + dot_tn(wide_logits, small_ref[...])
-    fetch[4].wait()
+    fetch[0].wait()
     unit2, inv2 = unit_of(resid_ref[...])
     n2 = (unit2 * small[9:10, :]).astype(BF)
     grad_router = dot_nn(wide_logits, n2)[0:EXPERTS]
     grad_gain2 = jnp.sum(grad_n2 * unit2, axis=0, keepdims=True)
+    sums_ref[...] = jnp.concatenate(
+        [grad_router, jnp.zeros((1, width), F32), grad_gain2, jnp.zeros((6, width), F32)], axis=0
+    )
     a = grad_n2 * small[9:10, :]
     grad_resid = cot_ref[0].astype(F32) + inv2 * (
         a
         - jnp.mean(a, axis=-1, keepdims=True)
         - unit2 * jnp.mean(a * unit2, axis=-1, keepdims=True)
     )
+    grad_resid_ref[...] = grad_resid
     branch = grad_resid.astype(BF)
-    fetch[0].wait()
-    fetch[3].wait()
-    place_grads(fast, reps, shards_n, pack_ref, 3, dot_tn(mixed_ref[...], branch))
-    grad_mixed = dot_nt(branch, full_ref[3]).astype(BF)
+    fetch[1].wait()
+    grad_mixed_ref[...] = dot_nt(branch, out_weight_ref[...]).astype(BF)
     fetch[2].wait()
+    grad_out_ref[...] = dot_tn(mixed_ref[...], branch).astype(BF)
+
+
+def tokens_back(back, cot, index, small, gates, full, mixed, resid):
+    count, width = resid.shape
+    held = pl.BlockSpec(memory_space=pltpu.HBM)
+    outs = (
+        ((count, width), F32),
+        ((count, width), BF),
+        ((width, width), BF),
+        ((16, width), F32),
+    )
+    return pl.pallas_call(
+        tokens_back_body,
+        out_shape=tuple(pltpu.HBM(*o) for o in outs),
+        in_specs=vmem(5) + [held] * 3,
+        out_specs=tuple(vmem(4)),
+        scratch_shapes=[
+            pltpu.VMEM((width, width), BF),
+            pltpu.VMEM((count, width), BF),
+            pltpu.VMEM((count, width), F32),
+            pltpu.SemaphoreType.DMA((3,)),
+        ],
+        compiler_params=params(24),
+        cost_estimate=SMALL,
+        name="tokens_back",
+    )(back, far(cot), index, small, gates, far(full), far(mixed), far(resid))
+
+
+def backward_body(fast, reps, shards_n, where_ref, *refs):
+    core = where_ref[0]
+    grad_mixed_ref, small_ref, early_ref = refs[:3]
+    sources = refs[3:8]
+    if fast:
+        gp_far, mine_ref, twin_ref, pack_ref = refs[8:12]
+        refs = refs[12:]
+    else:
+        gp_far, pack_ref, sums_ref = refs[8:11]
+        refs = refs[11:]
+    gp_ref, proj_ref, weights_ref, full_ref, x_ref, grad_out_ref = refs[:-1]
+    held, sem = refs[1:-1], refs[-1]
+    pairs = HEADS // 2
+    copies = {
+        i: pltpu.make_async_copy(sources[i], held[i], sem.at[i]) for i in range(5) if i != 1
+    }
+    for pair in range(pairs):
+        heads = pl.ds(2 * pair, 2)
+        copies[1, pair] = pltpu.make_async_copy(
+            sources[1].at[heads], weights_ref.at[heads], sem.at[5 + pair]
+        )
+    for which in (0, *((1, pair) for pair in range(pairs)), 3, 2, 4):
+        copies[which].start()
+    count, width = grad_mixed_ref.shape
+    small = small_ref[...].astype(F32)
     masks = head_masks(count)
     factor = HEAD_DIM**-0.5
-    for pair in range(HEADS // 2):
+    copies[0].wait()
+    for pair in range(pairs):
         lanes = slice(pair * 2 * HEAD_DIM, (pair + 1) * 2 * HEAD_DIM)
         q, k, v = proj_ref[0, :, lanes], proj_ref[1, :, lanes], proj_ref[2, :, lanes]
-        gm = grad_mixed[:, lanes]
-        fetch[1, pair].wait()
+        gm = grad_mixed_ref[:, lanes]
+        copies[1, pair].wait()
         parts = []
         for half in range(2):
             weights = weights_ref[2 * pair + half]
             probs = weights.astype(F32)
-            grad_probs = dot_nt(jnp.where(masks[half], gm, BF(0)), v)
-            total = jnp.sum(probs * grad_probs, axis=-1, keepdims=True)
+            grad_probs = dot_nt(v, jnp.where(masks[half], gm, BF(0)))
+            total = jnp.sum(probs * grad_probs, axis=0, keepdims=True)
             grad_scores = (probs * (grad_probs - total)).astype(BF)
             parts.append(
-                (dot_nn(grad_scores, k), dot_tn(grad_scores, q), dot_tn(weights, gm))
+                (dot_tn(grad_scores, k), dot_nn(grad_scores, q), dot_nn(weights, gm))
             )
         for s in range(3):
             both = jnp.where(masks[0], parts[0][s], parts[1][s])
             gp_ref[s, :, lanes] = (both * factor if s < 2 else both).astype(BF)
-    unit1, inv1 = unit_of(x_ref[0].astype(F32))
+    gp_send = pltpu.make_async_copy(gp_ref, gp_far, sem.at[5 + pairs])
+    gp_send.start()
+    copies[3].wait()
+    unit1, _ = unit_of(x_ref[0].astype(F32))
     n1 = (unit1 * small[8:9, :]).astype(BF)
-    grad_n1 = jnp.zeros((count, width), F32)
+    copies[2].wait()
+    product = jnp.zeros((width, width), F32)
     for s in range(3):
-        grads = gp_ref[s]
-        place_grads(fast, reps, shards_n, pack_ref, s, dot_tn(n1, grads))
-        grad_n1 = grad_n1 + dot_nt(grads, full_ref[s])
-    grad_gain1 = jnp.sum(grad_n1 * unit1, axis=0, keepdims=True)
-    b = grad_n1 * small[8:9, :]
-    grad_x = grad_resid + inv1 * (
-        b
-        - jnp.mean(b, axis=-1, keepdims=True)
-        - unit1 * jnp.mean(b * unit1, axis=-1, keepdims=True)
-    )
-    grad_x_ref[0] = grad_x.astype(BF)
-    sums = jnp.concatenate(
-        [grad_router, grad_gain1, grad_gain2, jnp.zeros((6, width), F32)], axis=0
-    )
-    if not fast:
+        grad = dot_tn(n1, gp_ref[s])
+        place_grads(fast, reps, shards_n, pack_ref, s, grad)
+        product = product + full_ref[s].astype(F32) * grad
+    copies[4].wait()
+    place_grads(fast, reps, shards_n, pack_ref, 3, grad_out_ref[...])
+    ones = jnp.ones((8, width), BF)
+    high = product.astype(BF)
+    low = (product - high.astype(F32)).astype(BF)
+    grad_gain1 = (dot_nt(ones, high) + dot_nt(ones, low))[0:1] / small[8:9, :]
+    sums = jnp.where(iota((16, width), 0) == 8, grad_gain1, early_ref[...])
+    sends = [gp_send]
+    if fast:
+        depth = width // shards_n
+        rows = depth // reps
+        for z in range(shards_n):
+            for half in range(2):
+                eight = sums[8 * half : 8 * half + 8, z * depth : (z + 1) * depth]
+                eight = jnp.concatenate([eight, jnp.zeros((8, width - depth), F32)], axis=1)
+                pack_ref[half, z, 2 * reps * rows :, :] = eight.astype(BF)
+        for i in range(2):
+            send = pltpu.make_async_copy(pack_ref.at[core ^ i], (mine_ref, twin_ref)[i], sem.at[i])
+            send.start()
+            sends.append(send)
+    else:
         sums_ref[...] = sums
-        return
-    depth = width // shards_n
-    rows = depth // reps
-    for z in range(shards_n):
-        for half in range(2):
-            eight = sums[8 * half : 8 * half + 8, z * depth : (z + 1) * depth]
-            eight = jnp.concatenate([eight, jnp.zeros((8, width - depth), F32)], axis=1)
-            pack_ref[half, z, 2 * reps * rows :, :] = eight.astype(BF)
-    copies = [
-        pltpu.make_async_copy(pack_ref.at[core ^ i], (mine_ref, twin_ref)[i], sem.at[i])
-        for i in range(2)
-    ]
-    for copy in copies:
-        copy.start()
-    for copy in copies:
-        copy.wait()
-
-
-def backward(fast, reps, shards_n, where, operands):
-    x = operands[1]
+    for send in sends:
+        send.wait()
+
+
+def backward(fast, reps, shards_n, where, grad_mixed, small, early, proj, weights, full, x, grad_out):
     _, count, width = x.shape
-    outs = [jax.ShapeDtypeStruct(x.shape, BF)]
+    sources = (proj, weights, full, x, grad_out)
+    held = pl.BlockSpec(memory_space=pltpu.HBM)
+    outs = [pltpu.HBM((3, count, width), BF)]
     scratch = [pltpu.VMEM((3, count, width), BF)]
     if fast:
         part = (shards_n, 2 * reps * (width // shards_n // reps) + 8, width)
         outs += [pltpu.HBM(part, BF)] * 2
-        out_specs = vmem(1) + [pl.BlockSpec(memory_space=pltpu.HBM)] * 2
+        out_specs = [held] * 3
         scratch = [pltpu.VMEM((2, *part), BF)] + scratch
     else:
         outs += [
             jax.ShapeDtypeStruct((4, width, width), BF),
             jax.ShapeDtypeStruct((16, width), F32),
         ]
-        out_specs = vmem(3)
+        out_specs = [held] + vmem(2)
     return pl.pallas_call(
         lambda *refs: backward_body(fast, reps, shards_n, *refs),
         out_shape=tuple(outs),
-        in_specs=[pl.BlockSpec(memory_space=pltpu.SMEM)]
-        + vmem(len(operands) - KEPT)
-        + [pl.BlockSpec(memory_space=pltpu.HBM)] * KEPT,
+        in_specs=[pl.BlockSpec(memory_space=pltpu.SMEM)] + vmem(3) + [held] * 5,
         out_specs=tuple(out_specs),
         scratch_shapes=[
             *scratch,
-            *(pltpu.VMEM(*k) for k in kept_shapes(count, width)),
-            pltpu.SemaphoreType.DMA((KEPT + HEADS // 2,)),
+            *(pltpu.VMEM(v.shape, v.dtype) for v in sources),
+            pltpu.SemaphoreType.DMA((6 + HEADS // 2,)),
         ],
         compiler_params=params(40),
         cost_estimate=SMALL,
         name="backward",
-    )(where, operands[0], *(far(v) for v in operands[1:3]), *operands[3:6], *(far(v) for v in operands[6:]))
+    )(where, grad_mixed, small, early, *(far(v) for v in sources))
+
+
+def input_back_body(gp_ref, full_ref, x_ref, grad_resid_ref, small_ref, grad_x_ref):
+    small = small_ref[...].astype(F32)
+    grad_n1 = dot_nt(gp_ref[0], full_ref[0])
+    for s in range(1, 3):
+        grad_n1 = grad_n1 + dot_nt(gp_ref[s], full_ref[s])
+    unit1, inv1 = unit_of(x_ref[0].astype(F32))
+    b = grad_n1 * small[8:9, :]
+    grad_x = grad_resid_ref[...] + inv1 * (
+        b
+        - jnp.mean(b, axis=-1, keepdims=True)
+        - unit1 * jnp.mean(b * unit1, axis=-1, keepdims=True)
+    )
+    grad_x_ref[0] = grad_x.astype(BF)
+
+
+def input_back(gp, full, x, grad_resid, small):
+    _, width = grad_resid.shape
+    return pl.pallas_call(
+        input_back_body,
+        out_shape=pltpu.HBM(x.shape, BF),
+        in_specs=vmem(5),
+        out_specs=vmem(1)[0],
+        compiler_params=params(20),
+        cost_estimate=SMALL,
+        name="input_back",
+    )(far(gp), far(full), far(x), far(grad_resid), small)
 
 
 def result_body(out_ref, index_ref, resid_ref, result_ref):
@@ -706,11 +786,25 @@
     sum_ref[...] = (a_ref[...].astype(F32) + b_ref[...].astype(F32)).astype(BF)
 
 
-def lead_sum(parts_ref, sum_ref):
+def line_sum(parts_ref, tall_ref, small_ref):
     total = parts_ref[0].astype(F32)
     for i in range(1, parts_ref.shape[0]):
         total = total + parts_ref[i].astype(F32)
-    sum_ref[...] = total.astype(BF)
+    rows = tall_ref.shape[0] * tall_ref.shape[1]
+    for p in range(tall_ref.shape[0]):
+        short = tall_ref.shape[1]
+        tall_ref[p] = total[p * short : (p + 1) * short].astype(BF)
+    small_ref[...] = total[rows:].astype(BF)
+
+
+def plane_sum(parts_ref, small_ref, shares_ref):
+    total = parts_ref[0].astype(F32)
+    for i in range(1, parts_ref.shape[0]):
+        total = total + parts_ref[i].astype(F32)
+    short = total.shape[0]
+    for r in range(shares_ref.shape[0]):
+        shares_ref[r, 0:short, :] = total.astype(BF)
+        shares_ref[r, short:, :] = small_ref[...]
 
 
 def widen_body(places, aliased, where_ref, *refs):
@@ -852,6 +946,13 @@
     if fast:
         axes = ((owned, 2 * owned), (2 * owned, owned))
         halves = [peer(grads[2 * half], axes[half][0]) for half in range(2)]
+        back_in = after(back_in, *grads)
+    full, weights, proj, mixed, resid = kept
+    grad_resid, grad_mixed, grad_out_w, early_sums = tokens_back(
+        back_in, cotangent, index, small, gates, full, mixed, resid
+    )
+    if fast:
+        grad_mixed, *halves = lax.optimization_barrier((grad_mixed, *halves))
         part = halves[0].shape[1:]
         small_part = jax.ShapeDtypeStruct(part, BF)
         keep, *leaves = plain(
@@ -863,14 +964,22 @@
             halves[1],
         )
         arrived = [peer(leaves[half], axes[half][1]) for half in range(2)]
-        back_in = after(back_in, keep)
-    grad_tokens, *packs = backward(
+        grad_mixed = after(grad_mixed, keep)
+    grad_proj, *packs = backward(
         fast,
         reps,
         shards_n,
         where,
-        [back_in, tokens, cotangent, index, small, gates, *kept],
-    )
+        grad_mixed,
+        small,
+        early_sums,
+        proj,
+        weights,
+        full,
+        tokens,
+        grad_out_w,
+    )
+    grad_tokens = input_back(grad_proj, full, tokens, grad_resid, small)
     result = combine(out_in, index, kept[4])
     if fast:
         mine, twin, *arrived = lax.optimization_barrier((*packs, *arrived))
@@ -878,11 +987,17 @@
         twin = after(twin, total)
         chip = plain(pair_sum, [jax.ShapeDtypeStruct(mine.shape, BF)], mine, peer(twin, 1))
         line = lax.all_to_all(after(chip, out_in), "shard", 0, 0, tiled=True)
-        line = plain(lead_sum, [jax.ShapeDtypeStruct(line.shape[1:], BF)], line)
-        tall = 2 * depth
-        own_small = line[tall:]
-        line = line[:tall].reshape(peers, tall // peers, width)
+        short = 2 * depth // peers
+        line, own_small = plain(
+            line_sum,
+            [
+                jax.ShapeDtypeStruct((peers, short, width), BF),
+                jax.ShapeDtypeStruct((8, width), BF),
+            ],
+            line,
+        )
         early = [total] + [peer(total, k * owned) for k in (1, 2)]
+        grad_tokens, *early = lax.optimization_barrier((grad_tokens, *early))
         late = [
             peer(early[axes[half][0] // owned][half], 3 * owned - axes[half][0]) for half in range(2)
         ]
@@ -893,13 +1008,12 @@
         plane_groups = [[p * owned + c for p in range(peers)] for c in range(owned)]
         plane = lax.all_to_all(line, "rep", 0, 0, axis_index_groups=plane_groups, tiled=True)
         plane, *so_far = lax.optimization_barrier((plane, *so_far))
-        share = plain(lead_sum, [jax.ShapeDtypeStruct(plane.shape[1:], BF)], plane)
-        share = jnp.concatenate([share, own_small], axis=0)
+        share = plain(
+            plane_sum, [jax.ShapeDtypeStruct((reps, short + 8, width), BF)], plane, own_small
+        )
         share, *late = lax.optimization_barrier((share, *late))
         late += [peer(value, 1) for value in late]
-        parts = lax.all_to_all(
-            jnp.broadcast_to(share, (reps, *share.shape)), "rep", 0, 0, tiled=True
-        )
+        parts = lax.all_to_all(share, "rep", 0, 0, tiled=True)
         places = [(other, 3, half) for other in range(2) for half in range(2)]
         grad_w_in, grad_w_out = widen(where, places, late, shape, so_far)
         parts = after(parts, grad_w_in, result)

time: 225 us -> 222 us (0.987)
  waiting for transfers between devices: 79.1 us -> 70.1 us
  Pallas kernels: 87.7 us -> 96 us
  local copies, waits for them, and re-layouts: 8.87 us -> 5.33 us
    pallas_call x0 -> x2, Pallas kernels: none -> 10.9 us  [the longest x1 6.3 us: tokens_back(): pl.pallas_call(tokens_back_body, out_shape=tuple((pltpu.HBM(*o) for o in...]
    ppermute x14, waiting for transfers between devices: 23.5 us -> 13.5 us  [peer(): return lax.ppermute(value, 'rep', [(i, i ^ k) for i in range(reps)])]
    pallas_call x1, Pallas kernels: 16.9 us -> 12.7 us  [backward(): pl.pallas_call(lambda *refs: backward_body(fast, reps, shards_n, *refs),...]
  transfers between devices with their start and end apart: 31 -> 31, of which waited for: 17 -> 15; matrix products, arithmetic and copies ran while one was open for 2% -> 1% of each run, Pallas kernels for 30% -> 34%
where the time goes in v3:
time: 222 us; the launch traced here: 221 us
  Pallas kernels  96 us (43%)
  waiting for transfers between devices  70.1 us (32%)
  starting transfers between devices  48.7 us (22%)
  local copies, waits for them, and re-layouts  5.33 us (2%)
    all_to_all x4, waiting for transfers between devices, to_experts(): lax.all_to_all(rows, AXES, 0, 0, axis_index_groups=column, tiled=True)  37.9 us
    pallas_call x1, Pallas kernels, experts(): pl.pallas_call(experts_body, out_shape=[pltpu.HBM((groups, ROWS, width),...  18.9 us
    all_to_all x4, starting transfers between devices, to_experts(): lax.all_to_all(rows, AXES, 0, 0, axis_index_groups=column, tiled=True)  15.5 us
    ppermute x14, waiting for transfers between devices, peer(): return lax.ppermute(value, 'rep', [(i, i ^ k) for i in range(reps)])  13.5 us
    pallas_call x1, Pallas kernels, backward(): pl.pallas_call(lambda *refs: backward_body(fast, reps, shards_n, *refs),...  12.7 us
    ppermute x14, starting transfers between devices, peer(): return lax.ppermute(value, 'rep', [(i, i ^ k) for i in range(reps)])  11.5 us
    pallas_call x1, Pallas kernels, expert_grads(): pl.pallas_call(lambda *refs: expert_grads_body(split, *refs), out_shape=g...  10.7 us
    pallas_call x2, Pallas kernels, widen(): pl.pallas_call(lambda *refs: widen_body(places, aliased, *refs), out_shap...  10.5 us
  transfers between devices with their start and end apart: 31, of which 15 were waited for; matrix products, arithmetic and copies ran while one was open for 1% of the time, Pallas kernels for 34%

profile of v3, /device:TPU:0, one launch (start us, length us, event | category | flops | bytes accessed | tf_op | source)
XLA Modules:
  0.0 221.2 jit_solution(14460810086620483894)
XLA Ops:
  0.6 1.1 pack_weights.1
  1.7 5.1 %collective-permute-start.2 = (bf16[5,16,512]{2,1,0:T(8,128)(2,1)S(1)}, bf16[5,16,512]{2,1,0:T(8,128)(2,1)S(1)}, u32[]{:S(2)}, u32[]{:S(2)}) collective-permute-start(bf16[5,16,512]{2,1,0:T(8,128)(2,1)S(1)} %pack_weights.1), channel_id=1, source_target_pairs={{0,3},{1,2},{2,1},{3,0},{4,7},{5,6},{6,5},{7,4},{8,11},{9,10},{10,... | collective-permute-start | bytes 245768 | tf_op jit(solution)/shard_map/ppermute | solution.py:180
  7.5 3.5 %route.1 = (s32[2,512]{1,0:T(2,128)S(1)}, bf16[8,136,512]{2,1,0:T(8,128)(2,1)}) custom-call(s32[2,512]{1,0:T(2,128)} %bitcast.19, s32[1,512]{1,0:T(1,128)} %prio_ref.1, bf16[1,512,512]{2,1,0:T(8,128)(2,1)} %cot_ref.3), custom_call_target="tpu_custom_call" | custom-call | flops 1000 | bytes 1000 | tf_op jit(solution)/shard_map/route/pallas_call | solution.py:135
  10.9 2.8 %collective-permute-done.1 = bf16[5,16,512]{2,1,0:T(8,128)(2,1)S(1)} collective-permute-done((bf16[5,16,512]{2,1,0:T(8,128)(2,1)S(1)}, bf16[5,16,512]{2,1,0:T(8,128)(2,1)S(1)}, u32[]{:S(2)}, u32[]{:S(2)}) %collective-permute-start.1) | collective-permute-done | bytes 81952 | tf_op jit(solution)/shard_map/ppermute | solution.py:180
  13.7 4.0 %all-to-all-start.1 = ((bf16[8,136,512]{2,1,0:T(8,128)(2,1)}), bf16[8,136,512]{2,1,0:T(8,128)(2,1)S(1)}, u32[]{:S(2)}, u32[]{:S(2)}) async-start(bf16[8,136,512]{2,1,0:T(8,128)(2,1)} %get-tuple-element.75), calls=%async_computation.1 | async-start | bytes 2228224 | tf_op jit(solution)/shard_map/all_to_all | solution.py:914
  17.7 2.5 %collective-permute-start.8 = (bf16[3,4,16,512]{3,2,1,0:T(8,128)(2,1)S(1)}, bf16[3,4,16,512]{3,2,1,0:T(8,128)(2,1)S(1)}, u32[]{:S(2)}, u32[]{:S(2)}) collective-permute-start(bf16[3,4,16,512]{3,2,1,0:T(8,128)(2,1)S(1)} %pad_maximum_fusion.refs_7_), channel_id=1, source_target_pairs={{0,24},{4,28},{8,16},{12,20},{16,8},{20,12},{24,0},{28,4},{1,25},{... | collective-permute-start | bytes 589832 | tf_op jit(solution)/shard_map/ppermute | solution.py:186
  21.3 5.1 %collective-permute-done.8.refs_13_ = bf16[3,4,16,512]{3,2,1,0:T(8,128)(2,1)S(1)} collective-permute-done((bf16[3,4,16,512]{3,2,1,0:T(8,128)(2,1)S(1)}, bf16[3,4,16,512]{3,2,1,0:T(8,128)(2,1)S(1)}, u32[]{:S(2)}, u32[]{:S(2)}) %collective-permute-start.8) | collective-permute-done | bytes 196640 | tf_op jit(solution)/shard_map/ppermute | solution.py:186
  26.4 3.8 %collective-permute-done.6.refs_11_ = bf16[3,4,16,512]{3,2,1,0:T(8,128)(2,1)S(1)} collective-permute-done((bf16[3,4,16,512]{3,2,1,0:T(8,128)(2,1)S(1)}, bf16[3,4,16,512]{3,2,1,0:T(8,128)(2,1)S(1)}, u32[]{:S(2)}, u32[]{:S(2)}) %collective-permute-start.6) | collective-permute-done | bytes 196640 | tf_op jit(solution)/shard_map/ppermute | solution.py:186
  30.9 0.8 collective-permute-done.7.refs_12_
  32.0 10.4 %forward.1 = (bf16[8,136,512]{2,1,0:T(8,128)(2,1)}, bf16[16,512]{1,0:T(8,128)(2,1)S(1)}, f32[8,512]{1,0:T(8,128)S(1)}, bf16[4,512,512]{2,1,0:T(8,128)(2,1)}, bf1...) custom-call(s32[2]{0:T(128)S(1)} %pad_add_fusion.1.refs_0_, ...), custom_call_target="tpu_custom_call" | custom-call | flops 1000 | bytes 1000 | tf_op jit(solution)/shard_map/forward/pallas_call | solution.py:329
  42.4 3.3 %all-to-all-done.1.cot_ref.refs_1_ = bf16[8,136,512]{2,1,0:T(8,128)(2,1)S(1)} async-done(((bf16[8,136,512]{2,1,0:T(8,128)(2,1)}), bf16[8,136,512]{2,1,0:T(8,128)(2,1)S(1)}, u32[]{:S(2)}, u32[]{:S(2)}) %all-to-all-start.1) | async-done | bytes 1114144 | tf_op jit(solution)/shard_map/all_to_all | solution.py:914
  45.7 3.7 %all-to-all-start = ((bf16[8,136,512]{2,1,0:T(8,128)(2,1)}), bf16[8,136,512]{2,1,0:T(8,128)(2,1)S(1)}, u32[]{:S(2)}, u32[]{:S(2)}) async-start(bf16[8,136,512]{2,1,0:T(8,128)(2,1)} %get-tuple-element.73), calls=%async_computation | async-start | bytes 2228224 | tf_op jit(solution)/shard_map/all_to_all | solution.py:914
  49.5 7.2 %cot_hidden.1.refs_2_ = f32[1088,2048]{1,0:T(8,128)} custom-call(s32[2]{0:T(128)S(1)} %pad_add_fusion.where_ref.refs_0_, bf16[8,136,512]{2,1,0:T(8,128)(2,1)S(1)} %all-to-all-done.1.cot_ref.refs_1_, bf16[2,512,2048]{2,1,0:T(8,128)(2,1)} %refs_4_.3), custom_call_target="tpu_custom_call" | custom-call | flops 1000 | bytes 1000 | tf_op jit(solution)/shard_map/cot_hidden/pallas_call | solution.py:354
  56.7 20.4 %all-to-all-done.refs_0_ = bf16[8,136,512]{2,1,0:T(8,128)(2,1)S(1)} async-done(((bf16[8,136,512]{2,1,0:T(8,128)(2,1)}), bf16[8,136,512]{2,1,0:T(8,128)(2,1)S(1)}, u32[]{:S(2)}, u32[]{:S(2)}) %all-to-all-start) | async-done | bytes 1114144 | tf_op jit(solution)/shard_map/all_to_all | solution.py:914
  77.2 18.9 %experts.1 = (bf16[8,136,512]{2,1,0:T(8,128)(2,1)}, bf16[8,136,512]{2,1,0:T(8,128)(2,1)}, bf16[1088,2048]{1,0:T(8,128)(2,1)}, bf16[1088,2048]{1,0:T(8,128)(2,1)}...) custom-call(s32[2]{0:T(128)S(1)} %pad_add_fusion.where_ref.refs_0_, ...), custom_call_target="tpu_custom_call" | custom-call | flops 1000 | bytes 1000 | tf_op jit(solution)/shard_map/experts/pallas_call | solution.py:424
  96.1 3.6 %all-to-all-start.2 = ((bf16[8,136,512]{2,1,0:T(8,128)(2,1)}), bf16[8,136,512]{2,1,0:T(8,128)(2,1)S(1)}, u32[]{:S(2)}, u32[]{:S(2)}) async-start(bf16[8,136,512]{2,1,0:T(8,128)(2,1)} %get-tuple-element.77), calls=%async_computation.2 | async-start | bytes 2228224 | tf_op jit(solution)/shard_map/all_to_all | solution.py:914
  99.7 10.7 %expert_grads.1 = (bf16[2,2,128,1024]{3,2,1,0:T(8,128)(2,1)}, bf16[2,2,128,1024]{3,2,1,0:T(8,128)(2,1)S(1)}, bf16[2,2,128,1024]{3,2,1,0:T(8,128)(2,1)}, bf16[2,2,128,1024]{3,2,1,0:T(8,128)(2,1)S(1)}) custom-call(s32[2]{0:T(128)S(1)} %pad_add_fusion.where_ref.refs_0_, bf16[1088,2048]{1,0:T(8,128)(2,1)} %get-tuple-element.80.refs_1_, ...), custom_call_target="tpu_custom_call" | custom-call | flops 1000 | bytes 1000 | tf_op jit(solution)/shard_map/expert_grads/pallas_call | solution.py:482
  110.3 1.5 collective-permute-start.10
  111.8 1.5 collective-permute-start.11
  113.3 14.2 %all-to-all-done.2.back_ref = bf16[8,136,512]{2,1,0:T(8,128)(2,1)S(1)} async-done(((bf16[8,136,512]{2,1,0:T(8,128)(2,1)}), bf16[8,136,512]{2,1,0:T(8,128)(2,1)S(1)}, u32[]{:S(2)}, u32[]{:S(2)}) %all-to-all-start.2) | async-done | bytes 1114144 | tf_op jit(solution)/shard_map/all_to_all | solution.py:914
  127.6 4.3 %all-to-all-start.3 = ((bf16[8,136,512]{2,1,0:T(8,128)(2,1)}), bf16[8,136,512]{2,1,0:T(8,128)(2,1)}, u32[]{:S(2)}, u32[]{:S(2)}) async-start(bf16[8,136,512]{2,1,0:T(8,128)(2,1)} %get-tuple-element.78), calls=%async_computation.3 | async-start | bytes 2228224 | tf_op jit(solution)/shard_map/all_to_all | solution.py:914
  131.8 6.3 %tokens_back.1 = (f32[512,512]{1,0:T(8,128)}, bf16[512,512]{1,0:T(8,128)(2,1)}, bf16[512,512]{1,0:T(8,128)(2,1)}, f32[16,512]{1,0:T(8,128)}) custom-call(bf16[8,136,512]{2,1,0:T(8,128)(2,1)S(1)} %all-to-all-done.2.back_ref, bf16[1,512,512]{2,1,0:T(8,128)(2,1)} %cot_ref.3, s32[2,512]{1,0:T(2,128)S(1)} %get-tuple-element.72.refs_3_.index_ref, ...), custom_call_target="tpu_custom_call" | custom-call | flops 1000 | bytes 1000 | tf_op jit(solution)/shard_map/tokens_back/pallas_call | solution.py:575
  138.2 2.3 %first_sums.1 = (bf16[2,2,128,1024]{3,2,1,0:T(8,128)(2,1)S(1)}, bf16[2,128,1024]{2,1,0:T(8,128)(2,1)S(1)}, bf16[2,128,1024]{2,1,0:T(8,128)(2,1)S(1)}) custom-call(bf16[2,2,128,1024]{3,2,1,0:T(8,128)(2,1)S(1)} %get-tuple-element.85.stay0_ref, bf16[2,2,128,1024]{3,2,1,0:T(8,128)(2,1)} %collective-permute-done.10.come0_ref, ...), custom_call_target="tpu_custom_call" | custom-call | flops 1000 | bytes 1000 | tf_op jit(solution)/shard_map/first_sums/pallas_call | solution.py:761
  140.5 1.6 collective-permute-start.12
  142.1 1.5 collective-permute-start.13
  143.6 12.7 %backward.1 = (bf16[3,512,512]{2,1,0:T(8,128)(2,1)}, bf16[4,264,512]{2,1,0:T(8,128)(2,1)}, bf16[4,264,512]{2,1,0:T(8,128)(2,1)}) custom-call(s32[2]{0:T(128)S(1)} %pad_add_fusion.where_ref.refs_0_, bf16[512,512]{1,0:T(8,128)(2,1)S(1)} %copy-done.2, bf16[16,512]{1,0:T(8,128)(2,1)S(1)} %get-tuple-element.89.small_ref.refs_2_, f32[16,512]{1,0:T(8,128)S(1)} %copy-done.3, ...), custom_call_target="tpu_custom_call" | custom-call | flops 1000 | bytes 1000 | tf_op jit(solution)/shard_map/backward/pallas_call | solution.py:692
  156.5 1.0 copy-done.7
  158.0 1.2 collective-permute-start.14
  159.2 1.0 collective-permute-done.16.b_ref
  160.2 1.2 pair_sum.1
  161.5 5.0 %all-to-all-start.4 = ((bf16[4,264,512]{2,1,0:T(8,128)(2,1)}), bf16[4,264,512]{2,1,0:T(8,128)(2,1)S(1)}, u32[]{:S(2)}, u32[]{:S(2)}) async-start(bf16[4,264,512]{2,1,0:T(8,128)(2,1)} %pair_sum.1), calls=%async_computation.4 | async-start | bytes 2162688 | tf_op jit(solution)/shard_map/all_to_all | solution.py:989
  166.4 4.6 %input_back.1 = bf16[1,512,512]{2,1,0:T(8,128)(2,1)} custom-call(bf16[3,512,512]{2,1,0:T(8,128)(2,1)} %get-tuple-element.103.gp_ref, bf16[4,512,512]{2,1,0:T(8,128)(2,1)} %get-tuple-element.91.refs_0_.refs_6_.full_ref, bf16[1,512,512]{2,1,0:T(8,128)(2,1)} %x_ref.1, f32[512,512]{1,0:T(8,128)} %get-tuple-element.104.grad_resid_ref, ...), custom_call_target="tpu_custom_call" | custom-call | flops 1000 | bytes 1000 | tf_op jit(solution)/shard_map/input_back/pallas_call | solution.py:725
  171.0 12.1 %collective-permute-done.15.refs_3_ = bf16[2,2,128,1024]{3,2,1,0:T(8,128)(2,1)S(1)} collective-permute-done((bf16[2,2,128,1024]{3,2,1,0:T(8,128)(2,1)S(1)}, bf16[2,2,128,1024]{3,2,1,0:T(8,128)(2,1)S(1)}, u32[]{:S(2)}, u32[]{:S(2)}) %collective-permute-start.15) | collective-permute-done | bytes 1048608 | tf_op jit(solution)/shard_map/ppermute | solution.py:939
  183.9 1.9 slice_bitcast_fusion.1
  185.8 0.8 slice_bitcast_fusion
  186.7 1.2 collective-permute-start.21
  187.8 1.5 collective-permute-start.20
  189.4 3.8 %all-to-all-done.4.parts_ref = bf16[4,264,512]{2,1,0:T(8,128)(2,1)S(1)} async-done(((bf16[4,264,512]{2,1,0:T(8,128)(2,1)}), bf16[4,264,512]{2,1,0:T(8,128)(2,1)S(1)}, u32[]{:S(2)}, u32[]{:S(2)}) %all-to-all-start.4) | async-done | bytes 1081376 | tf_op jit(solution)/shard_map/all_to_all | solution.py:989
  193.2 0.8 line_sum.1
  194.0 3.4 %all-to-all-start.5 = ((bf16[4,64,512]{2,1,0:T(8,128)(2,1)}), bf16[4,64,512]{2,1,0:T(8,128)(2,1)S(1)}, u32[]{:S(2)}, u32[]{:S(2)}) async-start(bf16[4,64,512]{2,1,0:T(8,128)(2,1)} %get-tuple-element.116), calls=%async_computation.5 | async-start | bytes 524288 | tf_op jit(solution)/shard_map/all_to_all | solution.py:1009
  197.4 6.8 %widen.2 = (f32[2,512,2048]{2,1,0:T(8,128)}, f32[2,512,2048]{2,1,0:T(8,128)}) custom-call(s32[2]{0:T(128)S(1)} %pad_add_fusion.where_ref.refs_0_, bf16[2,2,128,1024]{3,2,1,0:T(8,128)(2,1)} %copy-done, bf16[2,2,128,1024]{3,2,1,0:T(8,128)(2,1)} %collective-permute-done.14.refs_2_, bf16[2,2,128,1024]{3,2,1,0:T(8,128)(2,1)} %copy-done.4, ...), custom_call_target="tpu_custom_call" | custom-call | flops 1000 | bytes 1000 | tf_op jit(solution)/shard_map/widen/pallas_call | solution.py:842
  204.9 0.9 plane_sum.1
  206.3 3.5 %all-to-all-start.6 = ((bf16[8,72,512]{2,1,0:T(8,128)(2,1)}), bf16[8,72,512]{2,1,0:T(8,128)(2,1)S(1)}, u32[]{:S(2)}, u32[]{:S(2)}) async-start(bf16[8,72,512]{2,1,0:T(8,128)(2,1)} %plane_sum.1), calls=%async_computation.6 | async-start | bytes 1179648 | tf_op jit(solution)/shard_map/all_to_all | solution.py:1016
  209.8 3.7 %combine.1 = bf16[1,512,512]{2,1,0:T(8,128)(2,1)} custom-call(bf16[8,136,512]{2,1,0:T(8,128)(2,1)} %all-to-all-done.3.out_ref, s32[2,512]{1,0:T(2,128)S(1)} %get-tuple-element.72.refs_3_.index_ref, f32[512,512]{1,0:T(8,128)} %get-tuple-element.79.resid_ref.refs_2_), custom_call_target="tpu_custom_call" | custom-call | flops 1000 | bytes 1000 | tf_op jit(solution)/shard_map/combine/pallas_call | solution.py:749
  213.5 0.8 copy-done.5
  215.1 3.7 %widen.3 = (f32[2,512,2048]{2,1,0:T(8,128)}, f32[2,512,2048]{2,1,0:T(8,128)}) custom-call(s32[2]{0:T(128)S(1)} %pad_add_fusion.where_ref.refs_0_, bf16[2,128,1024]{2,1,0:T(8,128)(2,1)} %collective-permute-done.20.refs_1_, bf16[2,128,1024]{2,1,0:T(8,128)(2,1)} %collective-permute-done.21.refs_2_, ...), custom_call_target="tpu_custom_call", output_to_operand_aliasing={{0}: (5, {}), {1}: (6, {})} | custom-call | flops 1000 | bytes 1000 | tf_op jit(solution)/shard_map/widen/pallas_call | solution.py:842
  218.8 1.4 all-to-all-done.6.refs_0_
  220.3 1.0 finish.1
  (61 shorter events, 6.3 us)
Async XLA Ops:
  1.7 9.2 %collective-permute-start.2 = (bf16[5,16,512]{2,1,0:T(8,128)(2,1)S(1)}, bf16[5,16,512]{2,1,0:T(8,128)(2,1)S(1)}, u32[]{:S(2)}, u32[]{:S(2)}) collective-permute-start(bf16[5,16,512]{2,1,0:T(8,128)(2,1)S(1)} %pack_weights.1), channel_id=1, source_target_pairs={{0,3},{1,2},{2,1},{3,0},{4,7},{5,6},{6,5},{7,4},{8,11},{9,10},{10,... | collective-permute-start | bytes 245768 | tf_op jit(solution)/shard_map/ppermute | solution.py:180
  6.8 6.9 %collective-permute-start.1 = (bf16[5,16,512]{2,1,0:T(8,128)(2,1)S(1)}, bf16[5,16,512]{2,1,0:T(8,128)(2,1)S(1)}, u32[]{:S(2)}, u32[]{:S(2)}) collective-permute-start(bf16[5,16,512]{2,1,0:T(8,128)(2,1)S(1)} %pack_weights.1), channel_id=1, source_target_pairs={{0,2},{1,3},{2,0},{3,1},{4,6},{5,7},{6,4},{7,5},{8,10},{9,11},{10,... | collective-permute-start | bytes 245768 | tf_op jit(solution)/shard_map/ppermute | solution.py:180
  6.8 6.9 %collective-permute-start = (bf16[5,16,512]{2,1,0:T(8,128)(2,1)S(1)}, bf16[5,16,512]{2,1,0:T(8,128)(2,1)S(1)}, u32[]{:S(2)}, u32[]{:S(2)}) collective-permute-start(bf16[5,16,512]{2,1,0:T(8,128)(2,1)S(1)} %pack_weights.1), channel_id=1, source_target_pairs={{0,1},{1,0},{2,3},{3,2},{4,5},{5,4},{6,7},{7,6},{8,9},{9,8},{10,11... | collective-permute-start | bytes 245768 | tf_op jit(solution)/shard_map/ppermute | solution.py:180
  13.7 32.0 %all-to-all-start.1 = ((bf16[8,136,512]{2,1,0:T(8,128)(2,1)}), bf16[8,136,512]{2,1,0:T(8,128)(2,1)S(1)}, u32[]{:S(2)}, u32[]{:S(2)}) async-start(bf16[8,136,512]{2,1,0:T(8,128)(2,1)} %get-tuple-element.75), calls=%async_computation.1 | async-start | bytes 2228224 | tf_op jit(solution)/shard_map/all_to_all | solution.py:914
  17.7 8.7 %collective-permute-start.8 = (bf16[3,4,16,512]{3,2,1,0:T(8,128)(2,1)S(1)}, bf16[3,4,16,512]{3,2,1,0:T(8,128)(2,1)S(1)}, u32[]{:S(2)}, u32[]{:S(2)}) collective-permute-start(bf16[3,4,16,512]{3,2,1,0:T(8,128)(2,1)S(1)} %pad_maximum_fusion.refs_7_), channel_id=1, source_target_pairs={{0,24},{4,28},{8,16},{12,20},{16,8},{20,12},{24,0},{28,4},{1,25},{... | collective-permute-start | bytes 589832 | tf_op jit(solution)/shard_map/ppermute | solution.py:186
  20.3 10.0 %collective-permute-start.6 = (bf16[3,4,16,512]{3,2,1,0:T(8,128)(2,1)S(1)}, bf16[3,4,16,512]{3,2,1,0:T(8,128)(2,1)S(1)}, u32[]{:S(2)}, u32[]{:S(2)}) collective-permute-start(bf16[3,4,16,512]{3,2,1,0:T(8,128)(2,1)S(1)} %pad_maximum_fusion.refs_7_), channel_id=1, source_target_pairs={{0,16},{4,20},{8,24},{12,28},{16,0},{20,4},{24,8},{28,12},{1,17},{... | collective-permute-start | bytes 589832 | tf_op jit(solution)/shard_map/ppermute | solution.py:186
  20.8 9.6 %collective-permute-start.4 = (bf16[3,4,16,512]{3,2,1,0:T(8,128)(2,1)S(1)}, bf16[3,4,16,512]{3,2,1,0:T(8,128)(2,1)S(1)}, u32[]{:S(2)}, u32[]{:S(2)}) collective-permute-start(bf16[3,4,16,512]{3,2,1,0:T(8,128)(2,1)S(1)} %pad_maximum_fusion.refs_7_), channel_id=1, source_target_pairs={{0,8},{4,12},{8,0},{12,4},{16,24},{20,28},{24,16},{28,20},{1,9},{5... | collective-permute-start | bytes 589832 | tf_op jit(solution)/shard_map/ppermute | solution.py:186
  21.3 9.5 %collective-permute-start.3 = (bf16[3,4,16,512]{3,2,1,0:T(8,128)(2,1)S(1)}, bf16[3,4,16,512]{3,2,1,0:T(8,128)(2,1)S(1)}, u32[]{:S(2)}, u32[]{:S(2)}) collective-permute-start(bf16[3,4,16,512]{3,2,1,0:T(8,128)(2,1)S(1)} %pad_maximum_fusion.refs_7_), channel_id=1, source_target_pairs={{0,4},{4,0},{8,12},{12,8},{16,20},{20,16},{24,28},{28,24},{1,5},{5... | collective-permute-start | bytes 589832 | tf_op jit(solution)/shard_map/ppermute | solution.py:188
  26.4 4.4 %collective-permute-start.9 = (bf16[3,4,16,512]{3,2,1,0:T(8,128)(2,1)S(1)}, bf16[3,4,16,512]{3,2,1,0:T(8,128)(2,1)S(1)}, u32[]{:S(2)}, u32[]{:S(2)}) collective-permute-start(bf16[3,4,16,512]{3,2,1,0:T(8,128)(2,1)S(1)} %collective-permute-done.8.refs_13_), channel_id=1, source_target_pairs={{0,4},{4,0},{8,12},{12,8},{16,20},{20,16},{24,28},{28,24},{1,5},{5... | collective-permute-start | bytes 589832 | tf_op jit(solution)/shard_map/ppermute | solution.py:188
  30.2 1.4 collective-permute-start.7
  30.3 1.6 collective-permute-start.5
  45.7 31.5 %all-to-all-start = ((bf16[8,136,512]{2,1,0:T(8,128)(2,1)}), bf16[8,136,512]{2,1,0:T(8,128)(2,1)S(1)}, u32[]{:S(2)}, u32[]{:S(2)}) async-start(bf16[8,136,512]{2,1,0:T(8,128)(2,1)} %get-tuple-element.73), calls=%async_computation | async-start | bytes 2228224 | tf_op jit(solution)/shard_map/all_to_all | solution.py:914
  96.1 31.5 %all-to-all-start.2 = ((bf16[8,136,512]{2,1,0:T(8,128)(2,1)}), bf16[8,136,512]{2,1,0:T(8,128)(2,1)S(1)}, u32[]{:S(2)}, u32[]{:S(2)}) async-start(bf16[8,136,512]{2,1,0:T(8,128)(2,1)} %get-tuple-element.77), calls=%async_computation.2 | async-start | bytes 2228224 | tf_op jit(solution)/shard_map/all_to_all | solution.py:914
  110.3 27.8 %collective-permute-start.10 = (bf16[2,2,128,1024]{3,2,1,0:T(8,128)(2,1)}, bf16[2,2,128,1024]{3,2,1,0:T(8,128)(2,1)}, u32[]{:S(2)}, u32[]{:S(2)}) collective-permute-start(bf16[2,2,128,1024]{3,2,1,0:T(8,128)(2,1)} %get-tuple-element.84), channel_id=1, source_target_pairs={{0,8},{4,12},{8,0},{12,4},{16,24},{20,28},{24,16},{28,20},{1,9},{5... | collective-permute-start | bytes 3145736 | tf_op jit(solution)/shard_map/ppermute | solution.py:939
  111.8 26.3 %collective-permute-start.11 = (bf16[2,2,128,1024]{3,2,1,0:T(8,128)(2,1)}, bf16[2,2,128,1024]{3,2,1,0:T(8,128)(2,1)}, u32[]{:S(2)}, u32[]{:S(2)}) collective-permute-start(bf16[2,2,128,1024]{3,2,1,0:T(8,128)(2,1)} %get-tuple-element.86), channel_id=1, source_target_pairs={{0,16},{4,20},{8,24},{12,28},{16,0},{20,4},{24,8},{28,12},{1,17},{... | collective-permute-start | bytes 3145736 | tf_op jit(solution)/shard_map/ppermute | solution.py:939
  127.6 33.9 %all-to-all-start.3 = ((bf16[8,136,512]{2,1,0:T(8,128)(2,1)}), bf16[8,136,512]{2,1,0:T(8,128)(2,1)}, u32[]{:S(2)}, u32[]{:S(2)}) async-start(bf16[8,136,512]{2,1,0:T(8,128)(2,1)} %get-tuple-element.78), calls=%async_computation.3 | async-start | bytes 2228224 | tf_op jit(solution)/shard_map/all_to_all | solution.py:914
  138.2 5.4 %copy-start.2 = (bf16[512,512]{1,0:T(8,128)(2,1)S(1)}, bf16[512,512]{1,0:T(8,128)(2,1)}, u32[]{:S(2)}) copy-start(bf16[512,512]{1,0:T(8,128)(2,1)} %get-tuple-element.98.refs_1_) | copy-start | bytes 1572868
  138.2 5.4 %copy-start.3 = (f32[16,512]{1,0:T(8,128)S(1)}, f32[16,512]{1,0:T(8,128)}, u32[]{:S(2)}) copy-start(f32[16,512]{1,0:T(8,128)} %get-tuple-element.99.refs_3_) | copy-start | bytes 98308
  140.5 15.8 %collective-permute-start.12 = (bf16[2,128,1024]{2,1,0:T(8,128)(2,1)S(1)}, bf16[2,128,1024]{2,1,0:T(8,128)(2,1)S(1)}, u32[]{:S(2)}, u32[]{:S(2)}) collective-permute-start(bf16[2,128,1024]{2,1,0:T(8,128)(2,1)S(1)} %get-tuple-element.107), channel_id=1, source_target_pairs={{0,16},{4,20},{8,24},{12,28},{16,0},{20,4},{24,8},{28,12},{1,17},{... | collective-permute-start | bytes 1572872 | tf_op jit(solution)/shard_map/ppermute | solution.py:939
  142.1 14.2 %collective-permute-start.13 = (bf16[2,128,1024]{2,1,0:T(8,128)(2,1)S(1)}, bf16[2,128,1024]{2,1,0:T(8,128)(2,1)S(1)}, u32[]{:S(2)}, u32[]{:S(2)}) collective-permute-start(bf16[2,128,1024]{2,1,0:T(8,128)(2,1)S(1)} %get-tuple-element.108), channel_id=1, source_target_pairs={{0,8},{4,12},{8,0},{12,4},{16,24},{20,28},{24,16},{28,20},{1,9},{5... | collective-permute-start | bytes 1572872 | tf_op jit(solution)/shard_map/ppermute | solution.py:939
  156.3 1.2 copy-start.7
  156.3 3.9 %copy-start.1 = (bf16[4,264,512]{2,1,0:T(8,128)(2,1)S(1)}, bf16[4,264,512]{2,1,0:T(8,128)(2,1)}, u32[]{:S(2)}) copy-start(bf16[4,264,512]{2,1,0:T(8,128)(2,1)} %get-tuple-element.112.a_ref) | copy-start | bytes 3244036
  157.5 25.9 %copy-start = (bf16[2,2,128,1024]{3,2,1,0:T(8,128)(2,1)}, bf16[2,2,128,1024]{3,2,1,0:T(8,128)(2,1)S(1)}, u32[]{:S(2)}) copy-start(bf16[2,2,128,1024]{3,2,1,0:T(8,128)(2,1)S(1)} %second_sums.1.refs_1_) | copy-start | bytes 3145732
  157.5 2.7 %collective-permute-start.16 = (bf16[4,264,512]{2,1,0:T(8,128)(2,1)S(1)}, bf16[4,264,512]{2,1,0:T(8,128)(2,1)S(1)}, u32[]{:S(2)}, u32[]{:S(2)}) collective-permute-start(bf16[4,264,512]{2,1,0:T(8,128)(2,1)S(1)} %copy-done.7), channel_id=1, source_target_pairs={{0,4},{4,0},{8,12},{12,8},{16,20},{20,16},{24,28},{28,24},{1,5},{5... | collective-permute-start | bytes 3244040 | tf_op jit(solution)/shard_map/ppermute | solution.py:939
  157.5 25.6 %collective-permute-start.15 = (bf16[2,2,128,1024]{3,2,1,0:T(8,128)(2,1)S(1)}, bf16[2,2,128,1024]{3,2,1,0:T(8,128)(2,1)S(1)}, u32[]{:S(2)}, u32[]{:S(2)}) collective-permute-start(bf16[2,2,128,1024]{3,2,1,0:T(8,128)(2,1)S(1)} %second_sums.1.refs_1_), channel_id=1, source_target_pairs={{0,16},{4,20},{8,24},{12,28},{16,0},{20,4},{24,8},{28,12},{1,17},{... | collective-permute-start | bytes 3145736 | tf_op jit(solution)/shard_map/ppermute | solution.py:939
  158.0 25.4 %collective-permute-start.14 = (bf16[2,2,128,1024]{3,2,1,0:T(8,128)(2,1)S(1)}, bf16[2,2,128,1024]{3,2,1,0:T(8,128)(2,1)}, u32[]{:S(2)}, u32[]{:S(2)}) collective-permute-start(bf16[2,2,128,1024]{3,2,1,0:T(8,128)(2,1)S(1)} %second_sums.1.refs_1_), channel_id=1, source_target_pairs={{0,8},{4,12},{8,0},{12,4},{16,24},{20,28},{24,16},{28,20},{1,9},{5... | collective-permute-start | bytes 3145736 | tf_op jit(solution)/shard_map/ppermute | solution.py:939
  161.5 31.7 %all-to-all-start.4 = ((bf16[4,264,512]{2,1,0:T(8,128)(2,1)}), bf16[4,264,512]{2,1,0:T(8,128)(2,1)S(1)}, u32[]{:S(2)}, u32[]{:S(2)}) async-start(bf16[4,264,512]{2,1,0:T(8,128)(2,1)} %pair_sum.1), calls=%async_computation.4 | async-start | bytes 2162688 | tf_op jit(solution)/shard_map/all_to_all | solution.py:989
  183.1 10.9 %copy-start.4 = (bf16[2,2,128,1024]{3,2,1,0:T(8,128)(2,1)}, bf16[2,2,128,1024]{3,2,1,0:T(8,128)(2,1)S(1)}, u32[]{:S(2)}) copy-start(bf16[2,2,128,1024]{3,2,1,0:T(8,128)(2,1)S(1)} %collective-permute-done.15.refs_3_) | copy-start | bytes 3145732
  183.4 14.0 %collective-permute-start.17 = (bf16[2,2,128,1024]{3,2,1,0:T(8,128)(2,1)S(1)}, bf16[2,2,128,1024]{3,2,1,0:T(8,128)(2,1)}, u32[]{:S(2)}, u32[]{:S(2)}) collective-permute-start(bf16[2,2,128,1024]{3,2,1,0:T(8,128)(2,1)S(1)} %second_sums.1.refs_1_), channel_id=1, source_target_pairs={{0,4},{4,0},{8,12},{12,8},{16,20},{20,16},{24,28},{28,24},{1,5},{5... | collective-permute-start | bytes 3145736 | tf_op jit(solution)/shard_map/ppermute | solution.py:939
  183.4 14.0 %collective-permute-start.18 = (bf16[2,2,128,1024]{3,2,1,0:T(8,128)(2,1)}, bf16[2,2,128,1024]{3,2,1,0:T(8,128)(2,1)}, u32[]{:S(2)}, u32[]{:S(2)}) collective-permute-start(bf16[2,2,128,1024]{3,2,1,0:T(8,128)(2,1)} %collective-permute-done.14.refs_2_), channel_id=1, source_target_pairs={{0,4},{4,0},{8,12},{12,8},{16,20},{20,16},{24,28},{28,24},{1,5},{5... | collective-permute-start | bytes 3145736 | tf_op jit(solution)/shard_map/ppermute | solution.py:939
  183.9 13.5 %collective-permute-start.19 = (bf16[2,2,128,1024]{3,2,1,0:T(8,128)(2,1)S(1)}, bf16[2,2,128,1024]{3,2,1,0:T(8,128)(2,1)}, u32[]{:S(2)}, u32[]{:S(2)}) collective-permute-start(bf16[2,2,128,1024]{3,2,1,0:T(8,128)(2,1)S(1)} %collective-permute-done.15.refs_3_), channel_id=1, source_target_pairs={{0,4},{4,0},{8,12},{12,8},{16,20},{20,16},{24,28},{28,24},{1,5},{5... | collective-permute-start | bytes 3145736 | tf_op jit(solution)/shard_map/ppermute | solution.py:939
  186.7 19.1 %collective-permute-start.21 = (bf16[2,128,1024]{2,1,0:T(8,128)(2,1)}, bf16[2,128,1024]{2,1,0:T(8,128)(2,1)}, u32[]{:S(2)}, u32[]{:S(2)}) collective-permute-start(bf16[2,128,1024]{2,1,0:T(8,128)(2,1)} %slice_bitcast_fusion), channel_id=1, source_target_pairs={{0,8},{4,12},{8,0},{12,4},{16,24},{20,28},{24,16},{28,20},{1,9},{5... | collective-permute-start | bytes 1572872 | tf_op jit(solution)/shard_map/ppermute | solution.py:939
  187.8 17.9 %collective-permute-start.20 = (bf16[2,128,1024]{2,1,0:T(8,128)(2,1)}, bf16[2,128,1024]{2,1,0:T(8,128)(2,1)}, u32[]{:S(2)}, u32[]{:S(2)}) collective-permute-start(bf16[2,128,1024]{2,1,0:T(8,128)(2,1)} %slice_bitcast_fusion.1), channel_id=1, source_target_pairs={{0,16},{4,20},{8,24},{12,28},{16,0},{20,4},{24,8},{28,12},{1,17},{... | collective-permute-start | bytes 1572872 | tf_op jit(solution)/shard_map/ppermute | solution.py:939
  194.0 10.9 %all-to-all-start.5 = ((bf16[4,64,512]{2,1,0:T(8,128)(2,1)}), bf16[4,64,512]{2,1,0:T(8,128)(2,1)S(1)}, u32[]{:S(2)}, u32[]{:S(2)}) async-start(bf16[4,64,512]{2,1,0:T(8,128)(2,1)} %get-tuple-element.116), calls=%async_computation.5 | async-start | bytes 524288 | tf_op jit(solution)/shard_map/all_to_all | solution.py:1009
  205.8 7.7 %collective-permute-start.22 = (bf16[2,128,1024]{2,1,0:T(8,128)(2,1)}, bf16[2,128,1024]{2,1,0:T(8,128)(2,1)S(1)}, u32[]{:S(2)}, u32[]{:S(2)}) collective-permute-start(bf16[2,128,1024]{2,1,0:T(8,128)(2,1)} %collective-permute-done.20.refs_1_), channel_id=1, source_target_pairs={{0,4},{4,0},{8,12},{12,8},{16,20},{20,16},{24,28},{28,24},{1,5},{5... | collective-permute-start | bytes 1572872 | tf_op jit(solution)/shard_map/ppermute | solution.py:939
  205.8 7.7 %collective-permute-start.23 = (bf16[2,128,1024]{2,1,0:T(8,128)(2,1)}, bf16[2,128,1024]{2,1,0:T(8,128)(2,1)S(1)}, u32[]{:S(2)}, u32[]{:S(2)}) collective-permute-start(bf16[2,128,1024]{2,1,0:T(8,128)(2,1)} %collective-permute-done.21.refs_2_), channel_id=1, source_target_pairs={{0,4},{4,0},{8,12},{12,8},{16,20},{20,16},{24,28},{28,24},{1,5},{5... | collective-permute-start | bytes 1572872 | tf_op jit(solution)/shard_map/ppermute | solution.py:939
  206.3 14.0 %all-to-all-start.6 = ((bf16[8,72,512]{2,1,0:T(8,128)(2,1)}), bf16[8,72,512]{2,1,0:T(8,128)(2,1)S(1)}, u32[]{:S(2)}, u32[]{:S(2)}) async-start(bf16[8,72,512]{2,1,0:T(8,128)(2,1)} %plane_sum.1), calls=%async_computation.6 | async-start | bytes 1179648 | tf_op jit(solution)/shard_map/all_to_all | solution.py:1016
  213.5 0.8 copy-start.5
  214.3 0.8 copy-start.6

commit v4 on v3

--- a/solution.py
+++ b/solution.py
@@ -396,16 +396,15 @@
         pre_ref[span, cols] = (through_ref[:, cols] * (gate_col * slope)).astype(BF)
     grad_in = dot_nt(pre_ref[span], w_in_ref[0])
     result = dot_nt(hidden_ref[span], w_out_ref[0])
-    ones = jnp.ones((8, rows.shape[1]), BF)
+    lane = iota((ROWS, 8), 1)
     for g in range(2):
         part = slice(g * ROWS, (g + 1) * ROWS)
         out = (gates[g] * result[part]).astype(BF)
         out_ref[g] = out
-        product = out.astype(F32) * cot_ref[g].astype(F32)
-        high = product.astype(BF)
-        low = (product - high.astype(F32)).astype(BF)
-        inner = dot_nt(ones, high) + dot_nt(ones, low)
-        side = side_row(piece_rows(inner[0:1, :]), out.shape[1])
+        inner = jnp.sum(out.astype(F32) * cot_ref[g].astype(F32), axis=1, keepdims=True)
+        high, mid, low = (piece.astype(F32) for piece in split3(inner))
+        pieces = jnp.where(lane == 0, high, jnp.where(lane == 1, mid, jnp.where(lane == 2, low, 0.0)))
+        side = side_row(dot_tn(pieces.astype(BF), eye), out.shape[1])
         back_ref[g] = jnp.where(row == CAPACITY, side, grad_in[part]).astype(BF)
 
 
@@ -680,8 +679,8 @@
     scratch = [pltpu.VMEM((3, count, width), BF)]
     if fast:
         part = (shards_n, 2 * reps * (width // shards_n // reps) + 8, width)
-        outs += [pltpu.HBM(part, BF)] * 2
-        out_specs = [held] * 3
+        outs += [pltpu.VMEM(part, BF), pltpu.HBM(part, BF)]
+        out_specs = [held, *vmem(1), held]
         scratch = [pltpu.VMEM((2, *part), BF)] + scratch
     else:
         outs += [

time: 222 us -> 222 us (level)
  no operation moved by 1% of the time
where the time goes in v4:
time: 222 us; the launch traced here: 221 us
  Pallas kernels  95.2 us (43%)
  waiting for transfers between devices  69.6 us (31%)
  starting transfers between devices  49.5 us (22%)
  local copies, waits for them, and re-layouts  5.31 us (2%)
    all_to_all x4, waiting for transfers between devices, to_experts(): lax.all_to_all(rows, AXES, 0, 0, axis_index_groups=column, tiled=True)  37.9 us
    pallas_call x1, Pallas kernels, experts(): pl.pallas_call(experts_body, out_shape=[pltpu.HBM((groups, ROWS, width),...  18.4 us
    all_to_all x4, starting transfers between devices, to_experts(): lax.all_to_all(rows, AXES, 0, 0, axis_index_groups=column, tiled=True)  15.5 us
    ppermute x14, waiting for transfers between devices, peer(): return lax.ppermute(value, 'rep', [(i, i ^ k) for i in range(reps)])  13 us
    pallas_call x1, Pallas kernels, backward(): pl.pallas_call(lambda *refs: backward_body(fast, reps, shards_n, *refs),...  12.4 us
    ppermute x14, starting transfers between devices, peer(): return lax.ppermute(value, 'rep', [(i, i ^ k) for i in range(reps)])  12 us
    pallas_call x1, Pallas kernels, expert_grads(): pl.pallas_call(lambda *refs: expert_grads_body(split, *refs), out_shape=g...  10.6 us
    pallas_call x2, Pallas kernels, widen(): pl.pallas_call(lambda *refs: widen_body(places, aliased, *refs), out_shap...  10.5 us
  transfers between devices with their start and end apart: 31, of which 15 were waited for; matrix products, arithmetic and copies ran while one was open for 1% of the time, Pallas kernels for 34%

profile of v4, /device:TPU:0, one launch (start us, length us, event | category | flops | bytes accessed | tf_op | source)
XLA Modules:
  0.0 220.7 jit_solution(8283622505874463522)
XLA Ops:
  0.6 1.1 pack_weights.1
  1.7 5.1 %collective-permute-start.2 = (bf16[5,16,512]{2,1,0:T(8,128)(2,1)S(1)}, bf16[5,16,512]{2,1,0:T(8,128)(2,1)S(1)}, u32[]{:S(2)}, u32[]{:S(2)}) collective-permute-start(bf16[5,16,512]{2,1,0:T(8,128)(2,1)S(1)} %pack_weights.1), channel_id=1, source_target_pairs={{0,3},{1,2},{2,1},{3,0},{4,7},{5,6},{6,5},{7,4},{8,11},{9,10},{10,... | collective-permute-start | bytes 245768 | tf_op jit(solution)/shard_map/ppermute | solution.py:180
  7.5 3.5 %route.1 = (s32[2,512]{1,0:T(2,128)S(1)}, bf16[8,136,512]{2,1,0:T(8,128)(2,1)}) custom-call(s32[2,512]{1,0:T(2,128)} %bitcast.19, s32[1,512]{1,0:T(1,128)} %prio_ref.1, bf16[1,512,512]{2,1,0:T(8,128)(2,1)} %cot_ref.3), custom_call_target="tpu_custom_call" | custom-call | flops 1000 | bytes 1000 | tf_op jit(solution)/shard_map/route/pallas_call | solution.py:135
  10.9 2.8 %collective-permute-done.1 = bf16[5,16,512]{2,1,0:T(8,128)(2,1)S(1)} collective-permute-done((bf16[5,16,512]{2,1,0:T(8,128)(2,1)S(1)}, bf16[5,16,512]{2,1,0:T(8,128)(2,1)S(1)}, u32[]{:S(2)}, u32[]{:S(2)}) %collective-permute-start.1) | collective-permute-done | bytes 81952 | tf_op jit(solution)/shard_map/ppermute | solution.py:180
  13.7 4.0 %all-to-all-start.1 = ((bf16[8,136,512]{2,1,0:T(8,128)(2,1)}), bf16[8,136,512]{2,1,0:T(8,128)(2,1)S(1)}, u32[]{:S(2)}, u32[]{:S(2)}) async-start(bf16[8,136,512]{2,1,0:T(8,128)(2,1)} %get-tuple-element.75), calls=%async_computation.1 | async-start | bytes 2228224 | tf_op jit(solution)/shard_map/all_to_all | solution.py:913
  17.7 2.5 %collective-permute-start.8 = (bf16[3,4,16,512]{3,2,1,0:T(8,128)(2,1)S(1)}, bf16[3,4,16,512]{3,2,1,0:T(8,128)(2,1)S(1)}, u32[]{:S(2)}, u32[]{:S(2)}) collective-permute-start(bf16[3,4,16,512]{3,2,1,0:T(8,128)(2,1)S(1)} %pad_maximum_fusion.refs_7_), channel_id=1, source_target_pairs={{0,24},{4,28},{8,16},{12,20},{16,8},{20,12},{24,0},{28,4},{1,25},{... | collective-permute-start | bytes 589832 | tf_op jit(solution)/shard_map/ppermute | solution.py:186
  21.3 5.1 %collective-permute-done.8.refs_13_ = bf16[3,4,16,512]{3,2,1,0:T(8,128)(2,1)S(1)} collective-permute-done((bf16[3,4,16,512]{3,2,1,0:T(8,128)(2,1)S(1)}, bf16[3,4,16,512]{3,2,1,0:T(8,128)(2,1)S(1)}, u32[]{:S(2)}, u32[]{:S(2)}) %collective-permute-start.8) | collective-permute-done | bytes 196640 | tf_op jit(solution)/shard_map/ppermute | solution.py:186
  26.4 3.8 %collective-permute-done.6.refs_11_ = bf16[3,4,16,512]{3,2,1,0:T(8,128)(2,1)S(1)} collective-permute-done((bf16[3,4,16,512]{3,2,1,0:T(8,128)(2,1)S(1)}, bf16[3,4,16,512]{3,2,1,0:T(8,128)(2,1)S(1)}, u32[]{:S(2)}, u32[]{:S(2)}) %collective-permute-start.6) | collective-permute-done | bytes 196640 | tf_op jit(solution)/shard_map/ppermute | solution.py:186
  30.9 0.8 collective-permute-done.7.refs_12_
  32.0 10.4 %forward.1 = (bf16[8,136,512]{2,1,0:T(8,128)(2,1)}, bf16[16,512]{1,0:T(8,128)(2,1)S(1)}, f32[8,512]{1,0:T(8,128)S(1)}, bf16[4,512,512]{2,1,0:T(8,128)(2,1)}, bf1...) custom-call(s32[2]{0:T(128)S(1)} %pad_add_fusion.1.refs_0_, ...), custom_call_target="tpu_custom_call" | custom-call | flops 1000 | bytes 1000 | tf_op jit(solution)/shard_map/forward/pallas_call | solution.py:329
  42.4 3.3 %all-to-all-done.1.cot_ref.refs_1_ = bf16[8,136,512]{2,1,0:T(8,128)(2,1)S(1)} async-done(((bf16[8,136,512]{2,1,0:T(8,128)(2,1)}), bf16[8,136,512]{2,1,0:T(8,128)(2,1)S(1)}, u32[]{:S(2)}, u32[]{:S(2)}) %all-to-all-start.1) | async-done | bytes 1114144 | tf_op jit(solution)/shard_map/all_to_all | solution.py:913
  45.7 3.7 %all-to-all-start = ((bf16[8,136,512]{2,1,0:T(8,128)(2,1)}), bf16[8,136,512]{2,1,0:T(8,128)(2,1)S(1)}, u32[]{:S(2)}, u32[]{:S(2)}) async-start(bf16[8,136,512]{2,1,0:T(8,128)(2,1)} %get-tuple-element.73), calls=%async_computation | async-start | bytes 2228224 | tf_op jit(solution)/shard_map/all_to_all | solution.py:913
  49.5 7.2 %cot_hidden.1.refs_2_ = f32[1088,2048]{1,0:T(8,128)} custom-call(s32[2]{0:T(128)S(1)} %pad_add_fusion.where_ref.refs_0_, bf16[8,136,512]{2,1,0:T(8,128)(2,1)S(1)} %all-to-all-done.1.cot_ref.refs_1_, bf16[2,512,2048]{2,1,0:T(8,128)(2,1)} %refs_4_.3), custom_call_target="tpu_custom_call" | custom-call | flops 1000 | bytes 1000 | tf_op jit(solution)/shard_map/cot_hidden/pallas_call | solution.py:354
  56.7 20.4 %all-to-all-done.refs_0_ = bf16[8,136,512]{2,1,0:T(8,128)(2,1)S(1)} async-done(((bf16[8,136,512]{2,1,0:T(8,128)(2,1)}), bf16[8,136,512]{2,1,0:T(8,128)(2,1)S(1)}, u32[]{:S(2)}, u32[]{:S(2)}) %all-to-all-start) | async-done | bytes 1114144 | tf_op jit(solution)/shard_map/all_to_all | solution.py:913
  77.2 18.4 %experts.1 = (bf16[8,136,512]{2,1,0:T(8,128)(2,1)}, bf16[8,136,512]{2,1,0:T(8,128)(2,1)}, bf16[1088,2048]{1,0:T(8,128)(2,1)}, bf16[1088,2048]{1,0:T(8,128)(2,1)}...) custom-call(s32[2]{0:T(128)S(1)} %pad_add_fusion.where_ref.refs_0_, ...), custom_call_target="tpu_custom_call" | custom-call | flops 1000 | bytes 1000 | tf_op jit(solution)/shard_map/experts/pallas_call | solution.py:423
  95.6 3.6 %all-to-all-start.2 = ((bf16[8,136,512]{2,1,0:T(8,128)(2,1)}), bf16[8,136,512]{2,1,0:T(8,128)(2,1)S(1)}, u32[]{:S(2)}, u32[]{:S(2)}) async-start(bf16[8,136,512]{2,1,0:T(8,128)(2,1)} %get-tuple-element.77), calls=%async_computation.2 | async-start | bytes 2228224 | tf_op jit(solution)/shard_map/all_to_all | solution.py:913
  99.1 10.6 %expert_grads.1 = (bf16[2,2,128,1024]{3,2,1,0:T(8,128)(2,1)}, bf16[2,2,128,1024]{3,2,1,0:T(8,128)(2,1)S(1)}, bf16[2,2,128,1024]{3,2,1,0:T(8,128)(2,1)}, bf16[2,2,128,1024]{3,2,1,0:T(8,128)(2,1)S(1)}) custom-call(s32[2]{0:T(128)S(1)} %pad_add_fusion.where_ref.refs_0_, bf16[1088,2048]{1,0:T(8,128)(2,1)} %get-tuple-element.80.refs_1_, ...), custom_call_target="tpu_custom_call" | custom-call | flops 1000 | bytes 1000 | tf_op jit(solution)/shard_map/expert_grads/pallas_call | solution.py:481
  109.8 1.6 collective-permute-start.10
  111.4 1.5 collective-permute-start.11
  112.8 14.2 %all-to-all-done.2.back_ref = bf16[8,136,512]{2,1,0:T(8,128)(2,1)S(1)} async-done(((bf16[8,136,512]{2,1,0:T(8,128)(2,1)}), bf16[8,136,512]{2,1,0:T(8,128)(2,1)S(1)}, u32[]{:S(2)}, u32[]{:S(2)}) %all-to-all-start.2) | async-done | bytes 1114144 | tf_op jit(solution)/shard_map/all_to_all | solution.py:913
  127.1 4.3 %all-to-all-start.3 = ((bf16[8,136,512]{2,1,0:T(8,128)(2,1)}), bf16[8,136,512]{2,1,0:T(8,128)(2,1)}, u32[]{:S(2)}, u32[]{:S(2)}) async-start(bf16[8,136,512]{2,1,0:T(8,128)(2,1)} %get-tuple-element.78), calls=%async_computation.3 | async-start | bytes 2228224 | tf_op jit(solution)/shard_map/all_to_all | solution.py:913
  131.3 6.3 %tokens_back.1 = (f32[512,512]{1,0:T(8,128)}, bf16[512,512]{1,0:T(8,128)(2,1)}, bf16[512,512]{1,0:T(8,128)(2,1)}, f32[16,512]{1,0:T(8,128)}) custom-call(bf16[8,136,512]{2,1,0:T(8,128)(2,1)S(1)} %all-to-all-done.2.back_ref, bf16[1,512,512]{2,1,0:T(8,128)(2,1)} %cot_ref.3, s32[2,512]{1,0:T(2,128)S(1)} %get-tuple-element.72.refs_3_.index_ref, ...), custom_call_target="tpu_custom_call" | custom-call | flops 1000 | bytes 1000 | tf_op jit(solution)/shard_map/tokens_back/pallas_call | solution.py:574
  137.7 2.3 %first_sums.1 = (bf16[2,2,128,1024]{3,2,1,0:T(8,128)(2,1)S(1)}, bf16[2,128,1024]{2,1,0:T(8,128)(2,1)S(1)}, bf16[2,128,1024]{2,1,0:T(8,128)(2,1)S(1)}) custom-call(bf16[2,2,128,1024]{3,2,1,0:T(8,128)(2,1)S(1)} %get-tuple-element.85.stay0_ref, bf16[2,2,128,1024]{3,2,1,0:T(8,128)(2,1)} %collective-permute-done.10.come0_ref, ...), custom_call_target="tpu_custom_call" | custom-call | flops 1000 | bytes 1000 | tf_op jit(solution)/shard_map/first_sums/pallas_call | solution.py:760
  140.0 1.6 collective-permute-start.12
  141.6 1.5 collective-permute-start.13
  143.0 12.4 %backward.1 = (bf16[3,512,512]{2,1,0:T(8,128)(2,1)}, bf16[4,264,512]{2,1,0:T(8,128)(2,1)S(1)}, bf16[4,264,512]{2,1,0:T(8,128)(2,1)}) custom-call(s32[2]{0:T(128)S(1)} %pad_add_fusion.where_ref.refs_0_, bf16[512,512]{1,0:T(8,128)(2,1)S(1)} %copy-done.1, bf16[16,512]{1,0:T(8,128)(2,1)S(1)} %get-tuple-element.89.small_ref.refs_2_, f32[16,512]{1,0:T(8,128)S(1)} %copy-done.2, ...), custom_call_target="tpu_custom_call" | custom-call | flops 1000 | bytes 1000 | tf_op jit(solution)/shard_map/backward/pallas_call | solution.py:691
  155.8 1.0 copy-done.6
  157.3 1.4 collective-permute-start.14
  159.5 1.2 pair_sum.1
  160.7 5.2 %all-to-all-start.4 = ((bf16[4,264,512]{2,1,0:T(8,128)(2,1)}), bf16[4,264,512]{2,1,0:T(8,128)(2,1)S(1)}, u32[]{:S(2)}, u32[]{:S(2)}) async-start(bf16[4,264,512]{2,1,0:T(8,128)(2,1)} %pair_sum.1), calls=%async_computation.4 | async-start | bytes 2162688 | tf_op jit(solution)/shard_map/all_to_all | solution.py:988
  165.9 4.6 %input_back.1 = bf16[1,512,512]{2,1,0:T(8,128)(2,1)} custom-call(bf16[3,512,512]{2,1,0:T(8,128)(2,1)} %get-tuple-element.103.gp_ref, bf16[4,512,512]{2,1,0:T(8,128)(2,1)} %get-tuple-element.91.refs_0_.refs_6_.full_ref, bf16[1,512,512]{2,1,0:T(8,128)(2,1)} %x_ref.1, f32[512,512]{1,0:T(8,128)} %get-tuple-element.104.grad_resid_ref, ...), custom_call_target="tpu_custom_call" | custom-call | flops 1000 | bytes 1000 | tf_op jit(solution)/shard_map/input_back/pallas_call | solution.py:724
  170.5 11.9 %collective-permute-done.15.refs_3_ = bf16[2,2,128,1024]{3,2,1,0:T(8,128)(2,1)S(1)} collective-permute-done((bf16[2,2,128,1024]{3,2,1,0:T(8,128)(2,1)S(1)}, bf16[2,2,128,1024]{3,2,1,0:T(8,128)(2,1)S(1)}, u32[]{:S(2)}, u32[]{:S(2)}) %collective-permute-start.15) | collective-permute-done | bytes 1048608 | tf_op jit(solution)/shard_map/ppermute | solution.py:938
  183.2 1.9 slice_bitcast_fusion.1
  185.1 0.8 slice_bitcast_fusion
  185.9 1.4 collective-permute-start.21
  187.4 1.5 collective-permute-start.20
  188.8 3.8 %all-to-all-done.4.parts_ref = bf16[4,264,512]{2,1,0:T(8,128)(2,1)S(1)} async-done(((bf16[4,264,512]{2,1,0:T(8,128)(2,1)}), bf16[4,264,512]{2,1,0:T(8,128)(2,1)S(1)}, u32[]{:S(2)}, u32[]{:S(2)}) %all-to-all-start.4) | async-done | bytes 1081376 | tf_op jit(solution)/shard_map/all_to_all | solution.py:988
  192.6 0.8 line_sum.1
  193.5 3.4 %all-to-all-start.5 = ((bf16[4,64,512]{2,1,0:T(8,128)(2,1)}), bf16[4,64,512]{2,1,0:T(8,128)(2,1)S(1)}, u32[]{:S(2)}, u32[]{:S(2)}) async-start(bf16[4,64,512]{2,1,0:T(8,128)(2,1)} %get-tuple-element.116), calls=%async_computation.5 | async-start | bytes 524288 | tf_op jit(solution)/shard_map/all_to_all | solution.py:1008
  196.9 6.8 %widen.2 = (f32[2,512,2048]{2,1,0:T(8,128)}, f32[2,512,2048]{2,1,0:T(8,128)}) custom-call(s32[2]{0:T(128)S(1)} %pad_add_fusion.where_ref.refs_0_, bf16[2,2,128,1024]{3,2,1,0:T(8,128)(2,1)} %copy-done, bf16[2,2,128,1024]{3,2,1,0:T(8,128)(2,1)} %collective-permute-done.14.refs_2_, bf16[2,2,128,1024]{3,2,1,0:T(8,128)(2,1)} %copy-done.3, ...), custom_call_target="tpu_custom_call" | custom-call | flops 1000 | bytes 1000 | tf_op jit(solution)/shard_map/widen/pallas_call | solution.py:841
  204.4 0.9 plane_sum.1
  205.8 3.5 %all-to-all-start.6 = ((bf16[8,72,512]{2,1,0:T(8,128)(2,1)}), bf16[8,72,512]{2,1,0:T(8,128)(2,1)S(1)}, u32[]{:S(2)}, u32[]{:S(2)}) async-start(bf16[8,72,512]{2,1,0:T(8,128)(2,1)} %plane_sum.1), calls=%async_computation.6 | async-start | bytes 1179648 | tf_op jit(solution)/shard_map/all_to_all | solution.py:1015
  209.4 3.7 %combine.1 = bf16[1,512,512]{2,1,0:T(8,128)(2,1)} custom-call(bf16[8,136,512]{2,1,0:T(8,128)(2,1)} %all-to-all-done.3.out_ref, s32[2,512]{1,0:T(2,128)S(1)} %get-tuple-element.72.refs_3_.index_ref, f32[512,512]{1,0:T(8,128)} %get-tuple-element.79.resid_ref.refs_2_), custom_call_target="tpu_custom_call" | custom-call | flops 1000 | bytes 1000 | tf_op jit(solution)/shard_map/combine/pallas_call | solution.py:748
  213.0 0.8 copy-done.4
  213.8 0.8 copy-done.5
  214.6 3.7 %widen.3 = (f32[2,512,2048]{2,1,0:T(8,128)}, f32[2,512,2048]{2,1,0:T(8,128)}) custom-call(s32[2]{0:T(128)S(1)} %pad_add_fusion.where_ref.refs_0_, bf16[2,128,1024]{2,1,0:T(8,128)(2,1)} %collective-permute-done.20.refs_1_, bf16[2,128,1024]{2,1,0:T(8,128)(2,1)} %collective-permute-done.21.refs_2_, ...), custom_call_target="tpu_custom_call", output_to_operand_aliasing={{0}: (5, {}), {1}: (6, {})} | custom-call | flops 1000 | bytes 1000 | tf_op jit(solution)/shard_map/widen/pallas_call | solution.py:841
  218.3 1.4 all-to-all-done.6.refs_0_
  219.7 1.0 finish.1
  (59 shorter events, 6.4 us)
Async XLA Ops:
  1.7 9.2 %collective-permute-start.2 = (bf16[5,16,512]{2,1,0:T(8,128)(2,1)S(1)}, bf16[5,16,512]{2,1,0:T(8,128)(2,1)S(1)}, u32[]{:S(2)}, u32[]{:S(2)}) collective-permute-start(bf16[5,16,512]{2,1,0:T(8,128)(2,1)S(1)} %pack_weights.1), channel_id=1, source_target_pairs={{0,3},{1,2},{2,1},{3,0},{4,7},{5,6},{6,5},{7,4},{8,11},{9,10},{10,... | collective-permute-start | bytes 245768 | tf_op jit(solution)/shard_map/ppermute | solution.py:180
  6.8 6.9 %collective-permute-start.1 = (bf16[5,16,512]{2,1,0:T(8,128)(2,1)S(1)}, bf16[5,16,512]{2,1,0:T(8,128)(2,1)S(1)}, u32[]{:S(2)}, u32[]{:S(2)}) collective-permute-start(bf16[5,16,512]{2,1,0:T(8,128)(2,1)S(1)} %pack_weights.1), channel_id=1, source_target_pairs={{0,2},{1,3},{2,0},{3,1},{4,6},{5,7},{6,4},{7,5},{8,10},{9,11},{10,... | collective-permute-start | bytes 245768 | tf_op jit(solution)/shard_map/ppermute | solution.py:180
  6.8 6.9 %collective-permute-start = (bf16[5,16,512]{2,1,0:T(8,128)(2,1)S(1)}, bf16[5,16,512]{2,1,0:T(8,128)(2,1)S(1)}, u32[]{:S(2)}, u32[]{:S(2)}) collective-permute-start(bf16[5,16,512]{2,1,0:T(8,128)(2,1)S(1)} %pack_weights.1), channel_id=1, source_target_pairs={{0,1},{1,0},{2,3},{3,2},{4,5},{5,4},{6,7},{7,6},{8,9},{9,8},{10,11... | collective-permute-start | bytes 245768 | tf_op jit(solution)/shard_map/ppermute | solution.py:180
  13.7 32.0 %all-to-all-start.1 = ((bf16[8,136,512]{2,1,0:T(8,128)(2,1)}), bf16[8,136,512]{2,1,0:T(8,128)(2,1)S(1)}, u32[]{:S(2)}, u32[]{:S(2)}) async-start(bf16[8,136,512]{2,1,0:T(8,128)(2,1)} %get-tuple-element.75), calls=%async_computation.1 | async-start | bytes 2228224 | tf_op jit(solution)/shard_map/all_to_all | solution.py:913
  17.7 8.7 %collective-permute-start.8 = (bf16[3,4,16,512]{3,2,1,0:T(8,128)(2,1)S(1)}, bf16[3,4,16,512]{3,2,1,0:T(8,128)(2,1)S(1)}, u32[]{:S(2)}, u32[]{:S(2)}) collective-permute-start(bf16[3,4,16,512]{3,2,1,0:T(8,128)(2,1)S(1)} %pad_maximum_fusion.refs_7_), channel_id=1, source_target_pairs={{0,24},{4,28},{8,16},{12,20},{16,8},{20,12},{24,0},{28,4},{1,25},{... | collective-permute-start | bytes 589832 | tf_op jit(solution)/shard_map/ppermute | solution.py:186
  20.3 10.0 %collective-permute-start.6 = (bf16[3,4,16,512]{3,2,1,0:T(8,128)(2,1)S(1)}, bf16[3,4,16,512]{3,2,1,0:T(8,128)(2,1)S(1)}, u32[]{:S(2)}, u32[]{:S(2)}) collective-permute-start(bf16[3,4,16,512]{3,2,1,0:T(8,128)(2,1)S(1)} %pad_maximum_fusion.refs_7_), channel_id=1, source_target_pairs={{0,16},{4,20},{8,24},{12,28},{16,0},{20,4},{24,8},{28,12},{1,17},{... | collective-permute-start | bytes 589832 | tf_op jit(solution)/shard_map/ppermute | solution.py:186
  20.8 9.6 %collective-permute-start.4 = (bf16[3,4,16,512]{3,2,1,0:T(8,128)(2,1)S(1)}, bf16[3,4,16,512]{3,2,1,0:T(8,128)(2,1)S(1)}, u32[]{:S(2)}, u32[]{:S(2)}) collective-permute-start(bf16[3,4,16,512]{3,2,1,0:T(8,128)(2,1)S(1)} %pad_maximum_fusion.refs_7_), channel_id=1, source_target_pairs={{0,8},{4,12},{8,0},{12,4},{16,24},{20,28},{24,16},{28,20},{1,9},{5... | collective-permute-start | bytes 589832 | tf_op jit(solution)/shard_map/ppermute | solution.py:186
  21.3 9.5 %collective-permute-start.3 = (bf16[3,4,16,512]{3,2,1,0:T(8,128)(2,1)S(1)}, bf16[3,4,16,512]{3,2,1,0:T(8,128)(2,1)S(1)}, u32[]{:S(2)}, u32[]{:S(2)}) collective-permute-start(bf16[3,4,16,512]{3,2,1,0:T(8,128)(2,1)S(1)} %pad_maximum_fusion.refs_7_), channel_id=1, source_target_pairs={{0,4},{4,0},{8,12},{12,8},{16,20},{20,16},{24,28},{28,24},{1,5},{5... | collective-permute-start | bytes 589832 | tf_op jit(solution)/shard_map/ppermute | solution.py:188
  26.4 4.4 %collective-permute-start.9 = (bf16[3,4,16,512]{3,2,1,0:T(8,128)(2,1)S(1)}, bf16[3,4,16,512]{3,2,1,0:T(8,128)(2,1)S(1)}, u32[]{:S(2)}, u32[]{:S(2)}) collective-permute-start(bf16[3,4,16,512]{3,2,1,0:T(8,128)(2,1)S(1)} %collective-permute-done.8.refs_13_), channel_id=1, source_target_pairs={{0,4},{4,0},{8,12},{12,8},{16,20},{20,16},{24,28},{28,24},{1,5},{5... | collective-permute-start | bytes 589832 | tf_op jit(solution)/shard_map/ppermute | solution.py:188
  30.2 1.4 collective-permute-start.7
  30.3 1.6 collective-permute-start.5
  45.7 31.5 %all-to-all-start = ((bf16[8,136,512]{2,1,0:T(8,128)(2,1)}), bf16[8,136,512]{2,1,0:T(8,128)(2,1)S(1)}, u32[]{:S(2)}, u32[]{:S(2)}) async-start(bf16[8,136,512]{2,1,0:T(8,128)(2,1)} %get-tuple-element.73), calls=%async_computation | async-start | bytes 2228224 | tf_op jit(solution)/shard_map/all_to_all | solution.py:913
  95.6 31.5 %all-to-all-start.2 = ((bf16[8,136,512]{2,1,0:T(8,128)(2,1)}), bf16[8,136,512]{2,1,0:T(8,128)(2,1)S(1)}, u32[]{:S(2)}, u32[]{:S(2)}) async-start(bf16[8,136,512]{2,1,0:T(8,128)(2,1)} %get-tuple-element.77), calls=%async_computation.2 | async-start | bytes 2228224 | tf_op jit(solution)/shard_map/all_to_all | solution.py:913
  109.8 27.9 %collective-permute-start.10 = (bf16[2,2,128,1024]{3,2,1,0:T(8,128)(2,1)}, bf16[2,2,128,1024]{3,2,1,0:T(8,128)(2,1)}, u32[]{:S(2)}, u32[]{:S(2)}) collective-permute-start(bf16[2,2,128,1024]{3,2,1,0:T(8,128)(2,1)} %get-tuple-element.84), channel_id=1, source_target_pairs={{0,8},{4,12},{8,0},{12,4},{16,24},{20,28},{24,16},{28,20},{1,9},{5... | collective-permute-start | bytes 3145736 | tf_op jit(solution)/shard_map/ppermute | solution.py:938
  111.4 26.3 %collective-permute-start.11 = (bf16[2,2,128,1024]{3,2,1,0:T(8,128)(2,1)}, bf16[2,2,128,1024]{3,2,1,0:T(8,128)(2,1)}, u32[]{:S(2)}, u32[]{:S(2)}) collective-permute-start(bf16[2,2,128,1024]{3,2,1,0:T(8,128)(2,1)} %get-tuple-element.86), channel_id=1, source_target_pairs={{0,16},{4,20},{8,24},{12,28},{16,0},{20,4},{24,8},{28,12},{1,17},{... | collective-permute-start | bytes 3145736 | tf_op jit(solution)/shard_map/ppermute | solution.py:938
  127.1 33.6 %all-to-all-start.3 = ((bf16[8,136,512]{2,1,0:T(8,128)(2,1)}), bf16[8,136,512]{2,1,0:T(8,128)(2,1)}, u32[]{:S(2)}, u32[]{:S(2)}) async-start(bf16[8,136,512]{2,1,0:T(8,128)(2,1)} %get-tuple-element.78), calls=%async_computation.3 | async-start | bytes 2228224 | tf_op jit(solution)/shard_map/all_to_all | solution.py:913
  137.7 5.4 %copy-start.1 = (bf16[512,512]{1,0:T(8,128)(2,1)S(1)}, bf16[512,512]{1,0:T(8,128)(2,1)}, u32[]{:S(2)}) copy-start(bf16[512,512]{1,0:T(8,128)(2,1)} %get-tuple-element.98.refs_1_) | copy-start | bytes 1572868
  137.7 5.4 %copy-start.2 = (f32[16,512]{1,0:T(8,128)S(1)}, f32[16,512]{1,0:T(8,128)}, u32[]{:S(2)}) copy-start(f32[16,512]{1,0:T(8,128)} %get-tuple-element.99.refs_3_) | copy-start | bytes 98308
  140.0 15.5 %collective-permute-start.12 = (bf16[2,128,1024]{2,1,0:T(8,128)(2,1)S(1)}, bf16[2,128,1024]{2,1,0:T(8,128)(2,1)S(1)}, u32[]{:S(2)}, u32[]{:S(2)}) collective-permute-start(bf16[2,128,1024]{2,1,0:T(8,128)(2,1)S(1)} %get-tuple-element.107), channel_id=1, source_target_pairs={{0,16},{4,20},{8,24},{12,28},{16,0},{20,4},{24,8},{28,12},{1,17},{... | collective-permute-start | bytes 1572872 | tf_op jit(solution)/shard_map/ppermute | solution.py:938
  141.6 14.0 %collective-permute-start.13 = (bf16[2,128,1024]{2,1,0:T(8,128)(2,1)S(1)}, bf16[2,128,1024]{2,1,0:T(8,128)(2,1)S(1)}, u32[]{:S(2)}, u32[]{:S(2)}) collective-permute-start(bf16[2,128,1024]{2,1,0:T(8,128)(2,1)S(1)} %get-tuple-element.108), channel_id=1, source_target_pairs={{0,8},{4,12},{8,0},{12,4},{16,24},{20,28},{24,16},{28,20},{1,9},{5... | collective-permute-start | bytes 1572872 | tf_op jit(solution)/shard_map/ppermute | solution.py:938
  155.5 1.2 copy-start.6
  156.8 26.0 %copy-start = (bf16[2,2,128,1024]{3,2,1,0:T(8,128)(2,1)}, bf16[2,2,128,1024]{3,2,1,0:T(8,128)(2,1)S(1)}, u32[]{:S(2)}) copy-start(bf16[2,2,128,1024]{3,2,1,0:T(8,128)(2,1)S(1)} %second_sums.1.refs_1_) | copy-start | bytes 3145732
  156.8 2.7 %collective-permute-start.16 = (bf16[4,264,512]{2,1,0:T(8,128)(2,1)S(1)}, bf16[4,264,512]{2,1,0:T(8,128)(2,1)S(1)}, u32[]{:S(2)}, u32[]{:S(2)}) collective-permute-start(bf16[4,264,512]{2,1,0:T(8,128)(2,1)S(1)} %copy-done.6), channel_id=1, source_target_pairs={{0,4},{4,0},{8,12},{12,8},{16,20},{20,16},{24,28},{28,24},{1,5},{5... | collective-permute-start | bytes 3244040 | tf_op jit(solution)/shard_map/ppermute | solution.py:938
  156.8 25.6 %collective-permute-start.15 = (bf16[2,2,128,1024]{3,2,1,0:T(8,128)(2,1)S(1)}, bf16[2,2,128,1024]{3,2,1,0:T(8,128)(2,1)S(1)}, u32[]{:S(2)}, u32[]{:S(2)}) collective-permute-start(bf16[2,2,128,1024]{3,2,1,0:T(8,128)(2,1)S(1)} %second_sums.1.refs_1_), channel_id=1, source_target_pairs={{0,16},{4,20},{8,24},{12,28},{16,0},{20,4},{24,8},{28,12},{1,17},{... | collective-permute-start | bytes 3145736 | tf_op jit(solution)/shard_map/ppermute | solution.py:938
  157.3 25.4 %collective-permute-start.14 = (bf16[2,2,128,1024]{3,2,1,0:T(8,128)(2,1)S(1)}, bf16[2,2,128,1024]{3,2,1,0:T(8,128)(2,1)}, u32[]{:S(2)}, u32[]{:S(2)}) collective-permute-start(bf16[2,2,128,1024]{3,2,1,0:T(8,128)(2,1)S(1)} %second_sums.1.refs_1_), channel_id=1, source_target_pairs={{0,8},{4,12},{8,0},{12,4},{16,24},{20,28},{24,16},{28,20},{1,9},{5... | collective-permute-start | bytes 3145736 | tf_op jit(solution)/shard_map/ppermute | solution.py:938
  160.7 31.9 %all-to-all-start.4 = ((bf16[4,264,512]{2,1,0:T(8,128)(2,1)}), bf16[4,264,512]{2,1,0:T(8,128)(2,1)S(1)}, u32[]{:S(2)}, u32[]{:S(2)}) async-start(bf16[4,264,512]{2,1,0:T(8,128)(2,1)} %pair_sum.1), calls=%async_computation.4 | async-start | bytes 2162688 | tf_op jit(solution)/shard_map/all_to_all | solution.py:988
  182.3 11.1 %copy-start.3 = (bf16[2,2,128,1024]{3,2,1,0:T(8,128)(2,1)}, bf16[2,2,128,1024]{3,2,1,0:T(8,128)(2,1)S(1)}, u32[]{:S(2)}) copy-start(bf16[2,2,128,1024]{3,2,1,0:T(8,128)(2,1)S(1)} %collective-permute-done.15.refs_3_) | copy-start | bytes 3145732
  182.7 14.2 %collective-permute-start.17 = (bf16[2,2,128,1024]{3,2,1,0:T(8,128)(2,1)S(1)}, bf16[2,2,128,1024]{3,2,1,0:T(8,128)(2,1)}, u32[]{:S(2)}, u32[]{:S(2)}) collective-permute-start(bf16[2,2,128,1024]{3,2,1,0:T(8,128)(2,1)S(1)} %second_sums.1.refs_1_), channel_id=1, source_target_pairs={{0,4},{4,0},{8,12},{12,8},{16,20},{20,16},{24,28},{28,24},{1,5},{5... | collective-permute-start | bytes 3145736 | tf_op jit(solution)/shard_map/ppermute | solution.py:938
  182.7 14.2 %collective-permute-start.18 = (bf16[2,2,128,1024]{3,2,1,0:T(8,128)(2,1)}, bf16[2,2,128,1024]{3,2,1,0:T(8,128)(2,1)}, u32[]{:S(2)}, u32[]{:S(2)}) collective-permute-start(bf16[2,2,128,1024]{3,2,1,0:T(8,128)(2,1)} %collective-permute-done.14.refs_2_), channel_id=1, source_target_pairs={{0,4},{4,0},{8,12},{12,8},{16,20},{20,16},{24,28},{28,24},{1,5},{5... | collective-permute-start | bytes 3145736 | tf_op jit(solution)/shard_map/ppermute | solution.py:938
  183.2 13.7 %collective-permute-start.19 = (bf16[2,2,128,1024]{3,2,1,0:T(8,128)(2,1)S(1)}, bf16[2,2,128,1024]{3,2,1,0:T(8,128)(2,1)}, u32[]{:S(2)}, u32[]{:S(2)}) collective-permute-start(bf16[2,2,128,1024]{3,2,1,0:T(8,128)(2,1)S(1)} %collective-permute-done.15.refs_3_), channel_id=1, source_target_pairs={{0,4},{4,0},{8,12},{12,8},{16,20},{20,16},{24,28},{28,24},{1,5},{5... | collective-permute-start | bytes 3145736 | tf_op jit(solution)/shard_map/ppermute | solution.py:938
  185.9 19.4 %collective-permute-start.21 = (bf16[2,128,1024]{2,1,0:T(8,128)(2,1)}, bf16[2,128,1024]{2,1,0:T(8,128)(2,1)}, u32[]{:S(2)}, u32[]{:S(2)}) collective-permute-start(bf16[2,128,1024]{2,1,0:T(8,128)(2,1)} %slice_bitcast_fusion), channel_id=1, source_target_pairs={{0,8},{4,12},{8,0},{12,4},{16,24},{20,28},{24,16},{28,20},{1,9},{5... | collective-permute-start | bytes 1572872 | tf_op jit(solution)/shard_map/ppermute | solution.py:938
  187.4 17.9 %collective-permute-start.20 = (bf16[2,128,1024]{2,1,0:T(8,128)(2,1)}, bf16[2,128,1024]{2,1,0:T(8,128)(2,1)}, u32[]{:S(2)}, u32[]{:S(2)}) collective-permute-start(bf16[2,128,1024]{2,1,0:T(8,128)(2,1)} %slice_bitcast_fusion.1), channel_id=1, source_target_pairs={{0,16},{4,20},{8,24},{12,28},{16,0},{20,4},{24,8},{28,12},{1,17},{... | collective-permute-start | bytes 1572872 | tf_op jit(solution)/shard_map/ppermute | solution.py:938
  193.5 11.0 %all-to-all-start.5 = ((bf16[4,64,512]{2,1,0:T(8,128)(2,1)}), bf16[4,64,512]{2,1,0:T(8,128)(2,1)S(1)}, u32[]{:S(2)}, u32[]{:S(2)}) async-start(bf16[4,64,512]{2,1,0:T(8,128)(2,1)} %get-tuple-element.116), calls=%async_computation.5 | async-start | bytes 524288 | tf_op jit(solution)/shard_map/all_to_all | solution.py:1008
  205.3 7.7 %collective-permute-start.22 = (bf16[2,128,1024]{2,1,0:T(8,128)(2,1)}, bf16[2,128,1024]{2,1,0:T(8,128)(2,1)S(1)}, u32[]{:S(2)}, u32[]{:S(2)}) collective-permute-start(bf16[2,128,1024]{2,1,0:T(8,128)(2,1)} %collective-permute-done.20.refs_1_), channel_id=1, source_target_pairs={{0,4},{4,0},{8,12},{12,8},{16,20},{20,16},{24,28},{28,24},{1,5},{5... | collective-permute-start | bytes 1572872 | tf_op jit(solution)/shard_map/ppermute | solution.py:938
  205.3 7.7 %collective-permute-start.23 = (bf16[2,128,1024]{2,1,0:T(8,128)(2,1)}, bf16[2,128,1024]{2,1,0:T(8,128)(2,1)S(1)}, u32[]{:S(2)}, u32[]{:S(2)}) collective-permute-start(bf16[2,128,1024]{2,1,0:T(8,128)(2,1)} %collective-permute-done.21.refs_2_), channel_id=1, source_target_pairs={{0,4},{4,0},{8,12},{12,8},{16,20},{20,16},{24,28},{28,24},{1,5},{5... | collective-permute-start | bytes 1572872 | tf_op jit(solution)/shard_map/ppermute | solution.py:938
  205.8 13.9 %all-to-all-start.6 = ((bf16[8,72,512]{2,1,0:T(8,128)(2,1)}), bf16[8,72,512]{2,1,0:T(8,128)(2,1)S(1)}, u32[]{:S(2)}, u32[]{:S(2)}) async-start(bf16[8,72,512]{2,1,0:T(8,128)(2,1)} %plane_sum.1), calls=%async_computation.6 | async-start | bytes 1179648 | tf_op jit(solution)/shard_map/all_to_all | solution.py:1015
  213.0 0.8 copy-start.4
  213.8 0.8 copy-start.5

commit v5 on v4

--- a/solution.py
+++ b/solution.py
@@ -369,21 +369,21 @@
     )(where, cot, far(w_out))
 
 
-def expert_rows(n2_ref, cot_ref, through_ref, w_in_ref, w_out_ref, back_ref, out_ref, span, scratch):
-    hidden_ref, pre_ref, rows_ref, gso_ref = scratch
-    row = iota((ROWS, 1), 0)
+def experts_body(where_ref, *refs):
+    n2_ref, cot_ref, through_ref, w_in_ref, w_out_ref = refs[:5]
+    back_ref, out_ref, hidden_ref, pre_ref, gso_ref = refs[5:]
     eye = jnp.where(iota((ROWS, ROWS), 0) == iota((ROWS, ROWS), 1), 1.0, 0.0).astype(BF)
-    gates, rows_all, gso_all = [], [], []
+    lane = iota((ROWS, 8), 1)
+    gates = []
     for g in range(2):
-        rows = n2_ref[g].astype(F32)
-        parts = side_parts(rows[CAPACITY : CAPACITY + 1]).astype(BF)
-        gate = jnp.sum(dot_nt(eye, parts), axis=1, keepdims=True)
-        gates.append(gate)
-        rows_all.append(jnp.where(row < CAPACITY, rows, 0.0))
-        gso_all.append(gate * cot_ref[g].astype(F32))
-    rows = jnp.concatenate(rows_all, axis=0).astype(BF)
+        last = (g + 1) * ROWS - 1
+        start = last // 16 * 16
+        eight = n2_ref[start : start + 16, :].astype(F32)
+        parts = side_parts(eight[last - start : last - start + 1]).astype(BF)
+        gates.append(jnp.sum(dot_nt(eye, parts), axis=1, keepdims=True))
     gate_col = jnp.concatenate(gates, axis=0)
-    rows_ref[span], gso_ref[span] = rows, jnp.concatenate(gso_all, axis=0).astype(BF)
+    rows = n2_ref[...]
+    gso_ref[...] = (gate_col * cot_ref[...].astype(F32)).astype(BF)
     for start in range(0, w_in_ref.shape[2], FF_STEP):
         cols = slice(start, start + FF_STEP)
         u = dot_nn(rows, w_in_ref[0, :, cols])
@@ -392,24 +392,22 @@
         half = 0.5 * (1.0 + t)
         hidden = u * half
         slope = half + hidden * (1.0 - t) * (GELU_A * (1.0 + 3.0 * GELU_B * square))
-        hidden_ref[span, cols] = hidden.astype(BF)
-        pre_ref[span, cols] = (through_ref[:, cols] * (gate_col * slope)).astype(BF)
-    grad_in = dot_nt(pre_ref[span], w_in_ref[0])
-    result = dot_nt(hidden_ref[span], w_out_ref[0])
-    lane = iota((ROWS, 8), 1)
+        hidden_ref[:, cols] = hidden.astype(BF)
+        pre_ref[:, cols] = (through_ref[:, cols] * (gate_col * slope)).astype(BF)
+    grad_in = dot_nt(pre_ref[...], w_in_ref[0])
+    result = dot_nt(hidden_ref[...], w_out_ref[0])
+    out = (gate_col * result).astype(BF)
+    out_ref[...] = out
+    inner_all = jnp.sum(out.astype(F32) * cot_ref[...].astype(F32), axis=1, keepdims=True)
+    row = iota((2 * ROWS, 1), 0)
+    back = grad_in
     for g in range(2):
-        part = slice(g * ROWS, (g + 1) * ROWS)
-        out = (gates[g] * result[part]).astype(BF)
-        out_ref[g] = out
-        inner = jnp.sum(out.astype(F32) * cot_ref[g].astype(F32), axis=1, keepdims=True)
+        inner = inner_all[g * ROWS : (g + 1) * ROWS]
         high, mid, low = (piece.astype(F32) for piece in split3(inner))
         pieces = jnp.where(lane == 0, high, jnp.where(lane == 1, mid, jnp.where(lane == 2, low, 0.0)))
         side = side_row(dot_tn(pieces.astype(BF), eye), out.shape[1])
-        back_ref[g] = jnp.where(row == CAPACITY, side, grad_in[part]).astype(BF)
-
-
-def experts_body(where_ref, *refs):
-    expert_rows(*refs[:7], slice(None), refs[7:])
+        back = jnp.where(row == (g + 1) * ROWS - 1, side, back)
+    back_ref[...] = back.astype(BF)
 
 
 def experts(where, n2, cot, through, w_in, w_out):
@@ -417,26 +415,30 @@
     hidden_n = w_in.shape[2]
     total = groups * ROWS
     weight = pl.BlockSpec((1, width, hidden_n), lambda i, w: (w[0], 0, 0))
-    payload = pl.BlockSpec((2, ROWS, width), lambda i, w: (i, 0, 0))
     narrow = pl.BlockSpec((2 * ROWS, width), lambda i, w: (i, 0))
     wide = pl.BlockSpec((2 * ROWS, hidden_n), lambda i, w: (i, 0))
-    return pl.pallas_call(
+    n2, cot = n2.reshape(total, width), cot.reshape(total, width)
+    back, out, hidden, pre, gso = pl.pallas_call(
         experts_body,
-        out_shape=(
-            [pltpu.HBM((groups, ROWS, width), BF)] * 2
-            + [pltpu.HBM((total, hidden_n), BF)] * 2
-            + [pltpu.HBM((total, width), BF)] * 2
-        ),
+        out_shape=[
+            pltpu.HBM((total, width), BF),
+            pltpu.HBM((total, width), BF),
+            pltpu.HBM((total, hidden_n), BF),
+            pltpu.HBM((total, hidden_n), BF),
+            pltpu.HBM((total, width), BF),
+        ],
         grid_spec=pltpu.PrefetchScalarGridSpec(
             num_scalar_prefetch=1,
             grid=(groups // 2,),
-            in_specs=[payload, payload, wide, weight, weight],
-            out_specs=[payload, payload, wide, wide, narrow, narrow],
+            in_specs=[narrow, narrow, wide, weight, weight],
+            out_specs=[narrow, narrow, wide, wide, narrow],
         ),
         compiler_params=params(44),
         cost_estimate=SMALL,
         name="experts",
     )(where, n2, cot, through, far(w_in), far(w_out))
+    shape = (groups, ROWS, width)
+    return back.reshape(shape), out.reshape(shape), hidden, pre, n2, gso
 
 
 def expert_grads_body(split, where_ref, hidden_ref, pre_ref, rows_ref, gso_ref, *refs):

time: 222 us -> 222 us (level)
  no operation moved by 1% of the time
where the time goes in v5:
time: 222 us; the launch traced here: 221 us
  Pallas kernels  95.1 us (43%)
  waiting for transfers between devices  69.6 us (31%)
  starting transfers between devices  49.5 us (22%)
  local copies, waits for them, and re-layouts  5.34 us (2%)
    all_to_all x4, waiting for transfers between devices, to_experts(): lax.all_to_all(rows, AXES, 0, 0, axis_index_groups=column, tiled=True)  37.9 us
    pallas_call x1, Pallas kernels, experts(): pl.pallas_call(experts_body, out_shape=[pltpu.HBM((total, width), BF), pl...  18.4 us
    all_to_all x4, starting transfers between devices, to_experts(): lax.all_to_all(rows, AXES, 0, 0, axis_index_groups=column, tiled=True)  15.5 us
    ppermute x14, waiting for transfers between devices, peer(): return lax.ppermute(value, 'rep', [(i, i ^ k) for i in range(reps)])  13 us
    pallas_call x1, Pallas kernels, backward(): pl.pallas_call(lambda *refs: backward_body(fast, reps, shards_n, *refs),...  12.4 us
    ppermute x14, starting transfers between devices, peer(): return lax.ppermute(value, 'rep', [(i, i ^ k) for i in range(reps)])  12.1 us
    pallas_call x1, Pallas kernels, expert_grads(): pl.pallas_call(lambda *refs: expert_grads_body(split, *refs), out_shape=g...  10.7 us
    pallas_call x2, Pallas kernels, widen(): pl.pallas_call(lambda *refs: widen_body(places, aliased, *refs), out_shap...  10.5 us
  transfers between devices with their start and end apart: 31, of which 15 were waited for; matrix products, arithmetic and copies ran while one was open for 1% of the time, Pallas kernels for 34%

profile of v5, /device:TPU:0, one launch (start us, length us, event | category | flops | bytes accessed | tf_op | source)
XLA Modules:
  0.0 220.7 jit_solution(16476636983344757720)
XLA Ops:
  0.6 1.1 pack_weights.1
  1.7 5.1 %collective-permute-start.2 = (bf16[5,16,512]{2,1,0:T(8,128)(2,1)S(1)}, bf16[5,16,512]{2,1,0:T(8,128)(2,1)S(1)}, u32[]{:S(2)}, u32[]{:S(2)}) collective-permute-start(bf16[5,16,512]{2,1,0:T(8,128)(2,1)S(1)} %pack_weights.1), channel_id=1, source_target_pairs={{0,3},{1,2},{2,1},{3,0},{4,7},{5,6},{6,5},{7,4},{8,11},{9,10},{10,... | collective-permute-start | bytes 245768 | tf_op jit(solution)/shard_map/ppermute | solution.py:180
  7.5 3.5 %route.1 = (s32[2,512]{1,0:T(2,128)S(1)}, bf16[8,136,512]{2,1,0:T(8,128)(2,1)}) custom-call(s32[2,512]{1,0:T(2,128)} %bitcast.28, s32[1,512]{1,0:T(1,128)} %prio_ref.1, bf16[1,512,512]{2,1,0:T(8,128)(2,1)} %cot_ref.3), custom_call_target="tpu_custom_call" | custom-call | flops 1000 | bytes 1000 | tf_op jit(solution)/shard_map/route/pallas_call | solution.py:135
  10.9 2.8 %collective-permute-done.1 = bf16[5,16,512]{2,1,0:T(8,128)(2,1)S(1)} collective-permute-done((bf16[5,16,512]{2,1,0:T(8,128)(2,1)S(1)}, bf16[5,16,512]{2,1,0:T(8,128)(2,1)S(1)}, u32[]{:S(2)}, u32[]{:S(2)}) %collective-permute-start.1) | collective-permute-done | bytes 81952 | tf_op jit(solution)/shard_map/ppermute | solution.py:180
  13.7 4.0 %all-to-all-start.1 = ((bf16[8,136,512]{2,1,0:T(8,128)(2,1)}), bf16[8,136,512]{2,1,0:T(8,128)(2,1)S(1)}, u32[]{:S(2)}, u32[]{:S(2)}) async-start(bf16[8,136,512]{2,1,0:T(8,128)(2,1)} %get-tuple-element.74), calls=%async_computation.1 | async-start | bytes 2228224 | tf_op jit(solution)/shard_map/all_to_all | solution.py:915
  17.7 2.5 %collective-permute-start.8 = (bf16[3,4,16,512]{3,2,1,0:T(8,128)(2,1)S(1)}, bf16[3,4,16,512]{3,2,1,0:T(8,128)(2,1)S(1)}, u32[]{:S(2)}, u32[]{:S(2)}) collective-permute-start(bf16[3,4,16,512]{3,2,1,0:T(8,128)(2,1)S(1)} %pad_maximum_fusion.refs_7_), channel_id=1, source_target_pairs={{0,24},{4,28},{8,16},{12,20},{16,8},{20,12},{24,0},{28,4},{1,25},{... | collective-permute-start | bytes 589832 | tf_op jit(solution)/shard_map/ppermute | solution.py:186
  21.3 5.1 %collective-permute-done.8.refs_13_ = bf16[3,4,16,512]{3,2,1,0:T(8,128)(2,1)S(1)} collective-permute-done((bf16[3,4,16,512]{3,2,1,0:T(8,128)(2,1)S(1)}, bf16[3,4,16,512]{3,2,1,0:T(8,128)(2,1)S(1)}, u32[]{:S(2)}, u32[]{:S(2)}) %collective-permute-start.8) | collective-permute-done | bytes 196640 | tf_op jit(solution)/shard_map/ppermute | solution.py:186
  26.4 3.8 %collective-permute-done.6.refs_11_ = bf16[3,4,16,512]{3,2,1,0:T(8,128)(2,1)S(1)} collective-permute-done((bf16[3,4,16,512]{3,2,1,0:T(8,128)(2,1)S(1)}, bf16[3,4,16,512]{3,2,1,0:T(8,128)(2,1)S(1)}, u32[]{:S(2)}, u32[]{:S(2)}) %collective-permute-start.6) | collective-permute-done | bytes 196640 | tf_op jit(solution)/shard_map/ppermute | solution.py:186
  30.9 0.8 collective-permute-done.7.refs_12_
  32.0 10.4 %forward.1 = (bf16[8,136,512]{2,1,0:T(8,128)(2,1)}, bf16[16,512]{1,0:T(8,128)(2,1)S(1)}, f32[8,512]{1,0:T(8,128)S(1)}, bf16[4,512,512]{2,1,0:T(8,128)(2,1)}, bf1...) custom-call(s32[2]{0:T(128)S(1)} %pad_add_fusion.1.refs_0_, ...), custom_call_target="tpu_custom_call" | custom-call | flops 1000 | bytes 1000 | tf_op jit(solution)/shard_map/forward/pallas_call | solution.py:329
  42.4 3.3 %all-to-all-done.1.cot_ref = bf16[8,136,512]{2,1,0:T(8,128)(2,1)S(1)} async-done(((bf16[8,136,512]{2,1,0:T(8,128)(2,1)}), bf16[8,136,512]{2,1,0:T(8,128)(2,1)S(1)}, u32[]{:S(2)}, u32[]{:S(2)}) %all-to-all-start.1) | async-done | bytes 1114144 | tf_op jit(solution)/shard_map/all_to_all | solution.py:915
  45.7 3.7 %all-to-all-start = ((bf16[8,136,512]{2,1,0:T(8,128)(2,1)}), bf16[8,136,512]{2,1,0:T(8,128)(2,1)S(1)}, u32[]{:S(2)}, u32[]{:S(2)}) async-start(bf16[8,136,512]{2,1,0:T(8,128)(2,1)} %get-tuple-element.72), calls=%async_computation | async-start | bytes 2228224 | tf_op jit(solution)/shard_map/all_to_all | solution.py:915
  49.5 7.2 %cot_hidden.1.refs_2_ = f32[1088,2048]{1,0:T(8,128)} custom-call(s32[2]{0:T(128)S(1)} %pad_add_fusion.where_ref.refs_0_, bf16[8,136,512]{2,1,0:T(8,128)(2,1)S(1)} %all-to-all-done.1.cot_ref, bf16[2,512,2048]{2,1,0:T(8,128)(2,1)} %refs_4_.3), custom_call_target="tpu_custom_call" | custom-call | flops 1000 | bytes 1000 | tf_op jit(solution)/shard_map/cot_hidden/pallas_call | solution.py:354
  56.7 20.4 %all-to-all-done = bf16[8,136,512]{2,1,0:T(8,128)(2,1)S(1)} async-done(((bf16[8,136,512]{2,1,0:T(8,128)(2,1)}), bf16[8,136,512]{2,1,0:T(8,128)(2,1)S(1)}, u32[]{:S(2)}, u32[]{:S(2)}) %all-to-all-start) | async-done | bytes 1114144 | tf_op jit(solution)/shard_map/all_to_all | solution.py:915
  77.2 18.4 %experts.1 = (bf16[1088,512]{1,0:T(8,128)(2,1)}, bf16[1088,512]{1,0:T(8,128)(2,1)}, bf16[1088,2048]{1,0:T(8,128)(2,1)}, bf16[1088,2048]{1,0:T(8,128)(2,1)}, bf16[1088,512]{1,0:T(8,128)(2,1)}) custom-call(s32[2]{0:T(128)S(1)} %pad_add_fusion.where_ref.refs_0_, bf16[1088,512]{1,0:T(8,128)(2,1)S(1)} %bitcast.24, bf16[1088,512]{1,0:T(8,128)(2,1)S(1)} %bitcast.23, ...), custom_call_target="tpu_custom_call" | custom-call | flops 1000 | bytes 1000 | tf_op jit(solution)/shard_map/experts/pallas_call | solution.py:421
  95.5 3.6 %all-to-all-start.2 = ((bf16[8,136,512]{2,1,0:T(8,128)(2,1)}), bf16[8,136,512]{2,1,0:T(8,128)(2,1)S(1)}, u32[]{:S(2)}, u32[]{:S(2)}) async-start(bf16[8,136,512]{2,1,0:T(8,128)(2,1)} %bitcast.27), calls=%async_computation.2 | async-start | bytes 2228224 | tf_op jit(solution)/shard_map/all_to_all | solution.py:915
  99.1 10.7 %expert_grads.1 = (bf16[2,2,128,1024]{3,2,1,0:T(8,128)(2,1)}, bf16[2,2,128,1024]{3,2,1,0:T(8,128)(2,1)S(1)}, bf16[2,2,128,1024]{3,2,1,0:T(8,128)(2,1)}, bf16[2,2,128,1024]{3,2,1,0:T(8,128)(2,1)S(1)}) custom-call(s32[2]{0:T(128)S(1)} %pad_add_fusion.where_ref.refs_0_, bf16[1088,2048]{1,0:T(8,128)(2,1)} %get-tuple-element.79.refs_1_, ...), custom_call_target="tpu_custom_call" | custom-call | flops 1000 | bytes 1000 | tf_op jit(solution)/shard_map/expert_grads/pallas_call | solution.py:483
  109.8 1.5 collective-permute-start.10
  111.3 1.5 collective-permute-start.11
  112.8 14.2 %all-to-all-done.2.back_ref = bf16[8,136,512]{2,1,0:T(8,128)(2,1)S(1)} async-done(((bf16[8,136,512]{2,1,0:T(8,128)(2,1)}), bf16[8,136,512]{2,1,0:T(8,128)(2,1)S(1)}, u32[]{:S(2)}, u32[]{:S(2)}) %all-to-all-start.2) | async-done | bytes 1114144 | tf_op jit(solution)/shard_map/all_to_all | solution.py:915
  127.0 4.3 %all-to-all-start.3 = ((bf16[8,136,512]{2,1,0:T(8,128)(2,1)}), bf16[8,136,512]{2,1,0:T(8,128)(2,1)}, u32[]{:S(2)}, u32[]{:S(2)}) async-start(bf16[8,136,512]{2,1,0:T(8,128)(2,1)} %bitcast.26), calls=%async_computation.3 | async-start | bytes 2228224 | tf_op jit(solution)/shard_map/all_to_all | solution.py:915
  131.3 6.3 %tokens_back.1 = (f32[512,512]{1,0:T(8,128)}, bf16[512,512]{1,0:T(8,128)(2,1)}, bf16[512,512]{1,0:T(8,128)(2,1)}, f32[16,512]{1,0:T(8,128)}) custom-call(bf16[8,136,512]{2,1,0:T(8,128)(2,1)S(1)} %all-to-all-done.2.back_ref, bf16[1,512,512]{2,1,0:T(8,128)(2,1)} %cot_ref.3, s32[2,512]{1,0:T(2,128)S(1)} %get-tuple-element.71.refs_3_.index_ref, ...), custom_call_target="tpu_custom_call" | custom-call | flops 1000 | bytes 1000 | tf_op jit(solution)/shard_map/tokens_back/pallas_call | solution.py:576
  137.7 2.3 %first_sums.1 = (bf16[2,2,128,1024]{3,2,1,0:T(8,128)(2,1)S(1)}, bf16[2,128,1024]{2,1,0:T(8,128)(2,1)S(1)}, bf16[2,128,1024]{2,1,0:T(8,128)(2,1)S(1)}) custom-call(bf16[2,2,128,1024]{3,2,1,0:T(8,128)(2,1)S(1)} %get-tuple-element.83.stay0_ref, bf16[2,2,128,1024]{3,2,1,0:T(8,128)(2,1)} %collective-permute-done.10.come0_ref, ...), custom_call_target="tpu_custom_call" | custom-call | flops 1000 | bytes 1000 | tf_op jit(solution)/shard_map/first_sums/pallas_call | solution.py:762
  139.9 1.6 collective-permute-start.12
  141.5 1.5 collective-permute-start.13
  143.0 12.4 %backward.1 = (bf16[3,512,512]{2,1,0:T(8,128)(2,1)}, bf16[4,264,512]{2,1,0:T(8,128)(2,1)S(1)}, bf16[4,264,512]{2,1,0:T(8,128)(2,1)}) custom-call(s32[2]{0:T(128)S(1)} %pad_add_fusion.where_ref.refs_0_, bf16[512,512]{1,0:T(8,128)(2,1)S(1)} %copy-done.2, bf16[16,512]{1,0:T(8,128)(2,1)S(1)} %get-tuple-element.87.small_ref.refs_2_, f32[16,512]{1,0:T(8,128)S(1)} %copy-done.3, ...), custom_call_target="tpu_custom_call" | custom-call | flops 1000 | bytes 1000 | tf_op jit(solution)/shard_map/backward/pallas_call | solution.py:693
  155.8 1.0 copy-done.7
  157.3 1.4 collective-permute-start.14
  159.5 1.2 pair_sum.1
  160.7 5.2 %all-to-all-start.4 = ((bf16[4,264,512]{2,1,0:T(8,128)(2,1)}), bf16[4,264,512]{2,1,0:T(8,128)(2,1)S(1)}, u32[]{:S(2)}, u32[]{:S(2)}) async-start(bf16[4,264,512]{2,1,0:T(8,128)(2,1)} %pair_sum.1), calls=%async_computation.4 | async-start | bytes 2162688 | tf_op jit(solution)/shard_map/all_to_all | solution.py:990
  165.9 4.6 %input_back.1 = bf16[1,512,512]{2,1,0:T(8,128)(2,1)} custom-call(bf16[3,512,512]{2,1,0:T(8,128)(2,1)} %get-tuple-element.101.gp_ref, bf16[4,512,512]{2,1,0:T(8,128)(2,1)} %get-tuple-element.89.refs_0_.refs_6_.full_ref, bf16[1,512,512]{2,1,0:T(8,128)(2,1)} %x_ref.1, f32[512,512]{1,0:T(8,128)} %get-tuple-element.102.grad_resid_ref, ...), custom_call_target="tpu_custom_call" | custom-call | flops 1000 | bytes 1000 | tf_op jit(solution)/shard_map/input_back/pallas_call | solution.py:726
  170.4 11.9 %collective-permute-done.15.refs_3_ = bf16[2,2,128,1024]{3,2,1,0:T(8,128)(2,1)S(1)} collective-permute-done((bf16[2,2,128,1024]{3,2,1,0:T(8,128)(2,1)S(1)}, bf16[2,2,128,1024]{3,2,1,0:T(8,128)(2,1)S(1)}, u32[]{:S(2)}, u32[]{:S(2)}) %collective-permute-start.15) | collective-permute-done | bytes 1048608 | tf_op jit(solution)/shard_map/ppermute | solution.py:940
  183.2 1.9 slice_bitcast_fusion.1
  185.0 0.8 slice_bitcast_fusion
  185.9 1.4 collective-permute-start.21
  187.3 1.5 collective-permute-start.20
  188.8 3.8 %all-to-all-done.4.parts_ref = bf16[4,264,512]{2,1,0:T(8,128)(2,1)S(1)} async-done(((bf16[4,264,512]{2,1,0:T(8,128)(2,1)}), bf16[4,264,512]{2,1,0:T(8,128)(2,1)S(1)}, u32[]{:S(2)}, u32[]{:S(2)}) %all-to-all-start.4) | async-done | bytes 1081376 | tf_op jit(solution)/shard_map/all_to_all | solution.py:990
  192.6 0.8 line_sum.1
  193.4 3.4 %all-to-all-start.5 = ((bf16[4,64,512]{2,1,0:T(8,128)(2,1)}), bf16[4,64,512]{2,1,0:T(8,128)(2,1)S(1)}, u32[]{:S(2)}, u32[]{:S(2)}) async-start(bf16[4,64,512]{2,1,0:T(8,128)(2,1)} %get-tuple-element.114), calls=%async_computation.5 | async-start | bytes 524288 | tf_op jit(solution)/shard_map/all_to_all | solution.py:1010
  196.9 6.8 %widen.2 = (f32[2,512,2048]{2,1,0:T(8,128)}, f32[2,512,2048]{2,1,0:T(8,128)}) custom-call(s32[2]{0:T(128)S(1)} %pad_add_fusion.where_ref.refs_0_, bf16[2,2,128,1024]{3,2,1,0:T(8,128)(2,1)} %copy-done.1, bf16[2,2,128,1024]{3,2,1,0:T(8,128)(2,1)} %collective-permute-done.14.refs_2_, bf16[2,2,128,1024]{3,2,1,0:T(8,128)(2,1)} %copy-done.4, ...), custom_call_target="tpu_custom_call" | custom-call | flops 1000 | bytes 1000 | tf_op jit(solution)/shard_map/widen/pallas_call | solution.py:843
  204.4 0.9 plane_sum.1
  205.8 3.5 %all-to-all-start.6 = ((bf16[8,72,512]{2,1,0:T(8,128)(2,1)}), bf16[8,72,512]{2,1,0:T(8,128)(2,1)S(1)}, u32[]{:S(2)}, u32[]{:S(2)}) async-start(bf16[8,72,512]{2,1,0:T(8,128)(2,1)} %plane_sum.1), calls=%async_computation.6 | async-start | bytes 1179648 | tf_op jit(solution)/shard_map/all_to_all | solution.py:1017
  209.3 3.7 %combine.1 = bf16[1,512,512]{2,1,0:T(8,128)(2,1)} custom-call(bf16[8,136,512]{2,1,0:T(8,128)(2,1)} %all-to-all-done.3.out_ref, s32[2,512]{1,0:T(2,128)S(1)} %get-tuple-element.71.refs_3_.index_ref, f32[512,512]{1,0:T(8,128)} %get-tuple-element.78.resid_ref.refs_2_), custom_call_target="tpu_custom_call" | custom-call | flops 1000 | bytes 1000 | tf_op jit(solution)/shard_map/combine/pallas_call | solution.py:750
  213.0 0.8 copy-done.5
  213.8 0.8 copy-done.6
  214.6 3.7 %widen.3 = (f32[2,512,2048]{2,1,0:T(8,128)}, f32[2,512,2048]{2,1,0:T(8,128)}) custom-call(s32[2]{0:T(128)S(1)} %pad_add_fusion.where_ref.refs_0_, bf16[2,128,1024]{2,1,0:T(8,128)(2,1)} %collective-permute-done.20.refs_1_, bf16[2,128,1024]{2,1,0:T(8,128)(2,1)} %collective-permute-done.21.refs_2_, ...), custom_call_target="tpu_custom_call", output_to_operand_aliasing={{0}: (5, {}), {1}: (6, {})} | custom-call | flops 1000 | bytes 1000 | tf_op jit(solution)/shard_map/widen/pallas_call | solution.py:843
  218.3 1.4 all-to-all-done.6.refs_0_
  219.7 1.0 finish.1
  (61 shorter events, 6.3 us)
Async XLA Ops:
  1.7 9.2 %collective-permute-start.2 = (bf16[5,16,512]{2,1,0:T(8,128)(2,1)S(1)}, bf16[5,16,512]{2,1,0:T(8,128)(2,1)S(1)}, u32[]{:S(2)}, u32[]{:S(2)}) collective-permute-start(bf16[5,16,512]{2,1,0:T(8,128)(2,1)S(1)} %pack_weights.1), channel_id=1, source_target_pairs={{0,3},{1,2},{2,1},{3,0},{4,7},{5,6},{6,5},{7,4},{8,11},{9,10},{10,... | collective-permute-start | bytes 245768 | tf_op jit(solution)/shard_map/ppermute | solution.py:180
  6.8 6.9 %collective-permute-start.1 = (bf16[5,16,512]{2,1,0:T(8,128)(2,1)S(1)}, bf16[5,16,512]{2,1,0:T(8,128)(2,1)S(1)}, u32[]{:S(2)}, u32[]{:S(2)}) collective-permute-start(bf16[5,16,512]{2,1,0:T(8,128)(2,1)S(1)} %pack_weights.1), channel_id=1, source_target_pairs={{0,2},{1,3},{2,0},{3,1},{4,6},{5,7},{6,4},{7,5},{8,10},{9,11},{10,... | collective-permute-start | bytes 245768 | tf_op jit(solution)/shard_map/ppermute | solution.py:180
  6.8 6.9 %collective-permute-start = (bf16[5,16,512]{2,1,0:T(8,128)(2,1)S(1)}, bf16[5,16,512]{2,1,0:T(8,128)(2,1)S(1)}, u32[]{:S(2)}, u32[]{:S(2)}) collective-permute-start(bf16[5,16,512]{2,1,0:T(8,128)(2,1)S(1)} %pack_weights.1), channel_id=1, source_target_pairs={{0,1},{1,0},{2,3},{3,2},{4,5},{5,4},{6,7},{7,6},{8,9},{9,8},{10,11... | collective-permute-start | bytes 245768 | tf_op jit(solution)/shard_map/ppermute | solution.py:180
  13.7 32.0 %all-to-all-start.1 = ((bf16[8,136,512]{2,1,0:T(8,128)(2,1)}), bf16[8,136,512]{2,1,0:T(8,128)(2,1)S(1)}, u32[]{:S(2)}, u32[]{:S(2)}) async-start(bf16[8,136,512]{2,1,0:T(8,128)(2,1)} %get-tuple-element.74), calls=%async_computation.1 | async-start | bytes 2228224 | tf_op jit(solution)/shard_map/all_to_all | solution.py:915
  17.7 8.7 %collective-permute-start.8 = (bf16[3,4,16,512]{3,2,1,0:T(8,128)(2,1)S(1)}, bf16[3,4,16,512]{3,2,1,0:T(8,128)(2,1)S(1)}, u32[]{:S(2)}, u32[]{:S(2)}) collective-permute-start(bf16[3,4,16,512]{3,2,1,0:T(8,128)(2,1)S(1)} %pad_maximum_fusion.refs_7_), channel_id=1, source_target_pairs={{0,24},{4,28},{8,16},{12,20},{16,8},{20,12},{24,0},{28,4},{1,25},{... | collective-permute-start | bytes 589832 | tf_op jit(solution)/shard_map/ppermute | solution.py:186
  20.3 10.0 %collective-permute-start.6 = (bf16[3,4,16,512]{3,2,1,0:T(8,128)(2,1)S(1)}, bf16[3,4,16,512]{3,2,1,0:T(8,128)(2,1)S(1)}, u32[]{:S(2)}, u32[]{:S(2)}) collective-permute-start(bf16[3,4,16,512]{3,2,1,0:T(8,128)(2,1)S(1)} %pad_maximum_fusion.refs_7_), channel_id=1, source_target_pairs={{0,16},{4,20},{8,24},{12,28},{16,0},{20,4},{24,8},{28,12},{1,17},{... | collective-permute-start | bytes 589832 | tf_op jit(solution)/shard_map/ppermute | solution.py:186
  20.8 9.6 %collective-permute-start.4 = (bf16[3,4,16,512]{3,2,1,0:T(8,128)(2,1)S(1)}, bf16[3,4,16,512]{3,2,1,0:T(8,128)(2,1)S(1)}, u32[]{:S(2)}, u32[]{:S(2)}) collective-permute-start(bf16[3,4,16,512]{3,2,1,0:T(8,128)(2,1)S(1)} %pad_maximum_fusion.refs_7_), channel_id=1, source_target_pairs={{0,8},{4,12},{8,0},{12,4},{16,24},{20,28},{24,16},{28,20},{1,9},{5... | collective-permute-start | bytes 589832 | tf_op jit(solution)/shard_map/ppermute | solution.py:186
  21.3 9.5 %collective-permute-start.3 = (bf16[3,4,16,512]{3,2,1,0:T(8,128)(2,1)S(1)}, bf16[3,4,16,512]{3,2,1,0:T(8,128)(2,1)S(1)}, u32[]{:S(2)}, u32[]{:S(2)}) collective-permute-start(bf16[3,4,16,512]{3,2,1,0:T(8,128)(2,1)S(1)} %pad_maximum_fusion.refs_7_), channel_id=1, source_target_pairs={{0,4},{4,0},{8,12},{12,8},{16,20},{20,16},{24,28},{28,24},{1,5},{5... | collective-permute-start | bytes 589832 | tf_op jit(solution)/shard_map/ppermute | solution.py:188
  26.4 4.4 %collective-permute-start.9 = (bf16[3,4,16,512]{3,2,1,0:T(8,128)(2,1)S(1)}, bf16[3,4,16,512]{3,2,1,0:T(8,128)(2,1)S(1)}, u32[]{:S(2)}, u32[]{:S(2)}) collective-permute-start(bf16[3,4,16,512]{3,2,1,0:T(8,128)(2,1)S(1)} %collective-permute-done.8.refs_13_), channel_id=1, source_target_pairs={{0,4},{4,0},{8,12},{12,8},{16,20},{20,16},{24,28},{28,24},{1,5},{5... | collective-permute-start | bytes 589832 | tf_op jit(solution)/shard_map/ppermute | solution.py:188
  30.2 1.4 collective-permute-start.7
  30.3 1.6 collective-permute-start.5
  45.7 31.5 %all-to-all-start = ((bf16[8,136,512]{2,1,0:T(8,128)(2,1)}), bf16[8,136,512]{2,1,0:T(8,128)(2,1)S(1)}, u32[]{:S(2)}, u32[]{:S(2)}) async-start(bf16[8,136,512]{2,1,0:T(8,128)(2,1)} %get-tuple-element.72), calls=%async_computation | async-start | bytes 2228224 | tf_op jit(solution)/shard_map/all_to_all | solution.py:915
  77.2 18.4 %copy-start = (bf16[8,136,512]{2,1,0:T(8,128)(2,1)}, bf16[8,136,512]{2,1,0:T(8,128)(2,1)S(1)}, u32[]{:S(2)}) copy-start(bf16[8,136,512]{2,1,0:T(8,128)(2,1)S(1)} %all-to-all-done) | copy-start | bytes 3342340
  95.5 31.5 %all-to-all-start.2 = ((bf16[8,136,512]{2,1,0:T(8,128)(2,1)}), bf16[8,136,512]{2,1,0:T(8,128)(2,1)S(1)}, u32[]{:S(2)}, u32[]{:S(2)}) async-start(bf16[8,136,512]{2,1,0:T(8,128)(2,1)} %bitcast.27), calls=%async_computation.2 | async-start | bytes 2228224 | tf_op jit(solution)/shard_map/all_to_all | solution.py:915
  109.8 27.8 %collective-permute-start.10 = (bf16[2,2,128,1024]{3,2,1,0:T(8,128)(2,1)}, bf16[2,2,128,1024]{3,2,1,0:T(8,128)(2,1)}, u32[]{:S(2)}, u32[]{:S(2)}) collective-permute-start(bf16[2,2,128,1024]{3,2,1,0:T(8,128)(2,1)} %get-tuple-element.82), channel_id=1, source_target_pairs={{0,8},{4,12},{8,0},{12,4},{16,24},{20,28},{24,16},{28,20},{1,9},{5... | collective-permute-start | bytes 3145736 | tf_op jit(solution)/shard_map/ppermute | solution.py:940
  111.3 26.3 %collective-permute-start.11 = (bf16[2,2,128,1024]{3,2,1,0:T(8,128)(2,1)}, bf16[2,2,128,1024]{3,2,1,0:T(8,128)(2,1)}, u32[]{:S(2)}, u32[]{:S(2)}) collective-permute-start(bf16[2,2,128,1024]{3,2,1,0:T(8,128)(2,1)} %get-tuple-element.84), channel_id=1, source_target_pairs={{0,16},{4,20},{8,24},{12,28},{16,0},{20,4},{24,8},{28,12},{1,17},{... | collective-permute-start | bytes 3145736 | tf_op jit(solution)/shard_map/ppermute | solution.py:940
  127.0 33.6 %all-to-all-start.3 = ((bf16[8,136,512]{2,1,0:T(8,128)(2,1)}), bf16[8,136,512]{2,1,0:T(8,128)(2,1)}, u32[]{:S(2)}, u32[]{:S(2)}) async-start(bf16[8,136,512]{2,1,0:T(8,128)(2,1)} %bitcast.26), calls=%async_computation.3 | async-start | bytes 2228224 | tf_op jit(solution)/shard_map/all_to_all | solution.py:915
  137.6 5.4 %copy-start.2 = (bf16[512,512]{1,0:T(8,128)(2,1)S(1)}, bf16[512,512]{1,0:T(8,128)(2,1)}, u32[]{:S(2)}) copy-start(bf16[512,512]{1,0:T(8,128)(2,1)} %get-tuple-element.96.refs_1_) | copy-start | bytes 1572868
  137.6 5.4 %copy-start.3 = (f32[16,512]{1,0:T(8,128)S(1)}, f32[16,512]{1,0:T(8,128)}, u32[]{:S(2)}) copy-start(f32[16,512]{1,0:T(8,128)} %get-tuple-element.97.refs_3_) | copy-start | bytes 98308
  139.9 15.6 %collective-permute-start.12 = (bf16[2,128,1024]{2,1,0:T(8,128)(2,1)S(1)}, bf16[2,128,1024]{2,1,0:T(8,128)(2,1)S(1)}, u32[]{:S(2)}, u32[]{:S(2)}) collective-permute-start(bf16[2,128,1024]{2,1,0:T(8,128)(2,1)S(1)} %get-tuple-element.105), channel_id=1, source_target_pairs={{0,16},{4,20},{8,24},{12,28},{16,0},{20,4},{24,8},{28,12},{1,17},{... | collective-permute-start | bytes 1572872 | tf_op jit(solution)/shard_map/ppermute | solution.py:940
  141.5 14.0 %collective-permute-start.13 = (bf16[2,128,1024]{2,1,0:T(8,128)(2,1)S(1)}, bf16[2,128,1024]{2,1,0:T(8,128)(2,1)S(1)}, u32[]{:S(2)}, u32[]{:S(2)}) collective-permute-start(bf16[2,128,1024]{2,1,0:T(8,128)(2,1)S(1)} %get-tuple-element.106), channel_id=1, source_target_pairs={{0,8},{4,12},{8,0},{12,4},{16,24},{20,28},{24,16},{28,20},{1,9},{5... | collective-permute-start | bytes 1572872 | tf_op jit(solution)/shard_map/ppermute | solution.py:940
  155.5 1.2 copy-start.7
  156.7 25.9 %copy-start.1 = (bf16[2,2,128,1024]{3,2,1,0:T(8,128)(2,1)}, bf16[2,2,128,1024]{3,2,1,0:T(8,128)(2,1)S(1)}, u32[]{:S(2)}) copy-start(bf16[2,2,128,1024]{3,2,1,0:T(8,128)(2,1)S(1)} %second_sums.1.refs_1_) | copy-start | bytes 3145732
  156.7 2.7 %collective-permute-start.16 = (bf16[4,264,512]{2,1,0:T(8,128)(2,1)S(1)}, bf16[4,264,512]{2,1,0:T(8,128)(2,1)S(1)}, u32[]{:S(2)}, u32[]{:S(2)}) collective-permute-start(bf16[4,264,512]{2,1,0:T(8,128)(2,1)S(1)} %copy-done.7), channel_id=1, source_target_pairs={{0,4},{4,0},{8,12},{12,8},{16,20},{20,16},{24,28},{28,24},{1,5},{5... | collective-permute-start | bytes 3244040 | tf_op jit(solution)/shard_map/ppermute | solution.py:940
  156.7 25.6 %collective-permute-start.15 = (bf16[2,2,128,1024]{3,2,1,0:T(8,128)(2,1)S(1)}, bf16[2,2,128,1024]{3,2,1,0:T(8,128)(2,1)S(1)}, u32[]{:S(2)}, u32[]{:S(2)}) collective-permute-start(bf16[2,2,128,1024]{3,2,1,0:T(8,128)(2,1)S(1)} %second_sums.1.refs_1_), channel_id=1, source_target_pairs={{0,16},{4,20},{8,24},{12,28},{16,0},{20,4},{24,8},{28,12},{1,17},{... | collective-permute-start | bytes 3145736 | tf_op jit(solution)/shard_map/ppermute | solution.py:940
  157.3 25.4 %collective-permute-start.14 = (bf16[2,2,128,1024]{3,2,1,0:T(8,128)(2,1)S(1)}, bf16[2,2,128,1024]{3,2,1,0:T(8,128)(2,1)}, u32[]{:S(2)}, u32[]{:S(2)}) collective-permute-start(bf16[2,2,128,1024]{3,2,1,0:T(8,128)(2,1)S(1)} %second_sums.1.refs_1_), channel_id=1, source_target_pairs={{0,8},{4,12},{8,0},{12,4},{16,24},{20,28},{24,16},{28,20},{1,9},{5... | collective-permute-start | bytes 3145736 | tf_op jit(solution)/shard_map/ppermute | solution.py:940
  160.7 31.9 %all-to-all-start.4 = ((bf16[4,264,512]{2,1,0:T(8,128)(2,1)}), bf16[4,264,512]{2,1,0:T(8,128)(2,1)S(1)}, u32[]{:S(2)}, u32[]{:S(2)}) async-start(bf16[4,264,512]{2,1,0:T(8,128)(2,1)} %pair_sum.1), calls=%async_computation.4 | async-start | bytes 2162688 | tf_op jit(solution)/shard_map/all_to_all | solution.py:990
  182.3 11.1 %copy-start.4 = (bf16[2,2,128,1024]{3,2,1,0:T(8,128)(2,1)}, bf16[2,2,128,1024]{3,2,1,0:T(8,128)(2,1)S(1)}, u32[]{:S(2)}) copy-start(bf16[2,2,128,1024]{3,2,1,0:T(8,128)(2,1)S(1)} %collective-permute-done.15.refs_3_) | copy-start | bytes 3145732
  182.7 14.2 %collective-permute-start.17 = (bf16[2,2,128,1024]{3,2,1,0:T(8,128)(2,1)S(1)}, bf16[2,2,128,1024]{3,2,1,0:T(8,128)(2,1)}, u32[]{:S(2)}, u32[]{:S(2)}) collective-permute-start(bf16[2,2,128,1024]{3,2,1,0:T(8,128)(2,1)S(1)} %second_sums.1.refs_1_), channel_id=1, source_target_pairs={{0,4},{4,0},{8,12},{12,8},{16,20},{20,16},{24,28},{28,24},{1,5},{5... | collective-permute-start | bytes 3145736 | tf_op jit(solution)/shard_map/ppermute | solution.py:940
  182.7 14.2 %collective-permute-start.18 = (bf16[2,2,128,1024]{3,2,1,0:T(8,128)(2,1)}, bf16[2,2,128,1024]{3,2,1,0:T(8,128)(2,1)}, u32[]{:S(2)}, u32[]{:S(2)}) collective-permute-start(bf16[2,2,128,1024]{3,2,1,0:T(8,128)(2,1)} %collective-permute-done.14.refs_2_), channel_id=1, source_target_pairs={{0,4},{4,0},{8,12},{12,8},{16,20},{20,16},{24,28},{28,24},{1,5},{5... | collective-permute-start | bytes 3145736 | tf_op jit(solution)/shard_map/ppermute | solution.py:940
  183.2 13.7 %collective-permute-start.19 = (bf16[2,2,128,1024]{3,2,1,0:T(8,128)(2,1)S(1)}, bf16[2,2,128,1024]{3,2,1,0:T(8,128)(2,1)}, u32[]{:S(2)}, u32[]{:S(2)}) collective-permute-start(bf16[2,2,128,1024]{3,2,1,0:T(8,128)(2,1)S(1)} %collective-permute-done.15.refs_3_), channel_id=1, source_target_pairs={{0,4},{4,0},{8,12},{12,8},{16,20},{20,16},{24,28},{28,24},{1,5},{5... | collective-permute-start | bytes 3145736 | tf_op jit(solution)/shard_map/ppermute | solution.py:940
  185.9 19.4 %collective-permute-start.21 = (bf16[2,128,1024]{2,1,0:T(8,128)(2,1)}, bf16[2,128,1024]{2,1,0:T(8,128)(2,1)}, u32[]{:S(2)}, u32[]{:S(2)}) collective-permute-start(bf16[2,128,1024]{2,1,0:T(8,128)(2,1)} %slice_bitcast_fusion), channel_id=1, source_target_pairs={{0,8},{4,12},{8,0},{12,4},{16,24},{20,28},{24,16},{28,20},{1,9},{5... | collective-permute-start | bytes 1572872 | tf_op jit(solution)/shard_map/ppermute | solution.py:940
  187.3 17.9 %collective-permute-start.20 = (bf16[2,128,1024]{2,1,0:T(8,128)(2,1)}, bf16[2,128,1024]{2,1,0:T(8,128)(2,1)}, u32[]{:S(2)}, u32[]{:S(2)}) collective-permute-start(bf16[2,128,1024]{2,1,0:T(8,128)(2,1)} %slice_bitcast_fusion.1), channel_id=1, source_target_pairs={{0,16},{4,20},{8,24},{12,28},{16,0},{20,4},{24,8},{28,12},{1,17},{... | collective-permute-start | bytes 1572872 | tf_op jit(solution)/shard_map/ppermute | solution.py:940
  193.4 11.0 %all-to-all-start.5 = ((bf16[4,64,512]{2,1,0:T(8,128)(2,1)}), bf16[4,64,512]{2,1,0:T(8,128)(2,1)S(1)}, u32[]{:S(2)}, u32[]{:S(2)}) async-start(bf16[4,64,512]{2,1,0:T(8,128)(2,1)} %get-tuple-element.114), calls=%async_computation.5 | async-start | bytes 524288 | tf_op jit(solution)/shard_map/all_to_all | solution.py:1010
  205.3 7.7 %collective-permute-start.22 = (bf16[2,128,1024]{2,1,0:T(8,128)(2,1)}, bf16[2,128,1024]{2,1,0:T(8,128)(2,1)S(1)}, u32[]{:S(2)}, u32[]{:S(2)}) collective-permute-start(bf16[2,128,1024]{2,1,0:T(8,128)(2,1)} %collective-permute-done.20.refs_1_), channel_id=1, source_target_pairs={{0,4},{4,0},{8,12},{12,8},{16,20},{20,16},{24,28},{28,24},{1,5},{5... | collective-permute-start | bytes 1572872 | tf_op jit(solution)/shard_map/ppermute | solution.py:940
  205.3 7.7 %collective-permute-start.23 = (bf16[2,128,1024]{2,1,0:T(8,128)(2,1)}, bf16[2,128,1024]{2,1,0:T(8,128)(2,1)S(1)}, u32[]{:S(2)}, u32[]{:S(2)}) collective-permute-start(bf16[2,128,1024]{2,1,0:T(8,128)(2,1)} %collective-permute-done.21.refs_2_), channel_id=1, source_target_pairs={{0,4},{4,0},{8,12},{12,8},{16,20},{20,16},{24,28},{28,24},{1,5},{5... | collective-permute-start | bytes 1572872 | tf_op jit(solution)/shard_map/ppermute | solution.py:940
  205.8 13.9 %all-to-all-start.6 = ((bf16[8,72,512]{2,1,0:T(8,128)(2,1)}), bf16[8,72,512]{2,1,0:T(8,128)(2,1)S(1)}, u32[]{:S(2)}, u32[]{:S(2)}) async-start(bf16[8,72,512]{2,1,0:T(8,128)(2,1)} %plane_sum.1), calls=%async_computation.6 | async-start | bytes 1179648 | tf_op jit(solution)/shard_map/all_to_all | solution.py:1017
  213.0 0.8 copy-start.5
  213.8 0.8 copy-start.6

commit v6 on v5

--- a/solution.py
+++ b/solution.py
@@ -388,10 +388,10 @@
         cols = slice(start, start + FF_STEP)
         u = dot_nn(rows, w_in_ref[0, :, cols])
         square = u * u
-        t = jnp.tanh(GELU_A * (u + GELU_B * (u * square)))
-        half = 0.5 * (1.0 + t)
+        t = jnp.tanh(u * (GELU_A + (GELU_A * GELU_B) * square))
+        half = 0.5 + 0.5 * t
         hidden = u * half
-        slope = half + hidden * (1.0 - t) * (GELU_A * (1.0 + 3.0 * GELU_B * square))
+        slope = half + hidden * ((1.0 - t) * (GELU_A + (3.0 * GELU_A * GELU_B) * square))
         hidden_ref[:, cols] = hidden.astype(BF)
         pre_ref[:, cols] = (through_ref[:, cols] * (gate_col * slope)).astype(BF)
     grad_in = dot_nt(pre_ref[...], w_in_ref[0])

time: 222 us -> 221 us (level)
  no operation moved by 1% of the time
where the time goes in v6:
time: 221 us; the launch traced here: 220 us
  Pallas kernels  94.8 us (43%)
  waiting for transfers between devices  69.6 us (31%)
  starting transfers between devices  49.5 us (22%)
  local copies, waits for them, and re-layouts  5.34 us (2%)
    all_to_all x4, waiting for transfers between devices, to_experts(): lax.all_to_all(rows, AXES, 0, 0, axis_index_groups=column, tiled=True)  37.9 us
    pallas_call x1, Pallas kernels, experts(): pl.pallas_call(experts_body, out_shape=[pltpu.HBM((total, width), BF), pl...  18 us
    all_to_all x4, starting transfers between devices, to_experts(): lax.all_to_all(rows, AXES, 0, 0, axis_index_groups=column, tiled=True)  15.5 us
    ppermute x14, waiting for transfers between devices, peer(): return lax.ppermute(value, 'rep', [(i, i ^ k) for i in range(reps)])  13 us
    pallas_call x1, Pallas kernels, backward(): pl.pallas_call(lambda *refs: backward_body(fast, reps, shards_n, *refs),...  12.4 us
    ppermute x14, starting transfers between devices, peer(): return lax.ppermute(value, 'rep', [(i, i ^ k) for i in range(reps)])  12 us
    pallas_call x1, Pallas kernels, expert_grads(): pl.pallas_call(lambda *refs: expert_grads_body(split, *refs), out_shape=g...  10.7 us
    pallas_call x2, Pallas kernels, widen(): pl.pallas_call(lambda *refs: widen_body(places, aliased, *refs), out_shap...  10.5 us
  transfers between devices with their start and end apart: 31, of which 15 were waited for; matrix products, arithmetic and copies ran while one was open for 1% of the time, Pallas kernels for 34%

profile of v6, /device:TPU:0, one launch (start us, length us, event | category | flops | bytes accessed | tf_op | source)
XLA Modules:
  0.0 220.3 jit_solution(9476554110553917227)
XLA Ops:
  0.6 1.1 pack_weights.1
  1.7 5.1 %collective-permute-start.2 = (bf16[5,16,512]{2,1,0:T(8,128)(2,1)S(1)}, bf16[5,16,512]{2,1,0:T(8,128)(2,1)S(1)}, u32[]{:S(2)}, u32[]{:S(2)}) collective-permute-start(bf16[5,16,512]{2,1,0:T(8,128)(2,1)S(1)} %pack_weights.1), channel_id=1, source_target_pairs={{0,3},{1,2},{2,1},{3,0},{4,7},{5,6},{6,5},{7,4},{8,11},{9,10},{10,... | collective-permute-start | bytes 245768 | tf_op jit(solution)/shard_map/ppermute | solution.py:180
  7.5 3.5 %route.1 = (s32[2,512]{1,0:T(2,128)S(1)}, bf16[8,136,512]{2,1,0:T(8,128)(2,1)}) custom-call(s32[2,512]{1,0:T(2,128)} %bitcast.28, s32[1,512]{1,0:T(1,128)} %prio_ref.1, bf16[1,512,512]{2,1,0:T(8,128)(2,1)} %cot_ref.3), custom_call_target="tpu_custom_call" | custom-call | flops 1000 | bytes 1000 | tf_op jit(solution)/shard_map/route/pallas_call | solution.py:135
  10.9 2.8 %collective-permute-done.1 = bf16[5,16,512]{2,1,0:T(8,128)(2,1)S(1)} collective-permute-done((bf16[5,16,512]{2,1,0:T(8,128)(2,1)S(1)}, bf16[5,16,512]{2,1,0:T(8,128)(2,1)S(1)}, u32[]{:S(2)}, u32[]{:S(2)}) %collective-permute-start.1) | collective-permute-done | bytes 81952 | tf_op jit(solution)/shard_map/ppermute | solution.py:180
  13.7 4.0 %all-to-all-start.1 = ((bf16[8,136,512]{2,1,0:T(8,128)(2,1)}), bf16[8,136,512]{2,1,0:T(8,128)(2,1)S(1)}, u32[]{:S(2)}, u32[]{:S(2)}) async-start(bf16[8,136,512]{2,1,0:T(8,128)(2,1)} %get-tuple-element.74), calls=%async_computation.1 | async-start | bytes 2228224 | tf_op jit(solution)/shard_map/all_to_all | solution.py:915
  17.7 2.5 %collective-permute-start.8 = (bf16[3,4,16,512]{3,2,1,0:T(8,128)(2,1)S(1)}, bf16[3,4,16,512]{3,2,1,0:T(8,128)(2,1)S(1)}, u32[]{:S(2)}, u32[]{:S(2)}) collective-permute-start(bf16[3,4,16,512]{3,2,1,0:T(8,128)(2,1)S(1)} %pad_maximum_fusion.refs_7_), channel_id=1, source_target_pairs={{0,24},{4,28},{8,16},{12,20},{16,8},{20,12},{24,0},{28,4},{1,25},{... | collective-permute-start | bytes 589832 | tf_op jit(solution)/shard_map/ppermute | solution.py:186
  21.3 5.1 %collective-permute-done.8.refs_13_ = bf16[3,4,16,512]{3,2,1,0:T(8,128)(2,1)S(1)} collective-permute-done((bf16[3,4,16,512]{3,2,1,0:T(8,128)(2,1)S(1)}, bf16[3,4,16,512]{3,2,1,0:T(8,128)(2,1)S(1)}, u32[]{:S(2)}, u32[]{:S(2)}) %collective-permute-start.8) | collective-permute-done | bytes 196640 | tf_op jit(solution)/shard_map/ppermute | solution.py:186
  26.4 3.8 %collective-permute-done.6.refs_11_ = bf16[3,4,16,512]{3,2,1,0:T(8,128)(2,1)S(1)} collective-permute-done((bf16[3,4,16,512]{3,2,1,0:T(8,128)(2,1)S(1)}, bf16[3,4,16,512]{3,2,1,0:T(8,128)(2,1)S(1)}, u32[]{:S(2)}, u32[]{:S(2)}) %collective-permute-start.6) | collective-permute-done | bytes 196640 | tf_op jit(solution)/shard_map/ppermute | solution.py:186
  30.9 0.8 collective-permute-done.7.refs_12_
  32.0 10.4 %forward.1 = (bf16[8,136,512]{2,1,0:T(8,128)(2,1)}, bf16[16,512]{1,0:T(8,128)(2,1)S(1)}, f32[8,512]{1,0:T(8,128)S(1)}, bf16[4,512,512]{2,1,0:T(8,128)(2,1)}, bf1...) custom-call(s32[2]{0:T(128)S(1)} %pad_add_fusion.1.refs_0_, ...), custom_call_target="tpu_custom_call" | custom-call | flops 1000 | bytes 1000 | tf_op jit(solution)/shard_map/forward/pallas_call | solution.py:329
  42.4 3.3 %all-to-all-done.1.cot_ref = bf16[8,136,512]{2,1,0:T(8,128)(2,1)S(1)} async-done(((bf16[8,136,512]{2,1,0:T(8,128)(2,1)}), bf16[8,136,512]{2,1,0:T(8,128)(2,1)S(1)}, u32[]{:S(2)}, u32[]{:S(2)}) %all-to-all-start.1) | async-done | bytes 1114144 | tf_op jit(solution)/shard_map/all_to_all | solution.py:915
  45.7 3.7 %all-to-all-start = ((bf16[8,136,512]{2,1,0:T(8,128)(2,1)}), bf16[8,136,512]{2,1,0:T(8,128)(2,1)S(1)}, u32[]{:S(2)}, u32[]{:S(2)}) async-start(bf16[8,136,512]{2,1,0:T(8,128)(2,1)} %get-tuple-element.72), calls=%async_computation | async-start | bytes 2228224 | tf_op jit(solution)/shard_map/all_to_all | solution.py:915
  49.5 7.2 %cot_hidden.1.refs_2_ = f32[1088,2048]{1,0:T(8,128)} custom-call(s32[2]{0:T(128)S(1)} %pad_add_fusion.where_ref.refs_0_, bf16[8,136,512]{2,1,0:T(8,128)(2,1)S(1)} %all-to-all-done.1.cot_ref, bf16[2,512,2048]{2,1,0:T(8,128)(2,1)} %refs_4_.3), custom_call_target="tpu_custom_call" | custom-call | flops 1000 | bytes 1000 | tf_op jit(solution)/shard_map/cot_hidden/pallas_call | solution.py:354
  56.7 20.4 %all-to-all-done = bf16[8,136,512]{2,1,0:T(8,128)(2,1)S(1)} async-done(((bf16[8,136,512]{2,1,0:T(8,128)(2,1)}), bf16[8,136,512]{2,1,0:T(8,128)(2,1)S(1)}, u32[]{:S(2)}, u32[]{:S(2)}) %all-to-all-start) | async-done | bytes 1114144 | tf_op jit(solution)/shard_map/all_to_all | solution.py:915
  77.2 18.0 %experts.1 = (bf16[1088,512]{1,0:T(8,128)(2,1)}, bf16[1088,512]{1,0:T(8,128)(2,1)}, bf16[1088,2048]{1,0:T(8,128)(2,1)}, bf16[1088,2048]{1,0:T(8,128)(2,1)}, bf16[1088,512]{1,0:T(8,128)(2,1)}) custom-call(s32[2]{0:T(128)S(1)} %pad_add_fusion.where_ref.refs_0_, bf16[1088,512]{1,0:T(8,128)(2,1)S(1)} %bitcast.24, bf16[1088,512]{1,0:T(8,128)(2,1)S(1)} %bitcast.23, ...), custom_call_target="tpu_custom_call" | custom-call | flops 1000 | bytes 1000 | tf_op jit(solution)/shard_map/experts/pallas_call | solution.py:421
  95.2 3.6 %all-to-all-start.2 = ((bf16[8,136,512]{2,1,0:T(8,128)(2,1)}), bf16[8,136,512]{2,1,0:T(8,128)(2,1)S(1)}, u32[]{:S(2)}, u32[]{:S(2)}) async-start(bf16[8,136,512]{2,1,0:T(8,128)(2,1)} %bitcast.27), calls=%async_computation.2 | async-start | bytes 2228224 | tf_op jit(solution)/shard_map/all_to_all | solution.py:915
  98.8 10.7 %expert_grads.1 = (bf16[2,2,128,1024]{3,2,1,0:T(8,128)(2,1)}, bf16[2,2,128,1024]{3,2,1,0:T(8,128)(2,1)S(1)}, bf16[2,2,128,1024]{3,2,1,0:T(8,128)(2,1)}, bf16[2,2,128,1024]{3,2,1,0:T(8,128)(2,1)S(1)}) custom-call(s32[2]{0:T(128)S(1)} %pad_add_fusion.where_ref.refs_0_, bf16[1088,2048]{1,0:T(8,128)(2,1)} %get-tuple-element.79.refs_1_, ...), custom_call_target="tpu_custom_call" | custom-call | flops 1000 | bytes 1000 | tf_op jit(solution)/shard_map/expert_grads/pallas_call | solution.py:483
  109.4 1.5 collective-permute-start.10
  110.9 1.5 collective-permute-start.11
  112.4 14.2 %all-to-all-done.2.back_ref = bf16[8,136,512]{2,1,0:T(8,128)(2,1)S(1)} async-done(((bf16[8,136,512]{2,1,0:T(8,128)(2,1)}), bf16[8,136,512]{2,1,0:T(8,128)(2,1)S(1)}, u32[]{:S(2)}, u32[]{:S(2)}) %all-to-all-start.2) | async-done | bytes 1114144 | tf_op jit(solution)/shard_map/all_to_all | solution.py:915
  126.7 4.3 %all-to-all-start.3 = ((bf16[8,136,512]{2,1,0:T(8,128)(2,1)}), bf16[8,136,512]{2,1,0:T(8,128)(2,1)}, u32[]{:S(2)}, u32[]{:S(2)}) async-start(bf16[8,136,512]{2,1,0:T(8,128)(2,1)} %bitcast.26), calls=%async_computation.3 | async-start | bytes 2228224 | tf_op jit(solution)/shard_map/all_to_all | solution.py:915
  130.9 6.3 %tokens_back.1 = (f32[512,512]{1,0:T(8,128)}, bf16[512,512]{1,0:T(8,128)(2,1)}, bf16[512,512]{1,0:T(8,128)(2,1)}, f32[16,512]{1,0:T(8,128)}) custom-call(bf16[8,136,512]{2,1,0:T(8,128)(2,1)S(1)} %all-to-all-done.2.back_ref, bf16[1,512,512]{2,1,0:T(8,128)(2,1)} %cot_ref.3, s32[2,512]{1,0:T(2,128)S(1)} %get-tuple-element.71.refs_3_.index_ref, ...), custom_call_target="tpu_custom_call" | custom-call | flops 1000 | bytes 1000 | tf_op jit(solution)/shard_map/tokens_back/pallas_call | solution.py:576
  137.3 2.3 %first_sums.1 = (bf16[2,2,128,1024]{3,2,1,0:T(8,128)(2,1)S(1)}, bf16[2,128,1024]{2,1,0:T(8,128)(2,1)S(1)}, bf16[2,128,1024]{2,1,0:T(8,128)(2,1)S(1)}) custom-call(bf16[2,2,128,1024]{3,2,1,0:T(8,128)(2,1)S(1)} %get-tuple-element.83.stay0_ref, bf16[2,2,128,1024]{3,2,1,0:T(8,128)(2,1)} %collective-permute-done.10.come0_ref, ...), custom_call_target="tpu_custom_call" | custom-call | flops 1000 | bytes 1000 | tf_op jit(solution)/shard_map/first_sums/pallas_call | solution.py:762
  139.6 1.6 collective-permute-start.12
  141.2 1.5 collective-permute-start.13
  142.7 12.4 %backward.1 = (bf16[3,512,512]{2,1,0:T(8,128)(2,1)}, bf16[4,264,512]{2,1,0:T(8,128)(2,1)S(1)}, bf16[4,264,512]{2,1,0:T(8,128)(2,1)}) custom-call(s32[2]{0:T(128)S(1)} %pad_add_fusion.where_ref.refs_0_, bf16[512,512]{1,0:T(8,128)(2,1)S(1)} %copy-done.2, bf16[16,512]{1,0:T(8,128)(2,1)S(1)} %get-tuple-element.87.small_ref.refs_2_, f32[16,512]{1,0:T(8,128)S(1)} %copy-done.3, ...), custom_call_target="tpu_custom_call" | custom-call | flops 1000 | bytes 1000 | tf_op jit(solution)/shard_map/backward/pallas_call | solution.py:693
  155.4 1.0 copy-done.7
  156.9 1.4 collective-permute-start.14
  159.1 1.2 pair_sum.1
  160.3 5.2 %all-to-all-start.4 = ((bf16[4,264,512]{2,1,0:T(8,128)(2,1)}), bf16[4,264,512]{2,1,0:T(8,128)(2,1)S(1)}, u32[]{:S(2)}, u32[]{:S(2)}) async-start(bf16[4,264,512]{2,1,0:T(8,128)(2,1)} %pair_sum.1), calls=%async_computation.4 | async-start | bytes 2162688 | tf_op jit(solution)/shard_map/all_to_all | solution.py:990
  165.5 4.6 %input_back.1 = bf16[1,512,512]{2,1,0:T(8,128)(2,1)} custom-call(bf16[3,512,512]{2,1,0:T(8,128)(2,1)} %get-tuple-element.101.gp_ref, bf16[4,512,512]{2,1,0:T(8,128)(2,1)} %get-tuple-element.89.refs_0_.refs_6_.full_ref, bf16[1,512,512]{2,1,0:T(8,128)(2,1)} %x_ref.1, f32[512,512]{1,0:T(8,128)} %get-tuple-element.102.grad_resid_ref, ...), custom_call_target="tpu_custom_call" | custom-call | flops 1000 | bytes 1000 | tf_op jit(solution)/shard_map/input_back/pallas_call | solution.py:726
  170.1 11.9 %collective-permute-done.15.refs_3_ = bf16[2,2,128,1024]{3,2,1,0:T(8,128)(2,1)S(1)} collective-permute-done((bf16[2,2,128,1024]{3,2,1,0:T(8,128)(2,1)S(1)}, bf16[2,2,128,1024]{3,2,1,0:T(8,128)(2,1)S(1)}, u32[]{:S(2)}, u32[]{:S(2)}) %collective-permute-start.15) | collective-permute-done | bytes 1048608 | tf_op jit(solution)/shard_map/ppermute | solution.py:940
  182.8 1.9 slice_bitcast_fusion.1
  184.7 0.8 slice_bitcast_fusion
  185.5 1.4 collective-permute-start.21
  187.0 1.5 collective-permute-start.20
  188.5 3.8 %all-to-all-done.4.parts_ref = bf16[4,264,512]{2,1,0:T(8,128)(2,1)S(1)} async-done(((bf16[4,264,512]{2,1,0:T(8,128)(2,1)}), bf16[4,264,512]{2,1,0:T(8,128)(2,1)S(1)}, u32[]{:S(2)}, u32[]{:S(2)}) %all-to-all-start.4) | async-done | bytes 1081376 | tf_op jit(solution)/shard_map/all_to_all | solution.py:990
  192.3 0.8 line_sum.1
  193.1 3.4 %all-to-all-start.5 = ((bf16[4,64,512]{2,1,0:T(8,128)(2,1)}), bf16[4,64,512]{2,1,0:T(8,128)(2,1)S(1)}, u32[]{:S(2)}, u32[]{:S(2)}) async-start(bf16[4,64,512]{2,1,0:T(8,128)(2,1)} %get-tuple-element.114), calls=%async_computation.5 | async-start | bytes 524288 | tf_op jit(solution)/shard_map/all_to_all | solution.py:1010
  196.5 6.8 %widen.2 = (f32[2,512,2048]{2,1,0:T(8,128)}, f32[2,512,2048]{2,1,0:T(8,128)}) custom-call(s32[2]{0:T(128)S(1)} %pad_add_fusion.where_ref.refs_0_, bf16[2,2,128,1024]{3,2,1,0:T(8,128)(2,1)} %copy-done.1, bf16[2,2,128,1024]{3,2,1,0:T(8,128)(2,1)} %collective-permute-done.14.refs_2_, bf16[2,2,128,1024]{3,2,1,0:T(8,128)(2,1)} %copy-done.4, ...), custom_call_target="tpu_custom_call" | custom-call | flops 1000 | bytes 1000 | tf_op jit(solution)/shard_map/widen/pallas_call | solution.py:843
  204.0 0.9 plane_sum.1
  205.4 3.5 %all-to-all-start.6 = ((bf16[8,72,512]{2,1,0:T(8,128)(2,1)}), bf16[8,72,512]{2,1,0:T(8,128)(2,1)S(1)}, u32[]{:S(2)}, u32[]{:S(2)}) async-start(bf16[8,72,512]{2,1,0:T(8,128)(2,1)} %plane_sum.1), calls=%async_computation.6 | async-start | bytes 1179648 | tf_op jit(solution)/shard_map/all_to_all | solution.py:1017
  209.0 3.7 %combine.1 = bf16[1,512,512]{2,1,0:T(8,128)(2,1)} custom-call(bf16[8,136,512]{2,1,0:T(8,128)(2,1)} %all-to-all-done.3.out_ref, s32[2,512]{1,0:T(2,128)S(1)} %get-tuple-element.71.refs_3_.index_ref, f32[512,512]{1,0:T(8,128)} %get-tuple-element.78.resid_ref.refs_2_), custom_call_target="tpu_custom_call" | custom-call | flops 1000 | bytes 1000 | tf_op jit(solution)/shard_map/combine/pallas_call | solution.py:750
  212.6 0.8 copy-done.5
  213.4 0.8 copy-done.6
  214.2 3.7 %widen.3 = (f32[2,512,2048]{2,1,0:T(8,128)}, f32[2,512,2048]{2,1,0:T(8,128)}) custom-call(s32[2]{0:T(128)S(1)} %pad_add_fusion.where_ref.refs_0_, bf16[2,128,1024]{2,1,0:T(8,128)(2,1)} %collective-permute-done.20.refs_1_, bf16[2,128,1024]{2,1,0:T(8,128)(2,1)} %collective-permute-done.21.refs_2_, ...), custom_call_target="tpu_custom_call", output_to_operand_aliasing={{0}: (5, {}), {1}: (6, {})} | custom-call | flops 1000 | bytes 1000 | tf_op jit(solution)/shard_map/widen/pallas_call | solution.py:843
  217.9 1.4 all-to-all-done.6.refs_0_
  219.3 1.0 finish.1
  (61 shorter events, 6.3 us)
Async XLA Ops:
  1.7 9.2 %collective-permute-start.2 = (bf16[5,16,512]{2,1,0:T(8,128)(2,1)S(1)}, bf16[5,16,512]{2,1,0:T(8,128)(2,1)S(1)}, u32[]{:S(2)}, u32[]{:S(2)}) collective-permute-start(bf16[5,16,512]{2,1,0:T(8,128)(2,1)S(1)} %pack_weights.1), channel_id=1, source_target_pairs={{0,3},{1,2},{2,1},{3,0},{4,7},{5,6},{6,5},{7,4},{8,11},{9,10},{10,... | collective-permute-start | bytes 245768 | tf_op jit(solution)/shard_map/ppermute | solution.py:180
  6.8 6.9 %collective-permute-start.1 = (bf16[5,16,512]{2,1,0:T(8,128)(2,1)S(1)}, bf16[5,16,512]{2,1,0:T(8,128)(2,1)S(1)}, u32[]{:S(2)}, u32[]{:S(2)}) collective-permute-start(bf16[5,16,512]{2,1,0:T(8,128)(2,1)S(1)} %pack_weights.1), channel_id=1, source_target_pairs={{0,2},{1,3},{2,0},{3,1},{4,6},{5,7},{6,4},{7,5},{8,10},{9,11},{10,... | collective-permute-start | bytes 245768 | tf_op jit(solution)/shard_map/ppermute | solution.py:180
  6.8 6.9 %collective-permute-start = (bf16[5,16,512]{2,1,0:T(8,128)(2,1)S(1)}, bf16[5,16,512]{2,1,0:T(8,128)(2,1)S(1)}, u32[]{:S(2)}, u32[]{:S(2)}) collective-permute-start(bf16[5,16,512]{2,1,0:T(8,128)(2,1)S(1)} %pack_weights.1), channel_id=1, source_target_pairs={{0,1},{1,0},{2,3},{3,2},{4,5},{5,4},{6,7},{7,6},{8,9},{9,8},{10,11... | collective-permute-start | bytes 245768 | tf_op jit(solution)/shard_map/ppermute | solution.py:180
  13.7 32.0 %all-to-all-start.1 = ((bf16[8,136,512]{2,1,0:T(8,128)(2,1)}), bf16[8,136,512]{2,1,0:T(8,128)(2,1)S(1)}, u32[]{:S(2)}, u32[]{:S(2)}) async-start(bf16[8,136,512]{2,1,0:T(8,128)(2,1)} %get-tuple-element.74), calls=%async_computation.1 | async-start | bytes 2228224 | tf_op jit(solution)/shard_map/all_to_all | solution.py:915
  17.7 8.7 %collective-permute-start.8 = (bf16[3,4,16,512]{3,2,1,0:T(8,128)(2,1)S(1)}, bf16[3,4,16,512]{3,2,1,0:T(8,128)(2,1)S(1)}, u32[]{:S(2)}, u32[]{:S(2)}) collective-permute-start(bf16[3,4,16,512]{3,2,1,0:T(8,128)(2,1)S(1)} %pad_maximum_fusion.refs_7_), channel_id=1, source_target_pairs={{0,24},{4,28},{8,16},{12,20},{16,8},{20,12},{24,0},{28,4},{1,25},{... | collective-permute-start | bytes 589832 | tf_op jit(solution)/shard_map/ppermute | solution.py:186
  20.3 10.0 %collective-permute-start.6 = (bf16[3,4,16,512]{3,2,1,0:T(8,128)(2,1)S(1)}, bf16[3,4,16,512]{3,2,1,0:T(8,128)(2,1)S(1)}, u32[]{:S(2)}, u32[]{:S(2)}) collective-permute-start(bf16[3,4,16,512]{3,2,1,0:T(8,128)(2,1)S(1)} %pad_maximum_fusion.refs_7_), channel_id=1, source_target_pairs={{0,16},{4,20},{8,24},{12,28},{16,0},{20,4},{24,8},{28,12},{1,17},{... | collective-permute-start | bytes 589832 | tf_op jit(solution)/shard_map/ppermute | solution.py:186
  20.8 9.6 %collective-permute-start.4 = (bf16[3,4,16,512]{3,2,1,0:T(8,128)(2,1)S(1)}, bf16[3,4,16,512]{3,2,1,0:T(8,128)(2,1)S(1)}, u32[]{:S(2)}, u32[]{:S(2)}) collective-permute-start(bf16[3,4,16,512]{3,2,1,0:T(8,128)(2,1)S(1)} %pad_maximum_fusion.refs_7_), channel_id=1, source_target_pairs={{0,8},{4,12},{8,0},{12,4},{16,24},{20,28},{24,16},{28,20},{1,9},{5... | collective-permute-start | bytes 589832 | tf_op jit(solution)/shard_map/ppermute | solution.py:186
  21.3 9.5 %collective-permute-start.3 = (bf16[3,4,16,512]{3,2,1,0:T(8,128)(2,1)S(1)}, bf16[3,4,16,512]{3,2,1,0:T(8,128)(2,1)S(1)}, u32[]{:S(2)}, u32[]{:S(2)}) collective-permute-start(bf16[3,4,16,512]{3,2,1,0:T(8,128)(2,1)S(1)} %pad_maximum_fusion.refs_7_), channel_id=1, source_target_pairs={{0,4},{4,0},{8,12},{12,8},{16,20},{20,16},{24,28},{28,24},{1,5},{5... | collective-permute-start | bytes 589832 | tf_op jit(solution)/shard_map/ppermute | solution.py:188
  26.4 4.4 %collective-permute-start.9 = (bf16[3,4,16,512]{3,2,1,0:T(8,128)(2,1)S(1)}, bf16[3,4,16,512]{3,2,1,0:T(8,128)(2,1)S(1)}, u32[]{:S(2)}, u32[]{:S(2)}) collective-permute-start(bf16[3,4,16,512]{3,2,1,0:T(8,128)(2,1)S(1)} %collective-permute-done.8.refs_13_), channel_id=1, source_target_pairs={{0,4},{4,0},{8,12},{12,8},{16,20},{20,16},{24,28},{28,24},{1,5},{5... | collective-permute-start | bytes 589832 | tf_op jit(solution)/shard_map/ppermute | solution.py:188
  30.2 1.4 collective-permute-start.7
  30.3 1.6 collective-permute-start.5
  45.7 31.5 %all-to-all-start = ((bf16[8,136,512]{2,1,0:T(8,128)(2,1)}), bf16[8,136,512]{2,1,0:T(8,128)(2,1)S(1)}, u32[]{:S(2)}, u32[]{:S(2)}) async-start(bf16[8,136,512]{2,1,0:T(8,128)(2,1)} %get-tuple-element.72), calls=%async_computation | async-start | bytes 2228224 | tf_op jit(solution)/shard_map/all_to_all | solution.py:915
  77.2 18.0 %copy-start = (bf16[8,136,512]{2,1,0:T(8,128)(2,1)}, bf16[8,136,512]{2,1,0:T(8,128)(2,1)S(1)}, u32[]{:S(2)}) copy-start(bf16[8,136,512]{2,1,0:T(8,128)(2,1)S(1)} %all-to-all-done) | copy-start | bytes 3342340
  95.2 31.5 %all-to-all-start.2 = ((bf16[8,136,512]{2,1,0:T(8,128)(2,1)}), bf16[8,136,512]{2,1,0:T(8,128)(2,1)S(1)}, u32[]{:S(2)}, u32[]{:S(2)}) async-start(bf16[8,136,512]{2,1,0:T(8,128)(2,1)} %bitcast.27), calls=%async_computation.2 | async-start | bytes 2228224 | tf_op jit(solution)/shard_map/all_to_all | solution.py:915
  109.4 27.8 %collective-permute-start.10 = (bf16[2,2,128,1024]{3,2,1,0:T(8,128)(2,1)}, bf16[2,2,128,1024]{3,2,1,0:T(8,128)(2,1)}, u32[]{:S(2)}, u32[]{:S(2)}) collective-permute-start(bf16[2,2,128,1024]{3,2,1,0:T(8,128)(2,1)} %get-tuple-element.82), channel_id=1, source_target_pairs={{0,8},{4,12},{8,0},{12,4},{16,24},{20,28},{24,16},{28,20},{1,9},{5... | collective-permute-start | bytes 3145736 | tf_op jit(solution)/shard_map/ppermute | solution.py:940
  110.9 26.4 %collective-permute-start.11 = (bf16[2,2,128,1024]{3,2,1,0:T(8,128)(2,1)}, bf16[2,2,128,1024]{3,2,1,0:T(8,128)(2,1)}, u32[]{:S(2)}, u32[]{:S(2)}) collective-permute-start(bf16[2,2,128,1024]{3,2,1,0:T(8,128)(2,1)} %get-tuple-element.84), channel_id=1, source_target_pairs={{0,16},{4,20},{8,24},{12,28},{16,0},{20,4},{24,8},{28,12},{1,17},{... | collective-permute-start | bytes 3145736 | tf_op jit(solution)/shard_map/ppermute | solution.py:940
  126.7 33.6 %all-to-all-start.3 = ((bf16[8,136,512]{2,1,0:T(8,128)(2,1)}), bf16[8,136,512]{2,1,0:T(8,128)(2,1)}, u32[]{:S(2)}, u32[]{:S(2)}) async-start(bf16[8,136,512]{2,1,0:T(8,128)(2,1)} %bitcast.26), calls=%async_computation.3 | async-start | bytes 2228224 | tf_op jit(solution)/shard_map/all_to_all | solution.py:915
  137.3 5.4 %copy-start.2 = (bf16[512,512]{1,0:T(8,128)(2,1)S(1)}, bf16[512,512]{1,0:T(8,128)(2,1)}, u32[]{:S(2)}) copy-start(bf16[512,512]{1,0:T(8,128)(2,1)} %get-tuple-element.96.refs_1_) | copy-start | bytes 1572868
  137.3 5.4 %copy-start.3 = (f32[16,512]{1,0:T(8,128)S(1)}, f32[16,512]{1,0:T(8,128)}, u32[]{:S(2)}) copy-start(f32[16,512]{1,0:T(8,128)} %get-tuple-element.97.refs_3_) | copy-start | bytes 98308
  139.6 15.6 %collective-permute-start.12 = (bf16[2,128,1024]{2,1,0:T(8,128)(2,1)S(1)}, bf16[2,128,1024]{2,1,0:T(8,128)(2,1)S(1)}, u32[]{:S(2)}, u32[]{:S(2)}) collective-permute-start(bf16[2,128,1024]{2,1,0:T(8,128)(2,1)S(1)} %get-tuple-element.105), channel_id=1, source_target_pairs={{0,16},{4,20},{8,24},{12,28},{16,0},{20,4},{24,8},{28,12},{1,17},{... | collective-permute-start | bytes 1572872 | tf_op jit(solution)/shard_map/ppermute | solution.py:940
  141.2 14.0 %collective-permute-start.13 = (bf16[2,128,1024]{2,1,0:T(8,128)(2,1)S(1)}, bf16[2,128,1024]{2,1,0:T(8,128)(2,1)S(1)}, u32[]{:S(2)}, u32[]{:S(2)}) collective-permute-start(bf16[2,128,1024]{2,1,0:T(8,128)(2,1)S(1)} %get-tuple-element.106), channel_id=1, source_target_pairs={{0,8},{4,12},{8,0},{12,4},{16,24},{20,28},{24,16},{28,20},{1,9},{5... | collective-permute-start | bytes 1572872 | tf_op jit(solution)/shard_map/ppermute | solution.py:940
  155.1 1.2 copy-start.7
  156.4 25.9 %copy-start.1 = (bf16[2,2,128,1024]{3,2,1,0:T(8,128)(2,1)}, bf16[2,2,128,1024]{3,2,1,0:T(8,128)(2,1)S(1)}, u32[]{:S(2)}) copy-start(bf16[2,2,128,1024]{3,2,1,0:T(8,128)(2,1)S(1)} %second_sums.1.refs_1_) | copy-start | bytes 3145732
  156.4 2.7 %collective-permute-start.16 = (bf16[4,264,512]{2,1,0:T(8,128)(2,1)S(1)}, bf16[4,264,512]{2,1,0:T(8,128)(2,1)S(1)}, u32[]{:S(2)}, u32[]{:S(2)}) collective-permute-start(bf16[4,264,512]{2,1,0:T(8,128)(2,1)S(1)} %copy-done.7), channel_id=1, source_target_pairs={{0,4},{4,0},{8,12},{12,8},{16,20},{20,16},{24,28},{28,24},{1,5},{5... | collective-permute-start | bytes 3244040 | tf_op jit(solution)/shard_map/ppermute | solution.py:940
  156.4 25.6 %collective-permute-start.15 = (bf16[2,2,128,1024]{3,2,1,0:T(8,128)(2,1)S(1)}, bf16[2,2,128,1024]{3,2,1,0:T(8,128)(2,1)S(1)}, u32[]{:S(2)}, u32[]{:S(2)}) collective-permute-start(bf16[2,2,128,1024]{3,2,1,0:T(8,128)(2,1)S(1)} %second_sums.1.refs_1_), channel_id=1, source_target_pairs={{0,16},{4,20},{8,24},{12,28},{16,0},{20,4},{24,8},{28,12},{1,17},{... | collective-permute-start | bytes 3145736 | tf_op jit(solution)/shard_map/ppermute | solution.py:940
  156.9 25.4 %collective-permute-start.14 = (bf16[2,2,128,1024]{3,2,1,0:T(8,128)(2,1)S(1)}, bf16[2,2,128,1024]{3,2,1,0:T(8,128)(2,1)}, u32[]{:S(2)}, u32[]{:S(2)}) collective-permute-start(bf16[2,2,128,1024]{3,2,1,0:T(8,128)(2,1)S(1)} %second_sums.1.refs_1_), channel_id=1, source_target_pairs={{0,8},{4,12},{8,0},{12,4},{16,24},{20,28},{24,16},{28,20},{1,9},{5... | collective-permute-start | bytes 3145736 | tf_op jit(solution)/shard_map/ppermute | solution.py:940
  160.3 31.9 %all-to-all-start.4 = ((bf16[4,264,512]{2,1,0:T(8,128)(2,1)}), bf16[4,264,512]{2,1,0:T(8,128)(2,1)S(1)}, u32[]{:S(2)}, u32[]{:S(2)}) async-start(bf16[4,264,512]{2,1,0:T(8,128)(2,1)} %pair_sum.1), calls=%async_computation.4 | async-start | bytes 2162688 | tf_op jit(solution)/shard_map/all_to_all | solution.py:990
  182.0 11.1 %copy-start.4 = (bf16[2,2,128,1024]{3,2,1,0:T(8,128)(2,1)}, bf16[2,2,128,1024]{3,2,1,0:T(8,128)(2,1)S(1)}, u32[]{:S(2)}) copy-start(bf16[2,2,128,1024]{3,2,1,0:T(8,128)(2,1)S(1)} %collective-permute-done.15.refs_3_) | copy-start | bytes 3145732
  182.3 14.2 %collective-permute-start.17 = (bf16[2,2,128,1024]{3,2,1,0:T(8,128)(2,1)S(1)}, bf16[2,2,128,1024]{3,2,1,0:T(8,128)(2,1)}, u32[]{:S(2)}, u32[]{:S(2)}) collective-permute-start(bf16[2,2,128,1024]{3,2,1,0:T(8,128)(2,1)S(1)} %second_sums.1.refs_1_), channel_id=1, source_target_pairs={{0,4},{4,0},{8,12},{12,8},{16,20},{20,16},{24,28},{28,24},{1,5},{5... | collective-permute-start | bytes 3145736 | tf_op jit(solution)/shard_map/ppermute | solution.py:940
  182.3 14.2 %collective-permute-start.18 = (bf16[2,2,128,1024]{3,2,1,0:T(8,128)(2,1)}, bf16[2,2,128,1024]{3,2,1,0:T(8,128)(2,1)}, u32[]{:S(2)}, u32[]{:S(2)}) collective-permute-start(bf16[2,2,128,1024]{3,2,1,0:T(8,128)(2,1)} %collective-permute-done.14.refs_2_), channel_id=1, source_target_pairs={{0,4},{4,0},{8,12},{12,8},{16,20},{20,16},{24,28},{28,24},{1,5},{5... | collective-permute-start | bytes 3145736 | tf_op jit(solution)/shard_map/ppermute | solution.py:940
  182.8 13.7 %collective-permute-start.19 = (bf16[2,2,128,1024]{3,2,1,0:T(8,128)(2,1)S(1)}, bf16[2,2,128,1024]{3,2,1,0:T(8,128)(2,1)}, u32[]{:S(2)}, u32[]{:S(2)}) collective-permute-start(bf16[2,2,128,1024]{3,2,1,0:T(8,128)(2,1)S(1)} %collective-permute-done.15.refs_3_), channel_id=1, source_target_pairs={{0,4},{4,0},{8,12},{12,8},{16,20},{20,16},{24,28},{28,24},{1,5},{5... | collective-permute-start | bytes 3145736 | tf_op jit(solution)/shard_map/ppermute | solution.py:940
  185.5 19.4 %collective-permute-start.21 = (bf16[2,128,1024]{2,1,0:T(8,128)(2,1)}, bf16[2,128,1024]{2,1,0:T(8,128)(2,1)}, u32[]{:S(2)}, u32[]{:S(2)}) collective-permute-start(bf16[2,128,1024]{2,1,0:T(8,128)(2,1)} %slice_bitcast_fusion), channel_id=1, source_target_pairs={{0,8},{4,12},{8,0},{12,4},{16,24},{20,28},{24,16},{28,20},{1,9},{5... | collective-permute-start | bytes 1572872 | tf_op jit(solution)/shard_map/ppermute | solution.py:940
  187.0 17.9 %collective-permute-start.20 = (bf16[2,128,1024]{2,1,0:T(8,128)(2,1)}, bf16[2,128,1024]{2,1,0:T(8,128)(2,1)}, u32[]{:S(2)}, u32[]{:S(2)}) collective-permute-start(bf16[2,128,1024]{2,1,0:T(8,128)(2,1)} %slice_bitcast_fusion.1), channel_id=1, source_target_pairs={{0,16},{4,20},{8,24},{12,28},{16,0},{20,4},{24,8},{28,12},{1,17},{... | collective-permute-start | bytes 1572872 | tf_op jit(solution)/shard_map/ppermute | solution.py:940
  193.1 10.9 %all-to-all-start.5 = ((bf16[4,64,512]{2,1,0:T(8,128)(2,1)}), bf16[4,64,512]{2,1,0:T(8,128)(2,1)S(1)}, u32[]{:S(2)}, u32[]{:S(2)}) async-start(bf16[4,64,512]{2,1,0:T(8,128)(2,1)} %get-tuple-element.114), calls=%async_computation.5 | async-start | bytes 524288 | tf_op jit(solution)/shard_map/all_to_all | solution.py:1010
  204.9 7.7 %collective-permute-start.22 = (bf16[2,128,1024]{2,1,0:T(8,128)(2,1)}, bf16[2,128,1024]{2,1,0:T(8,128)(2,1)S(1)}, u32[]{:S(2)}, u32[]{:S(2)}) collective-permute-start(bf16[2,128,1024]{2,1,0:T(8,128)(2,1)} %collective-permute-done.20.refs_1_), channel_id=1, source_target_pairs={{0,4},{4,0},{8,12},{12,8},{16,20},{20,16},{24,28},{28,24},{1,5},{5... | collective-permute-start | bytes 1572872 | tf_op jit(solution)/shard_map/ppermute | solution.py:940
  204.9 7.7 %collective-permute-start.23 = (bf16[2,128,1024]{2,1,0:T(8,128)(2,1)}, bf16[2,128,1024]{2,1,0:T(8,128)(2,1)S(1)}, u32[]{:S(2)}, u32[]{:S(2)}) collective-permute-start(bf16[2,128,1024]{2,1,0:T(8,128)(2,1)} %collective-permute-done.21.refs_2_), channel_id=1, source_target_pairs={{0,4},{4,0},{8,12},{12,8},{16,20},{20,16},{24,28},{28,24},{1,5},{5... | collective-permute-start | bytes 1572872 | tf_op jit(solution)/shard_map/ppermute | solution.py:940
  205.4 13.9 %all-to-all-start.6 = ((bf16[8,72,512]{2,1,0:T(8,128)(2,1)}), bf16[8,72,512]{2,1,0:T(8,128)(2,1)S(1)}, u32[]{:S(2)}, u32[]{:S(2)}) async-start(bf16[8,72,512]{2,1,0:T(8,128)(2,1)} %plane_sum.1), calls=%async_computation.6 | async-start | bytes 1179648 | tf_op jit(solution)/shard_map/all_to_all | solution.py:1017
  212.6 0.8 copy-start.5
  213.4 0.8 copy-start.6
